TPU v7x, 32 devices: a whole 2x2x4 slice. The times are simulated.
32 devices in a mesh: groups: 2 (over x), seq: 8 (over z, y), chan: 2 (over core).
Axes of the slice: x: 2, y: 2, z: 4, core: 2. Of those that a mesh axis runs over, the one named last changes fastest.
Arguments:
- tower_input: bfloat16 [16384, 1536], P(('groups', 'seq'), 'chan'), parts along dimension 0, may hold values from -6 to 6
- dna_bases: int32 [16384, 32], P(('groups', 'seq')), parts along dimension 0, may hold values from 0 to 3
- base_embed: bfloat16 [128, 1536], P(None, 'chan'), may hold values from -1 to 1
- in_scale: float32 [2, 1536], P(None, 'chan'), may hold values from 0.5 to 1.5
- entry_norm_shift: float32 [2, 1536], P(None, 'chan'), may hold values from -0.5 to 0.5
- conv_w: bfloat16 [2, 3, 1536, 768], P(None, None, 'chan'), may hold values from -0.09375 to 0.09375
- mid_scale: float32 [2, 768], P(None, 'chan'), may hold values from 0.5 to 1.5
- mid_shift: float32 [2, 768], P(None, 'chan'), may hold values from -0.5 to 0.5
- point_w: bfloat16 [2, 768, 1536], P(None, None, 'chan'), may hold values from -0.21875 to 0.21875
- pooling_weight: bfloat16 [1536, 1536], P(None, 'chan'), may hold values from -0.15625 to 0.15625
Outputs:
- pooled: bfloat16 [8192, 1536], P(('groups', 'seq'), 'chan'), parts along dimension 0
There are 2 independent parts, one for each index of `groups`. A program takes and returns all parts, laid end to end along the dimension named above; an argument that names none is the same for every part. Nothing has to cross between parts.
All inputs are finite; a program needn't handle non-finite values.
Results may differ from a plain program's by a relative error of at most 0.018.
Values may be sent and summed in bfloat16 or wider, within the bound.
No kernel may reach another device: no remote copies, remote signals or barrier semaphores. Data moves between devices by JAX's collectives and lax.ppermute only.
A program may use at most 128 MiB of HBM per device.

v0:
```python
import jax
import jax.numpy as jnp
from jax import lax
from jax.sharding import PartitionSpec as P

NBLK = 2
FIRST_SPACING = 32
SECOND_SPACING = 48


def extended(block, sides, width):
    for axis, dim in sides:
        count = lax.axis_size(axis)
        forward = [(i, i + 1) for i in range(count - 1)]
        backward = [(target, source) for source, target in forward]
        low = lax.ppermute(
            lax.slice_in_dim(block, block.shape[dim] - width, None, axis=dim), axis, forward
        )
        high = lax.ppermute(lax.slice_in_dim(block, 0, width, axis=dim), axis, backward)
        block = jnp.concatenate([low, block, high], axis=dim)
    return block


def gelu_tanh(value):
    return jax.nn.gelu(value, approximate=True)


def with_rims(act, spread):
    return extended(act, (("seq", 0),), spread)


def local(
    tower_input,
    dna_bases,
    base_embed,
    in_scale,
    entry_norm_shift,
    conv_w,
    mid_scale,
    mid_shift,
    point_w,
    pooling_weight,
):
    rows = tower_input.shape[0]
    width = tower_input.shape[1]
    onehot = (dna_bases[:, :, None] == jnp.arange(4, dtype=jnp.int32)[None, None, :]).astype(
        jnp.bfloat16
    )
    onehot = onehot.reshape(rows, dna_bases.shape[1] * 4)
    stream = (
        tower_input.astype(jnp.float32)
        + jnp.dot(onehot, base_embed, preferred_element_type=jnp.float32)
    ).astype(jnp.bfloat16)
    spacing_list = (FIRST_SPACING, SECOND_SPACING)
    for layer_idx in range(NBLK):
        spread = spacing_list[layer_idx]
        act = gelu_tanh(
            stream.astype(jnp.float32) * in_scale[layer_idx] + entry_norm_shift[layer_idx]
        ).astype(jnp.bfloat16)
        padded = with_rims(act, spread)
        partial_value = jnp.dot(
            padded[0:rows], conv_w[layer_idx, 0], preferred_element_type=jnp.float32
        )
        partial_value = partial_value + jnp.dot(
            act, conv_w[layer_idx, 1], preferred_element_type=jnp.float32
        )
        partial_value = partial_value + jnp.dot(
            padded[2 * spread : 2 * spread + rows],
            conv_w[layer_idx, 2],
            preferred_element_type=jnp.float32,
        )
        partial_value = lax.psum_scatter(partial_value, "chan", scatter_dimension=1, tiled=True)
        inner = gelu_tanh(partial_value * mid_scale[layer_idx] + mid_shift[layer_idx]).astype(
            jnp.bfloat16
        )
        weights = point_w[layer_idx]

        def project(total, piece, start, weights=weights):
            return jnp.dot(piece, weights, preferred_element_type=jnp.float32)

        update = project(
            jnp.zeros((rows, width), jnp.float32),
            lax.all_gather(inner, "chan", axis=1, tiled=True),
            jnp.int32(0),
        )
        stream = (stream.astype(jnp.float32) + update).astype(jnp.bfloat16)
    score_logits = jnp.dot(
        lax.all_gather(stream, "chan", axis=1, tiled=True),
        pooling_weight,
        preferred_element_type=jnp.float32,
    )
    pairs = stream.astype(jnp.float32).reshape(rows // 2, 2, width)
    logit_pairs = score_logits.reshape(rows // 2, 2, width)
    weight_first = jax.nn.sigmoid(logit_pairs[:, 0] - logit_pairs[:, 1])
    result = pairs[:, 1] + weight_first * (pairs[:, 0] - pairs[:, 1])
    return result.astype(jnp.bfloat16)


def solution(mesh):
    return jax.shard_map(
        local,
        mesh=mesh,
        in_specs=(
            P(("groups", "seq"), "chan"),
            P(("groups", "seq"), None),
            P(None, "chan"),
            P(None, "chan"),
            P(None, "chan"),
            P(None, None, "chan", None),
            P(None, "chan"),
            P(None, "chan"),
            P(None, None, "chan"),
            P(None, "chan"),
        ),
        out_specs=P(("groups", "seq"), "chan"),
        check_vma=False,
    )
```

profile of v0, /device:TPU:17, one launch (start us, length us, event | category | flops | bytes accessed | tf_op | source)
XLA Modules:
  0.0 145.2 jit_solution(14105619052551638038)
XLA Ops:
  6.5 0.0 copy-start
  6.5 0.0 copy-start.4
  6.5 0.0 copy-start.5
  6.5 0.0 reduce-scatter.3.cloned.1.call-start
  6.6 0.1 eq.23
  6.7 1.2 eq.20
  7.8 0.2 eq.21
  8.0 0.0 copy-done.4
  8.1 0.0 copy-done.5
  8.1 0.0 copy-start.3
  8.1 4.5 %fusion.3 = (bf16[1024,768]{1,0:T(8,128)(2,1)S(1)}, bf16[1024,768]{1,0:T(8,128)(2,1)}) fusion(f32[768]{0:T(1024)S(1)} %get-tuple-element.8, f32[768]{0:T(1024)S(1)} %get-tuple-element.25, bf16[128,768]{1,0:T(8,128)(2,1)} %param.12, s32[1024,128]{0,1:T(8,128)S(1)} %eq.21, s32[128]{0:T(128)S(1)} %eq.23, bf16[1024,768]{1,0:T(8,128)(2,1)} %param.10), kind=kOutput, calls=%fused_computation.9 | convolution fusion | flops 213254144 | bytes 5446144 | tf_op jit(solution)/shard_map/dot_general | solution.py:52
  12.7 3.0 %collective-permute-start.1 = (bf16[32,768]{1,0:T(8,128)(2,1)S(1)}, bf16[32,768]{1,0:T(8,128)(2,1)S(1)}, u32[]{:S(2)}, u32[]{:S(2)}) collective-permute-start(bf16[32,768]{1,0:T(8,128)(2,1)S(1)} %get-tuple-element.19), channel_id=1, source_target_pairs={{2,0},{4,2},{6,4},{8,6},{10,8},{12,10},{14,12},{3,1},{5,3},{7,5},{... | collective-permute-start | bytes 147464 | tf_op jit(solution)/shard_map/ppermute | solution.py:19
  15.7 2.3 %collective-permute-start = (bf16[32,768]{1,0:T(8,128)(2,1)S(1)}, bf16[32,768]{1,0:T(8,128)(2,1)S(1)}, u32[]{:S(2)}, u32[]{:S(2)}) collective-permute-start(bf16[32,768]{1,0:T(8,128)(2,1)S(1)} %get-tuple-element.20), channel_id=1, source_target_pairs={{0,2},{2,4},{4,6},{6,8},{8,10},{10,12},{12,14},{1,3},{3,5},{5,7},{... | collective-permute-start | bytes 147464 | tf_op jit(solution)/shard_map/ppermute | solution.py:16
  18.0 0.0 copy-done.3
  18.0 1.4 fusion.60
  19.4 2.1 %collective-permute-done = bf16[32,768]{1,0:T(8,128)(2,1)S(1)} collective-permute-done((bf16[32,768]{1,0:T(8,128)(2,1)S(1)}, bf16[32,768]{1,0:T(8,128)(2,1)S(1)}, u32[]{:S(2)}, u32[]{:S(2)}) %collective-permute-start) | collective-permute-done | bytes 49184 | tf_op jit(solution)/shard_map/ppermute | solution.py:16
  21.4 1.4 fusion.42
  22.8 0.0 collective-permute-done.1
  22.9 3.0 %add_add_fusion.1 = f32[1024,768]{1,0:T(8,128)} fusion(f32[1024,768]{1,0:T(8,128)S(1)} %fusion.42, f32[1024,768]{1,0:T(8,128)S(1)} %fusion.60, bf16[32,768]{1,0:T(8,128)(2,1)S(1)} %collective-permute-done.1, bf16[1024,768]{1,0:T(8,128)(2,1)S(1)} %get-tuple-element.21, bf16[2,3,768,768]{3,2,1,0:T(8,128)(2,1)S(1)} %copy-done.3), kind=kOutput, calls=%fused_computation.27 | convolution fusion | flops 1212678144 | bytes 12238848 | tf_op jit(solution)/shard_map/dot_general | solution.py:67
  25.9 0.0 copy-start.6
  25.9 0.0 copy-start.7
  25.9 0.0 reduce-scatter.3.cloned.1.call-update
  25.9 0.0 all-gather.4.cloned.1.call-start
  26.0 0.6 copy-done.6
  26.6 0.0 copy-done.7
  26.6 12.6 %reduce-scatter.3.cloned.1.call-done = f32[1024,384]{1,0:T(8,128)} async-done(((f32[1024,768]{1,0:T(8,128)}), f32[1024,384]{1,0:T(8,128)}) %reduce-scatter.3.cloned.1.call-update) | async-done | bytes 1572880 | tf_op jit(solution)/shard_map/reduce_scatter | solution.py:72
  39.3 2.9 %fusion.27 = bf16[1024,384]{1,0:T(8,128)(2,1)} fusion(f32[1024,384]{1,0:T(8,128)} %reduce-scatter.3.cloned.1.call-done, f32[384]{0:T(512)S(1)} %get-tuple-element.12, f32[384]{0:T(512)S(1)} %get-tuple-element.27), kind=kLoop, calls=%fused_computation.38 | loop fusion | flops 4325376 | bytes 2362368 | tf_op jit(solution)/shard_map/convert_element_type | solution.py:73
  42.2 0.0 all-gather.4.cloned.1.call-update
  42.2 0.0 reduce-scatter.5.cloned.1.call-start
  42.2 11.2 %all-gather.4.cloned.1.call-done = bf16[1024,768]{1,0:T(8,128)(2,1)} async-done(((bf16[1024,384]{1,0:T(8,128)(2,1)}), bf16[1024,768]{1,0:T(8,128)(2,1)}) %all-gather.4.cloned.1.call-update) | async-done | bytes 1572880 | tf_op jit(solution)/shard_map/all_gather | solution.py:83
  53.4 5.5 %fusion.12 = (bf16[1024,768]{1,0:T(8,128)(2,1)S(1)}, bf16[1024,768]{1,0:T(8,128)(2,1)}) fusion(f32[768]{0:T(1024)S(1)} %get-tuple-element.7, f32[768]{0:T(1024)S(1)} %get-tuple-element.26, bf16[1024,768]{1,0:T(8,128)(2,1)} %all-gather.4.cloned.1.call-done, bf16[2,768,768]{2,1,0:T(8,128)(2,1)} %param.18, bf16[1024,768]{1,0:T(8,128)(2,1)} %get-tuple-element.22), kind=kOutput, calls=%fused_computation.18 | convolution fusion | flops 1219756032 | bytes 7477248 | tf_op jit(solution)/shard_map/dot_general | solution.py:79
  59.0 3.1 %collective-permute-start.2 = (bf16[48,768]{1,0:T(8,128)(2,1)S(1)}, bf16[48,768]{1,0:T(8,128)(2,1)S(1)}, u32[]{:S(2)}, u32[]{:S(2)}) collective-permute-start(bf16[48,768]{1,0:T(8,128)(2,1)S(1)} %get-tuple-element.18), channel_id=1, source_target_pairs={{0,2},{2,4},{4,6},{6,8},{8,10},{10,12},{12,14},{1,3},{3,5},{5,7},{... | collective-permute-start | bytes 221192 | tf_op jit(solution)/shard_map/ppermute | solution.py:16
  62.1 2.7 %fusion.55 = f32[1024,768]{1,0:T(8,128)S(1)} fusion(bf16[1024,768]{1,0:T(8,128)(2,1)S(1)} %get-tuple-element.23, bf16[2,3,768,768]{3,2,1,0:T(8,128)(2,1)} %param.15), kind=kOutput, calls=%fused_computation.73 | convolution fusion | flops 1207959552 | bytes 5898240 | tf_op jit(solution)/shard_map/dot_general | solution.py:64
  64.7 3.1 %collective-permute-start.3 = (bf16[48,768]{1,0:T(8,128)(2,1)S(1)}, bf16[48,768]{1,0:T(8,128)(2,1)S(1)}, u32[]{:S(2)}, u32[]{:S(2)}) collective-permute-start(bf16[48,768]{1,0:T(8,128)(2,1)S(1)} %get-tuple-element.17), channel_id=1, source_target_pairs={{2,0},{4,2},{6,4},{8,6},{10,8},{12,10},{14,12},{3,1},{5,3},{7,5},{... | collective-permute-start | bytes 221192 | tf_op jit(solution)/shard_map/ppermute | solution.py:19
  67.8 0.0 collective-permute-done.2
  67.8 2.7 %fusion.38 = f32[1024,768]{1,0:T(8,128)S(1)} fusion(bf16[1024,768]{1,0:T(8,128)(2,1)S(1)} %get-tuple-element.23, bf16[48,768]{1,0:T(8,128)(2,1)S(1)} %collective-permute-done.2, bf16[2,3,768,768]{3,2,1,0:T(8,128)(2,1)} %param.15), kind=kOutput, calls=%fused_computation.51 | convolution fusion | flops 1211105280 | bytes 5971968 | tf_op jit(solution)/shard_map/dot_general | solution.py:61
  70.5 0.0 collective-permute-done.3
  70.5 4.3 %add_add_fusion = f32[1024,768]{1,0:T(8,128)} fusion(f32[1024,768]{1,0:T(8,128)S(1)} %fusion.38, f32[1024,768]{1,0:T(8,128)S(1)} %fusion.55, bf16[48,768]{1,0:T(8,128)(2,1)S(1)} %collective-permute-done.3, bf16[1024,768]{1,0:T(8,128)(2,1)S(1)} %get-tuple-element.23, bf16[2,3,768,768]{3,2,1,0:T(8,128)(2,1)} %param.15), kind=kOutput, calls=%fused_computation.26 | convolution fusion | flops 1212678144 | bytes 12263424 | tf_op jit(solution)/shard_map/dot_general | solution.py:67
  74.8 0.0 reduce-scatter.5.cloned.1.call-update
  74.9 0.0 all-gather.6.cloned.1.call-start
  74.9 12.9 %reduce-scatter.5.cloned.1.call-done = f32[1024,384]{1,0:T(8,128)} async-done(((f32[1024,768]{1,0:T(8,128)}), f32[1024,384]{1,0:T(8,128)}) %reduce-scatter.5.cloned.1.call-update) | async-done | bytes 1572880 | tf_op jit(solution)/shard_map/reduce_scatter | solution.py:72
  87.8 2.9 %fusion.35 = bf16[1024,384]{1,0:T(8,128)(2,1)} fusion(f32[1024,384]{1,0:T(8,128)} %reduce-scatter.5.cloned.1.call-done, f32[384]{0:T(512)S(1)} %get-tuple-element.11, f32[384]{0:T(512)S(1)} %get-tuple-element.28), kind=kLoop, calls=%fused_computation.46 | loop fusion | flops 4325376 | bytes 2362368 | tf_op jit(solution)/shard_map/convert_element_type | solution.py:73
  90.7 0.0 all-gather.6.cloned.1.call-update
  90.8 0.2 all-gather.8.cloned.1.call-start
  91.0 11.0 %all-gather.6.cloned.1.call-done = bf16[1024,768]{1,0:T(8,128)(2,1)} async-done(((bf16[1024,384]{1,0:T(8,128)(2,1)}), bf16[1024,768]{1,0:T(8,128)(2,1)}) %all-gather.6.cloned.1.call-update) | async-done | bytes 1572880 | tf_op jit(solution)/shard_map/all_gather | solution.py:83
  102.0 4.8 %fusion.17 = bf16[1024,768]{1,0:T(8,128)(2,1)} fusion(bf16[1024,768]{1,0:T(8,128)(2,1)} %get-tuple-element.24, bf16[1024,768]{1,0:T(8,128)(2,1)} %all-gather.6.cloned.1.call-done, bf16[2,768,768]{2,1,0:T(8,128)(2,1)} %param.18), kind=kOutput, calls=%fused_computation.23 | convolution fusion | flops 1210318848 | bytes 5898240 | tf_op jit(solution)/shard_map/dot_general | solution.py:79
  106.8 0.0 all-gather.8.cloned.1.call-update
  106.8 4.9 %reshape.22 = f32[512,2,768]{2,1,0:T(2,128)} reshape(bf16[1024,768]{1,0:T(8,128)(2,1)} %fusion.17) | data formatting | bytes 4718592 | tf_op jit(solution)/shard_map/reshape | solution.py:92
  111.7 7.4 %fusion.77 = (f32[512,1,768]{2,1,0:T(1,128)}, f32[512,1,768]{2,1,0:T(1,128)}) fusion(f32[512,2,768]{2,1,0:T(2,128)} %reshape.22), kind=kLoop, calls=%fused_computation.103 | loop fusion | bytes 6291456 | tf_op jit(solution)/shard_map/slice | solution.py:95
  119.1 1.1 all-gather.8.cloned.1.call-done
  120.3 0.0 copy-done
  120.3 6.2 %fusion.81 = f32[1024,768]{1,0:T(8,128)} fusion(bf16[1024,1536]{1,0:T(8,128)(2,1)} %all-gather.8.cloned.1.call-done, bf16[1536,768]{1,0:T(8,128)(2,1)S(1)} %copy-done), kind=kOutput, calls=%fused_computation.107 | convolution fusion | flops 2415919104 | bytes 8650752 | tf_op jit(solution)/shard_map/dot_general | solution.py:87
  126.4 5.1 %reshape.20 = f32[512,2,768]{2,1,0:T(2,128)} reshape(f32[1024,768]{1,0:T(8,128)} %fusion.81) | data formatting | bytes 6291456 | tf_op jit(solution)/shard_map/reshape | solution.py:93
  131.6 0.0 copy-start.1
  131.6 0.0 copy-start.2
  131.6 5.7 %fusion.78 = (f32[512,1,768]{2,1,0:T(1,128)S(1)}, f32[512,1,768]{2,1,0:T(1,128)S(1)}) fusion(f32[512,2,768]{2,1,0:T(2,128)} %reshape.20), kind=kLoop, calls=%fused_computation.104 | loop fusion | bytes 6291456 | tf_op jit(solution)/shard_map/slice | solution.py:94
  137.3 0.0 copy-done.1
  137.3 0.0 copy-done.2
  137.3 1.4 fusion.47
  (5 shorter events, 0.1 us)
Async XLA Ops:
  6.5 113.7 %copy-start = (bf16[1536,768]{1,0:T(8,128)(2,1)S(1)}, bf16[1536,768]{1,0:T(8,128)(2,1)}, u32[]{:S(2)}) copy-start(bf16[1536,768]{1,0:T(8,128)(2,1)} %param.19) | copy-start | bytes 7077892
  6.5 1.5 %copy-start.4 = (f32[2,768]{1,0:T(2,128)S(1)}, f32[2,768]{1,0:T(2,128)}, u32[]{:S(2)}) copy-start(f32[2,768]{1,0:T(2,128)} %param.14) | copy-start | bytes 18436
  6.5 1.5 %copy-start.5 = (f32[2,768]{1,0:T(2,128)S(1)}, f32[2,768]{1,0:T(2,128)}, u32[]{:S(2)}) copy-start(f32[2,768]{1,0:T(2,128)} %param.13) | copy-start | bytes 18436
  6.5 32.7 %reduce-scatter.3.cloned.1.call-start = ((), (), s32[]{:S(2)}) async-start(), calls=%async_computation.2 | async-start | bytes 4718592 | tf_op jit(solution)/shard_map/reduce_scatter | solution.py:72
  8.1 9.9 %copy-start.3 = (bf16[2,3,768,768]{3,2,1,0:T(8,128)(2,1)S(1)}, bf16[2,3,768,768]{3,2,1,0:T(8,128)(2,1)}, u32[]{:S(2)}) copy-start(bf16[2,3,768,768]{3,2,1,0:T(8,128)(2,1)} %param.15) | copy-start | bytes 21233668
  12.7 10.2 %collective-permute-start.1 = (bf16[32,768]{1,0:T(8,128)(2,1)S(1)}, bf16[32,768]{1,0:T(8,128)(2,1)S(1)}, u32[]{:S(2)}, u32[]{:S(2)}) collective-permute-start(bf16[32,768]{1,0:T(8,128)(2,1)S(1)} %get-tuple-element.19), channel_id=1, source_target_pairs={{2,0},{4,2},{6,4},{8,6},{10,8},{12,10},{14,12},{3,1},{5,3},{7,5},{... | collective-permute-start | bytes 147464 | tf_op jit(solution)/shard_map/ppermute | solution.py:19
  15.7 5.7 %collective-permute-start = (bf16[32,768]{1,0:T(8,128)(2,1)S(1)}, bf16[32,768]{1,0:T(8,128)(2,1)S(1)}, u32[]{:S(2)}, u32[]{:S(2)}) collective-permute-start(bf16[32,768]{1,0:T(8,128)(2,1)S(1)} %get-tuple-element.20), channel_id=1, source_target_pairs={{0,2},{2,4},{4,6},{6,8},{8,10},{10,12},{12,14},{1,3},{3,5},{5,7},{... | collective-permute-start | bytes 147464 | tf_op jit(solution)/shard_map/ppermute | solution.py:16
  25.9 0.7 copy-start.6
  25.9 0.7 copy-start.7
  25.9 27.5 %all-gather.4.cloned.1.call-start = ((), (), s32[]{:S(2)}) async-start(), calls=%async_computation.3 | async-start | bytes 2359296 | tf_op jit(solution)/shard_map/all_gather | solution.py:83
  42.2 45.7 %reduce-scatter.5.cloned.1.call-start = ((), (), s32[]{:S(2)}) async-start(), calls=%async_computation.4 | async-start | bytes 4718592 | tf_op jit(solution)/shard_map/reduce_scatter | solution.py:72
  59.0 8.9 %collective-permute-start.2 = (bf16[48,768]{1,0:T(8,128)(2,1)S(1)}, bf16[48,768]{1,0:T(8,128)(2,1)S(1)}, u32[]{:S(2)}, u32[]{:S(2)}) collective-permute-start(bf16[48,768]{1,0:T(8,128)(2,1)S(1)} %get-tuple-element.18), channel_id=1, source_target_pairs={{0,2},{2,4},{4,6},{6,8},{8,10},{10,12},{12,14},{1,3},{3,5},{5,7},{... | collective-permute-start | bytes 221192 | tf_op jit(solution)/shard_map/ppermute | solution.py:16
  64.7 5.8 %collective-permute-start.3 = (bf16[48,768]{1,0:T(8,128)(2,1)S(1)}, bf16[48,768]{1,0:T(8,128)(2,1)S(1)}, u32[]{:S(2)}, u32[]{:S(2)}) collective-permute-start(bf16[48,768]{1,0:T(8,128)(2,1)S(1)} %get-tuple-element.17), channel_id=1, source_target_pairs={{2,0},{4,2},{6,4},{8,6},{10,8},{12,10},{14,12},{3,1},{5,3},{7,5},{... | collective-permute-start | bytes 221192 | tf_op jit(solution)/shard_map/ppermute | solution.py:19
  74.9 27.1 %all-gather.6.cloned.1.call-start = ((), (), s32[]{:S(2)}) async-start(), calls=%async_computation.5 | async-start | bytes 2359296 | tf_op jit(solution)/shard_map/all_gather | solution.py:83
  90.8 29.5 %all-gather.8.cloned.1.call-start = ((), (), s32[]{:S(2)}) async-start(), calls=%async_computation.6 | async-start | bytes 4718592 | tf_op jit(solution)/shard_map/all_gather | solution.py:88
  131.6 5.7 %copy-start.1 = (f32[512,1,768]{2,1,0:T(1,128)S(1)}, f32[512,1,768]{2,1,0:T(1,128)}, u32[]{:S(2)}) copy-start(f32[512,1,768]{2,1,0:T(1,128)} %get-tuple-element.13) | copy-start | bytes 4718596
  131.6 5.7 %copy-start.2 = (f32[512,1,768]{2,1,0:T(1,128)S(1)}, f32[512,1,768]{2,1,0:T(1,128)}, u32[]{:S(2)}) copy-start(f32[512,1,768]{2,1,0:T(1,128)} %get-tuple-element.14) | copy-start | bytes 4718596
Sparse Core Ops, SparseCore 0:
  26.0 13.1 reduce-scatter.2
  42.3 11.0 all-gather.3
  75.0 12.8 reduce-scatter.4
  90.9 11.0 all-gather.5
  106.9 13.2 all-gather.7
where the time goes:
time: 147 us; the launch traced here: 145 us
  waiting for transfers between devices  51 us (35%)
  matrix products  36.5 us (25%)
  local copies, waits for them, and re-layouts  25.4 us (17%)
  between operations  13.3 us (9%)
  starting transfers between devices  11.8 us (8%)
  other arithmetic  7.14 us (5%)
    reduce_scatter x2, waiting for transfers between devices, local(): lax.psum_scatter(partial_value, 'chan', scatter_dimension=1, tiled=True)  25.6 us
    all_gather x2, waiting for transfers between devices, local(): lax.all_gather(inner, 'chan', axis=1, tiled=True)  22.2 us
    dot_general x2, matrix products, project(): return jnp.dot(piece, weights, preferred_element_type=jnp.float32)  10.3 us
    slice x1, local copies, waits for them, and re-layouts, local(): result = pairs[:, 1] + weight_first * (pairs[:, 0] - pairs[:, 1])  7.45 us
    dot_general x2, matrix products, local(): jnp.dot(padded[2 * spread:2 * spread + rows], conv_w[layer_idx, 2], prefe...  7.37 us
    dot_general x1, matrix products, local(): jnp.dot(lax.all_gather(stream, 'chan', axis=1, tiled=True), pooling_weigh...  6.16 us
    ppermute x2, starting transfers between devices, extended(): lax.ppermute(lax.slice_in_dim(block, 0, width, axis=dim), axis, backward)  6.11 us
    convert_element_type x2, other arithmetic, local(): gelu_tanh(partial_value * mid_scale[layer_idx] + mid_shift[layer_idx])  5.78 us
  transfers between devices with their start and end apart: 9, of which 6 were waited for; matrix products, arithmetic and copies ran while one was open for 14% of the time, Pallas kernels for 0%

commit v1 on v0

v1 whole, which is shorter than its diff:
```python
import jax
import jax.numpy as jnp
from jax import lax
from jax.experimental import pallas as pl
from jax.experimental.pallas import tpu as pltpu
from jax.sharding import PartitionSpec as P

D0 = 32
D1 = 48
HALO = D0 + D1
EXTRA = 16
BF = jnp.bfloat16
F32 = jnp.float32
VM = pl.BlockSpec(memory_space=pltpu.VMEM)
HBM = pl.BlockSpec(memory_space=pltpu.HBM)
GRANT = 14 << 20


def call(kernel, outs, hbm, vmem, scratch=(), grant=GRANT):
    hbm = [pltpu.with_memory_space_constraint(a, pltpu.HBM) for a in hbm]
    vmem = [pltpu.with_memory_space_constraint(a, pltpu.VMEM) for a in vmem]
    return pl.pallas_call(
        kernel,
        out_shape=[pltpu.VMEM(shape, dtype) for shape, dtype in outs],
        in_specs=[HBM] * len(hbm) + [VM] * len(vmem),
        out_specs=[VM] * len(outs),
        scratch_shapes=list(scratch),
        compiler_params=pltpu.CompilerParams(vmem_limit_bytes=grant),
    )(*hbm, *vmem)


def gelu(v):
    inner = v * (0.7978845608028654 + 0.035677408136300125 * (v * v))
    half = 0.5 * v
    return half + half * jnp.tanh(inner)


def dot(a, b):
    return jnp.dot(a, b, preferred_element_type=F32)


def tiles(start, stop, step):
    return [(i, min(step, stop - i)) for i in range(start, stop, step)]


def act_rows(x, s_ref, b_ref, layer):
    return gelu(x.astype(F32) * s_ref[layer : layer + 1] + b_ref[layer : layer + 1]).astype(BF)


def conv_rows(h_ref, base, spread, n, w_ref):
    lhs = jnp.concatenate(
        [h_ref[base + k * spread : base + k * spread + n] for k in (-1, 0, 1)], axis=1
    )
    return dot(lhs, w_ref[...])


def mid_rows(own, other, mid_ref, layer):
    u = own.astype(F32) + other.astype(F32)
    return gelu(u * mid_ref[layer : layer + 1] + mid_ref[2 + layer : 3 + layer]).astype(BF)


def embed_first(a_lo, a_hi, rows, width):
    def kernel(
        tower, dna, embed, ins, inb, conv_w, mids, midb, point_w,
        x0, h0, e_a, e_b, pa, w0, pw0, w1, s_in, b_in, own_mid,
        tower_v, dna_v, embed_v, mids_v, midb_v, sem,
    ):
        cp = pltpu.make_async_copy
        half = rows // 2
        c_dna = cp(dna, dna_v, sem.at[0])
        c_emb = cp(embed, embed_v, sem.at[1])
        c_tow = [
            cp(tower.at[pl.ds(i * half, half)], tower_v.at[pl.ds(i * half, half)], sem.at[2 + i])
            for i in range(2)
        ]
        c_s = cp(ins, s_in, sem.at[4])
        c_b = cp(inb, b_in, sem.at[5])
        c_ms = cp(mids, mids_v, sem.at[6])
        c_mb = cp(midb, midb_v, sem.at[7])
        c_w0 = [
            cp(conv_w.at[0, k], w0.at[pl.ds(k * width, width)], sem.at[8 + k]) for k in range(3)
        ]
        c_pw = cp(point_w.at[0], pw0, sem.at[11])
        c_w1 = [
            cp(conv_w.at[1, k], w1.at[pl.ds(k * width, width)], sem.at[12 + k]) for k in range(3)
        ]
        for c in [c_dna, c_emb, *c_tow, c_s, c_b, c_ms, c_mb, *c_w0, c_pw, *c_w1]:
            c.start()
        slots = dna.shape[0]
        row = lax.broadcasted_iota(jnp.int32, (4 * slots, slots), 0)
        col = lax.broadcasted_iota(jnp.int32, (4 * slots, slots), 1)
        spread_map = jnp.where((row >> 2) == col, 1.0, 0.0).astype(BF)
        c_dna.wait()
        c_emb.wait()
        c_s.wait()
        c_b.wait()
        for i, n in tiles(0, rows, 128):
            if i % half == 0:
                c_tow[i // half].wait()
            code = (lax.broadcasted_iota(jnp.int32, (4 * slots, n), 0) & 3).astype(F32)
            base = dot(spread_map, dna_v[:, i : i + n].astype(F32).astype(BF))
            onehot = jnp.where(base == code, 1.0, 0.0).T.astype(BF)
            x = (tower_v[i : i + n].astype(F32) + dot(onehot, embed_v[...])).astype(BF)
            x0[i : i + n] = x
            h0[i : i + n] = act_rows(x, s_in, b_in, 0)
        even = lax.rem(lax.axis_index("seq"), 2) == 0
        low = x0[0:HALO]
        high = x0[rows - HALO : rows]
        e_a[...] = jnp.where(even, high, low)
        e_b[...] = jnp.where(even, low, high)
        c_ms.wait()
        c_mb.wait()
        first = lax.axis_index("chan") == 0
        mid = jnp.concatenate([mids_v[...], midb_v[...]], axis=0)
        mid = jnp.concatenate(
            [jnp.where(first, mid, 0.0), jnp.where(first, 0.0, mid)], axis=1
        )
        own_mid[...] = mid
        big = mid.astype(BF)
        rest = mid - big.astype(F32)
        middle = rest.astype(BF)
        small = (rest - middle.astype(F32)).astype(BF)
        pa[a_hi - a_lo : a_hi - a_lo + EXTRA] = jnp.concatenate(
            [big.astype(F32), middle.astype(F32), small.astype(F32), jnp.zeros_like(mid)], axis=0
        ).astype(BF)
        for c in c_w0:
            c.wait()
        for i, n in tiles(a_lo, a_hi, 256):
            pa[i - a_lo : i - a_lo + n] = conv_rows(h0, i, D0, n, w0).astype(BF)
        c_pw.wait()
        for c in c_w1:
            c.wait()

    return kernel


def first_rest(b_lo, b_hi):
    def kernel(point_w, pool_w, h0, w0, pb, pw1, pool, sem):
        copies = [
            pltpu.make_async_copy(point_w.at[1], pw1, sem.at[0]),
            pltpu.make_async_copy(pool_w, pool, sem.at[1]),
        ]
        for c in copies:
            c.start()
        for i, n in tiles(b_lo, b_hi, 224):
            pb[i - b_lo : i - b_lo + n] = conv_rows(h0, i, D0, n, w0).astype(BF)
        for c in copies:
            c.wait()

    return kernel


def first_edges(rows):
    def kernel(r_a, r_b, h0, w0, s_in, b_in, pe, lo, hi, ext):
        seq = lax.axis_index("seq")
        even = lax.rem(seq, 2) == 0
        low = jnp.where(even, r_b[...], r_a[...])
        high = jnp.where(even, r_a[...], r_b[...])
        lo[...] = low
        hi[...] = high
        zero = jnp.zeros(low.shape, BF)
        inner = 2 * D0
        span = HALO + inner
        ext[0:HALO] = jnp.where(seq == 0, zero, act_rows(low, s_in, b_in, 0))
        ext[HALO:span] = h0[0:inner]
        ext[span : span + inner] = h0[rows - inner : rows]
        ext[span + inner : 2 * span] = jnp.where(
            seq == lax.axis_size("seq") - 1, zero, act_rows(high, s_in, b_in, 0)
        )
        lhs = [
            jnp.concatenate(
                [ext[s + k * D0 : s + k * D0 + HALO] for k in range(3)], axis=1
            )
            for s in (0, span)
        ]
        pe[...] = dot(jnp.concatenate(lhs, axis=0), w0[...]).astype(BF)

    return kernel


def second_first(a_lo, a_hi, c_lo, c_hi):
    def kernel(pa, ra, x0, pw0, w1, s_in, b_in, own_mid, x1a, h1a, qa, mid):
        n_a = a_hi - a_lo
        tail = ra[n_a : n_a + EXTRA].astype(F32)
        mid[...] = own_mid[...] + (tail[0:4] + tail[4:8] + tail[8:12])
        for i, n in tiles(0, n_a, 256):
            z = mid_rows(pa[i : i + n], ra[i : i + n], mid, 0)
            x = (x0[a_lo + i : a_lo + i + n].astype(F32) + dot(z, pw0[...])).astype(BF)
            x1a[i : i + n] = x
            h1a[i : i + n] = act_rows(x, s_in, b_in, 1)
        for i, n in tiles(c_lo, c_hi, 192):
            qa[i - c_lo : i - c_lo + n] = conv_rows(h1a, i - a_lo, D1, n, w1).astype(BF)

    return kernel


def second_rest(rows, a_lo, a_hi, c_lo, c_hi):
    def kernel(
        pb, rb, pe, re, x0, lo, hi, x1a, h1a, pw0, w1, mid, s_in, b_in, x1b, qb, h1
    ):
        seq = lax.axis_index("seq")
        b_hi = rows - D0
        for i, n in tiles(0, b_hi - a_hi, 224):
            z = mid_rows(pb[i : i + n], rb[i : i + n], mid, 0)
            g = a_hi + i
            x = (x0[g : g + n].astype(F32) + dot(z, pw0[...])).astype(BF)
            x1b[c_lo + g - c_hi : c_lo + g - c_hi + n] = x
            h1[D1 + g : D1 + g + n] = act_rows(x, s_in, b_in, 1)
        z = mid_rows(pe[...], re[...], mid, 0)
        base = jnp.concatenate(
            [lo[HALO - D1 : HALO], x0[0:D0], x0[rows - D0 : rows], hi[0:D1]], axis=0
        )
        x = (base.astype(F32) + dot(z, pw0[...])).astype(BF)
        x1b[0:D0] = x[D1 : D1 + D0]
        x1b[D0:c_lo] = x1a[0 : c_lo - a_lo]
        x1b[c_lo : c_lo + a_hi - c_hi] = x1a[c_hi - a_lo : a_hi - a_lo]
        x1b[c_lo + b_hi - c_hi : c_lo + rows - c_hi] = x[HALO : HALO + D0]
        h = act_rows(x, s_in, b_in, 1)
        zero = jnp.zeros((D1, h.shape[1]), BF)
        h1[0:D1] = jnp.where(seq == 0, zero, h[0:D1])
        h1[D1:HALO] = h[D1:HALO]
        h1[D1 + b_hi : D1 + rows] = h[HALO : HALO + D0]
        h1[D1 + rows : 2 * D1 + rows] = jnp.where(
            seq == lax.axis_size("seq") - 1, zero, h[HALO + D0 :]
        )
        keep = 2 * D1
        h1[D1 + a_lo : D1 + c_lo + D1] = h1a[0 : c_lo + D1 - a_lo]
        h1[D1 + c_hi - D1 : D1 + a_hi] = h1a[c_hi - D1 - a_lo : a_hi - a_lo]
        qb[0:c_lo] = conv_rows(h1, D1, D1, c_lo, w1).astype(BF)
        for i, n in tiles(c_hi, rows, 272):
            qb[c_lo + i - c_hi : c_lo + i - c_hi + n] = conv_rows(h1, D1 + i, D1, n, w1).astype(BF)

    return kernel


def last_point(x_base, n_rows, step):
    def kernel(q, r, x1, pw1, mid, dm, df, xo, wide):
        for i, n in tiles(0, n_rows, step):
            z = mid_rows(q[i : i + n], r[i : i + n], mid, 1)
            x = x1[x_base + i : x_base + i + n].astype(F32) + dot(z, pw1[...])
            x = x.astype(BF).astype(F32)
            j, m = i // 2, n // 2
            for k in range(wide.shape[0]):
                cols = slice(128 * k, 128 * (k + 1))
                wide[k, i : i + n] = x[:, cols]
                first = wide[k, pl.ds(i, m, stride=2), :]
                second = wide[k, pl.ds(i + 1, m, stride=2), :]
                d = first - second
                dm[j : j + m, cols] = d.astype(BF)
                df[j : j + m, cols] = d
                xo[j : j + m, cols] = second.astype(BF)

    return kernel


def pool_first(da, ra, db, pool, dfa, xoa, ya, lb):
    width = da.shape[1]
    chan = lax.axis_index("chan")
    mine = pl.ds(pl.multiple_of(chan * width, 128), width)
    theirs = pl.ds(pl.multiple_of((1 - chan) * width, 128), width)
    lb[...] = dot(db[...], pool[mine, :])
    logit = dot(da[...], pool[mine, :]) + dot(ra[...], pool[theirs, :])
    ya[...] = (xoa[...].astype(F32) + jax.nn.sigmoid(logit) * dfa[...]).astype(BF)


def pool_last(p_lo, p_hi, pairs):
    def kernel(rb, lb, pool, dfb, xob, ya, out, y, sem):
        width = rb.shape[1]
        chan = lax.axis_index("chan")
        theirs = pl.ds(pl.multiple_of((1 - chan) * width, 128), width)
        copies = [pltpu.make_async_copy(ya, out.at[pl.ds(p_lo, p_hi - p_lo)], sem.at[0])]
        copies[0].start()
        for slot, (i, n) in enumerate([(0, p_lo)] + tiles(p_lo, rb.shape[0], 160)):
            logit = lb[i : i + n] + dot(rb[i : i + n], pool[theirs, :])
            y[i : i + n] = (
                xob[i : i + n].astype(F32) + jax.nn.sigmoid(logit) * dfb[i : i + n]
            ).astype(BF)
            at = i if i < p_lo else i - p_lo + p_hi
            copies.append(
                pltpu.make_async_copy(
                    y.at[pl.ds(i, n)], out.at[pl.ds(at, n)], sem.at[1 + slot]
                )
            )
            copies[-1].start()
        for c in copies:
            c.wait()

    return kernel


def swap_chan(a):
    return lax.ppermute(a, "chan", [(0, 1), (1, 0)])


def local(
    tower_input, dna_bases, base_embed, in_scale, entry_norm_shift,
    conv_w, mid_scale, mid_shift, point_w, pooling_weight,
):
    rows, width = tower_input.shape
    inner = conv_w.shape[3]
    a_lo, a_hi = D0, rows // 2 + 32
    c_lo, c_hi = 96, rows // 2 - 32
    b_hi = rows - D0
    n_a, n_b = a_hi - a_lo, b_hi - a_hi
    m_a = c_hi - c_lo
    m_b = rows - m_a
    dma = pltpu.SemaphoreType.DMA
    x0, h0, e_a, e_b, pa, w0, pw0, w1, s_in, b_in, own_mid = call(
        embed_first(a_lo, a_hi, rows, width),
        [
            ((rows, width), BF), ((rows, width), BF), ((HALO, width), BF), ((HALO, width), BF),
            ((n_a + EXTRA, inner), BF), ((3 * width, inner), BF), ((inner, width), BF),
            ((3 * width, inner), BF), ((2, width), F32), ((2, width), F32), ((4, inner), F32),
        ],
        [
            tower_input, dna_bases.T, base_embed, in_scale, entry_norm_shift, conv_w,
            mid_scale, mid_shift, point_w,
        ],
        [],
        [
            pltpu.VMEM((rows, width), BF), pltpu.VMEM(dna_bases.shape[::-1], jnp.int32),
            pltpu.VMEM(base_embed.shape, BF), pltpu.VMEM(mid_scale.shape, F32),
            pltpu.VMEM(mid_shift.shape, F32), dma((15,)),
        ],
    )
    ra = swap_chan(pa)
    count = lax.axis_size("seq")
    pairs_a = [(i, i ^ 1) for i in range(count)]
    pairs_b = [(i, ((i - 1) ^ 1) + 1) for i in range(1, count - 1)]
    r_a = lax.ppermute(e_a, "seq", pairs_a)
    r_b = lax.ppermute(e_b, "seq", pairs_b)
    pb, pw1, pool = call(
        first_rest(a_hi, b_hi),
        [((n_b, inner), BF), ((inner, width), BF), (pooling_weight.shape, BF)],
        [point_w, pooling_weight],
        [h0, w0],
        [dma((2,))],
    )
    rb = swap_chan(pb)
    pe, lo, hi = call(
        first_edges(rows),
        [((2 * HALO, inner), BF), ((HALO, width), BF), ((HALO, width), BF)],
        [],
        [r_a, r_b, h0, w0, s_in, b_in],
        [pltpu.VMEM((2 * (HALO + 2 * D0), width), BF)],
    )
    re = swap_chan(pe)
    x1a, h1a, qa, mid = call(
        second_first(a_lo, a_hi, c_lo, c_hi),
        [((n_a, width), BF), ((n_a, width), BF), ((m_a, inner), BF), ((4, inner), F32)],
        [],
        [pa, ra, x0, pw0, w1, s_in, b_in, own_mid],
    )
    sa = swap_chan(qa)
    x1b, qb = call(
        second_rest(rows, a_lo, a_hi, c_lo, c_hi),
        [((m_b, width), BF), ((m_b, inner), BF)],
        [],
        [pb, rb, pe, re, x0, lo, hi, x1a, h1a, pw0, w1, mid, s_in, b_in],
        [pltpu.VMEM((rows + 2 * D1, width), BF)],
    )
    sb = swap_chan(qb)
    da, dfa, xoa = call(
        last_point(c_lo - a_lo, m_a, 192),
        [((m_a // 2, width), BF), ((m_a // 2, width), F32), ((m_a // 2, width), BF)],
        [],
        [qa, sa, x1a, pw1, mid],
        [pltpu.VMEM((width // 128, m_a, 128), F32)],
    )
    ta = swap_chan(da)
    db, dfb, xob = call(
        last_point(0, m_b, 160),
        [((m_b // 2, width), BF), ((m_b // 2, width), F32), ((m_b // 2, width), BF)],
        [],
        [qb, sb, x1b, pw1, mid],
        [pltpu.VMEM((width // 128, m_b, 128), F32)],
    )
    tb = swap_chan(db)
    ya, lb = call(
        pool_first,
        [((m_a // 2, width), BF), ((m_b // 2, width), F32)],
        [],
        [da, ta, db, pool, dfa, xoa],
    )
    vm = [pltpu.with_memory_space_constraint(a, pltpu.VMEM) for a in (tb, lb, pool, dfb, xob, ya)]
    return pl.pallas_call(
        pool_last(c_lo // 2, c_hi // 2, rows // 2),
        out_shape=jax.ShapeDtypeStruct((rows // 2, width), BF),
        in_specs=[VM] * 6,
        out_specs=HBM,
        scratch_shapes=[pltpu.VMEM((m_b // 2, width), BF), dma((8,))],
        compiler_params=pltpu.CompilerParams(vmem_limit_bytes=GRANT),
    )(*vm)


def solution(mesh):
    return jax.shard_map(
        local,
        mesh=mesh,
        in_specs=(
            P(("groups", "seq"), "chan"),
            P(("groups", "seq"), None),
            P(None, "chan"),
            P(None, "chan"),
            P(None, "chan"),
            P(None, None, "chan", None),
            P(None, "chan"),
            P(None, "chan"),
            P(None, None, "chan"),
            P(None, "chan"),
        ),
        out_specs=P(("groups", "seq"), "chan"),
        check_vma=False,
    )
```

time: 147 us -> 37.7 us (0.26); the launches traced: 145 us -> 37.5 us
  waiting for transfers between devices: 51 us -> 8.03 us
  matrix products: 36.5 us -> 0 us
  local copies, waits for them, and re-layouts: 25.4 us -> 0 us
  Pallas kernels: 0 us -> 22.1 us
  between operations: 13.3 us -> 0.26 us
  other arithmetic: 7.14 us -> 0 us
  starting transfers between devices: 11.8 us -> 7.17 us
    dot_general x10 -> x0, matrix products: 36.5 us -> none  [the longest x2 10.3 us: project(): return jnp.dot(piece, weights, preferred_element_type=jnp.float32)]
    reduce_scatter x2 -> x0, waiting for transfers between devices: 25.6 us -> none  [local(): lax.psum_scatter(partial_value, 'chan', scatter_dimension=1, tiled=True)]
    all_gather x3 -> x0, waiting for transfers between devices: 23.3 us -> none  [the longest x2 22.2 us: local(): lax.all_gather(inner, 'chan', axis=1, tiled=True)]
    pallas_call x0 -> x9, Pallas kernels: none -> 22.1 us  [the longest x8 20.5 us: call(): pl.pallas_call(kernel, out_shape=[pltpu.VMEM(shape, dtype) for shape, dty...]
    slice x6 -> x0, local copies, waits for them, and re-layouts: 13.2 us -> none  [the longest x1 7.45 us: local(): result = pairs[:, 1] + weight_first * (pairs[:, 0] - pairs[:, 1])]
    reshape x2 -> x0, local copies, waits for them, and re-layouts: 10 us -> none  [the longest x1 5.15 us: local(): logit_pairs = score_logits.reshape(rows // 2, 2, width)]
    convert_element_type x3 -> x0, other arithmetic: 7.14 us -> none  [the longest x2 5.78 us: local(): gelu_tanh(partial_value * mid_scale[layer_idx] + mid_shift[layer_idx])]
    ppermute x4 -> x9, waiting for transfers between devices: 2.08 us -> 8.03 us  [the longest x1 3.74 us: local(): r_b = lax.ppermute(e_b, 'seq', pairs_b)]
  transfers between devices with their start and end apart: 9 -> 9, of which waited for: 6 -> 4; matrix products, arithmetic and copies ran while one was open for 14% -> 0% of each run, Pallas kernels for 0% -> 26%
where the time goes in v1:
time: 37.7 us; the launch traced here: 37.5 us
  Pallas kernels  22.1 us (59%)
  waiting for transfers between devices  8.03 us (21%)
  starting transfers between devices  7.17 us (19%)
    pallas_call x8, Pallas kernels, call(): pl.pallas_call(kernel, out_shape=[pltpu.VMEM(shape, dtype) for shape, dty...  20.5 us
    ppermute x1, waiting for transfers between devices, local(): r_b = lax.ppermute(e_b, 'seq', pairs_b)  3.74 us
    ppermute x7, starting transfers between devices, swap_chan(): return lax.ppermute(a, 'chan', [(0, 1), (1, 0)])  3.67 us
    ppermute x7, waiting for transfers between devices, swap_chan(): return lax.ppermute(a, 'chan', [(0, 1), (1, 0)])  3.28 us
    ppermute x1, starting transfers between devices, local(): r_b = lax.ppermute(e_b, 'seq', pairs_b)  2.19 us
    pallas_call x1, Pallas kernels, local(): pl.pallas_call(pool_last(c_lo // 2, c_hi // 2, rows // 2), out_shape=jax....  1.54 us
    ppermute x1, starting transfers between devices, local(): r_a = lax.ppermute(e_a, 'seq', pairs_a)  1.3 us
    ppermute x1, waiting for transfers between devices, local(): r_a = lax.ppermute(e_a, 'seq', pairs_a)  1.01 us
  transfers between devices with their start and end apart: 9, of which 4 were waited for; matrix products, arithmetic and copies ran while one was open for 0% of the time, Pallas kernels for 26%

profile of v1, /device:TPU:17, one launch (start us, length us, event | category | flops | bytes accessed | tf_op | source)
XLA Modules:
  0.0 37.5 jit_solution(2577948429224601401)
XLA Ops:
  0.0 6.6 %shard_map.100 = (bf16[1024,768]{1,0:T(8,128)(2,1)S(1)}, bf16[1024,768]{1,0:T(8,128)(2,1)S(1)}, bf16[80,768]{1,0:T(8,128)(2,1)S(1)}, bf16[80,768]{1,0:T(8,128)(2...) custom-call(bf16[1024,768]{1,0:T(8,128)(2,1)} %tower.1, ...), custom_call_target="tpu_custom_call" | custom-call | tf_op jit(solution)/shard_map/pallas_call | solution.py:22
  6.6 0.7 %collective-permute-start.4 = (bf16[528,768]{1,0:T(8,128)(2,1)S(1)}, bf16[528,768]{1,0:T(8,128)(2,1)S(1)}, u32[]{:S(2)}, u32[]{:S(2)}) collective-permute-start(bf16[528,768]{1,0:T(8,128)(2,1)S(1)} %get-tuple-element.47.pa), channel_id=1, source_target_pairs={{0,1},{1,0},{2,3},{3,2},{4,5},{5,4},{6,7},{7,6},{8,9},{9,8},{10,11... | collective-permute-start | bytes 2433032 | tf_op jit(solution)/shard_map/ppermute | solution.py:292
  7.4 2.1 %shard_map.101 = (bf16[448,768]{1,0:T(8,128)(2,1)S(1)}, bf16[768,768]{1,0:T(8,128)(2,1)S(1)}, bf16[1536,768]{1,0:T(8,128)(2,1)S(1)}) custom-call(bf16[2,768,768]{2,1,0:T(8,128)(2,1)} %point_w.3, bf16[1536,768]{1,0:T(8,128)(2,1)} %pool_w.1, bf16[1024,768]{1,0:T(8,128)(2,1)S(1)} %get-tuple-element.36.h0, bf16[2304,768]{1,0:T(8,128)(2,1)S(1)} %get-tuple-element.37.w0), custom_call_target="tpu_custom_call" | custom-call | tf_op jit(solution)/shard_map/pallas_call | solution.py:22
  9.4 0.1 collective-permute-start
  9.5 1.3 %collective-permute-start.1 = (bf16[80,768]{1,0:T(8,128)(2,1)S(1)}, bf16[80,768]{1,0:T(8,128)(2,1)S(1)}, u32[]{:S(2)}, u32[]{:S(2)}) collective-permute-start(bf16[80,768]{1,0:T(8,128)(2,1)S(1)} %get-tuple-element.39), channel_id=1, source_target_pairs={{0,2},{2,0},{4,6},{6,4},{8,10},{10,8},{12,14},{14,12},{1,3},{3,1},... | collective-permute-start | bytes 368648 | tf_op jit(solution)/shard_map/ppermute | solution.py:330
  10.8 2.2 %collective-permute-start.2 = (bf16[80,768]{1,0:T(8,128)(2,1)S(1)}, bf16[80,768]{1,0:T(8,128)(2,1)S(1)}, u32[]{:S(2)}, u32[]{:S(2)}) collective-permute-start(bf16[80,768]{1,0:T(8,128)(2,1)S(1)} %get-tuple-element.40), channel_id=1, source_target_pairs={{2,4},{4,2},{6,8},{8,6},{10,12},{12,10},{3,5},{5,3},{7,9},{9,7},{1... | collective-permute-start | bytes 368648 | tf_op jit(solution)/shard_map/ppermute | solution.py:331
  13.0 1.0 %collective-permute-done.1.r_a = bf16[80,768]{1,0:T(8,128)(2,1)S(1)} collective-permute-done((bf16[80,768]{1,0:T(8,128)(2,1)S(1)}, bf16[80,768]{1,0:T(8,128)(2,1)S(1)}, u32[]{:S(2)}, u32[]{:S(2)}) %collective-permute-start.1) | collective-permute-done | bytes 122912 | tf_op jit(solution)/shard_map/ppermute | solution.py:330
  14.0 3.7 %collective-permute-done.2.r_b = bf16[80,768]{1,0:T(8,128)(2,1)S(1)} collective-permute-done((bf16[80,768]{1,0:T(8,128)(2,1)S(1)}, bf16[80,768]{1,0:T(8,128)(2,1)S(1)}, u32[]{:S(2)}, u32[]{:S(2)}) %collective-permute-start.2) | collective-permute-done | bytes 122912 | tf_op jit(solution)/shard_map/ppermute | solution.py:331
  17.8 0.8 %shard_map.102 = (bf16[160,768]{1,0:T(8,128)(2,1)S(1)}, bf16[80,768]{1,0:T(8,128)(2,1)S(1)}, bf16[80,768]{1,0:T(8,128)(2,1)S(1)}) custom-call(bf16[80,768]{1,0:T(8,128)(2,1)S(1)} %collective-permute-done.1.r_a, bf16[80,768]{1,0:T(8,128)(2,1)S(1)} %collective-permute-done.2.r_b, bf16[1024,768]{1,0:T(8,128)(2,1)S(1)} %get-tuple-element.36.h0, ...), custom_call_target="tpu_custom_call" | custom-call | tf_op jit(solution)/shard_map/pallas_call | solution.py:22
  18.6 1.6 %collective-permute-start.3 = (bf16[160,768]{1,0:T(8,128)(2,1)S(1)}, bf16[160,768]{1,0:T(8,128)(2,1)S(1)}, u32[]{:S(2)}, u32[]{:S(2)}) collective-permute-start(bf16[160,768]{1,0:T(8,128)(2,1)S(1)} %get-tuple-element.43.pe), channel_id=1, source_target_pairs={{0,1},{1,0},{2,3},{3,2},{4,5},{5,4},{6,7},{7,6},{8,9},{9,8},{10,11... | collective-permute-start | bytes 737288 | tf_op jit(solution)/shard_map/ppermute | solution.py:292
  20.2 0.0 collective-permute-done.4.ra
  20.2 3.0 %shard_map.103 = (bf16[512,768]{1,0:T(8,128)(2,1)S(1)}, bf16[512,768]{1,0:T(8,128)(2,1)S(1)}, bf16[384,768]{1,0:T(8,128)(2,1)S(1)}, f32[4,768]{1,0:T(4,128)S(1)}) custom-call(bf16[528,768]{1,0:T(8,128)(2,1)S(1)} %get-tuple-element.47.pa, bf16[528,768]{1,0:T(8,128)(2,1)S(1)} %collective-permute-done.4.ra, bf16[1024,768]{1,0:T(8,128)(2,1)S(1)} %get-tuple-element.44.x0, ...), custom_call_target="tpu_custom_call" | custom-call | tf_op jit(solution)/shard_map/pallas_call | solution.py:22
  23.3 0.0 collective-permute-done.3.re
  23.3 0.0 collective-permute-done.rb
  23.3 4.2 %shard_map.104 = (bf16[640,768]{1,0:T(8,128)(2,1)S(1)}, bf16[640,768]{1,0:T(8,128)(2,1)S(1)}) custom-call(bf16[448,768]{1,0:T(8,128)(2,1)S(1)} %get-tuple-element.38.pb, bf16[448,768]{1,0:T(8,128)(2,1)S(1)} %collective-permute-done.rb, bf16[160,768]{1,0:T(8,128)(2,1)S(1)} %get-tuple-element.43.pe, bf16[160,768]{1,0:T(8,128)(2,1)S(1)} %collective-permute-done.3.re, ...), custom_call_target="tpu_custom_call" | custom-call | tf_op jit(solution)/shard_map/pallas_call | solution.py:22
  27.5 0.1 collective-permute-start.5
  27.6 0.5 %collective-permute-start.7 = (bf16[384,768]{1,0:T(8,128)(2,1)S(1)}, bf16[384,768]{1,0:T(8,128)(2,1)S(1)}, u32[]{:S(2)}, u32[]{:S(2)}) collective-permute-start(bf16[384,768]{1,0:T(8,128)(2,1)S(1)} %get-tuple-element.58.q), channel_id=1, source_target_pairs={{0,1},{1,0},{2,3},{3,2},{4,5},{5,4},{6,7},{7,6},{8,9},{9,8},{10,11... | collective-permute-start | bytes 1769480 | tf_op jit(solution)/shard_map/ppermute | solution.py:292
  28.1 2.1 %collective-permute-done.5.r = bf16[640,768]{1,0:T(8,128)(2,1)S(1)} collective-permute-done((bf16[640,768]{1,0:T(8,128)(2,1)S(1)}, bf16[640,768]{1,0:T(8,128)(2,1)S(1)}, u32[]{:S(2)}, u32[]{:S(2)}) %collective-permute-start.5) | collective-permute-done | bytes 983072 | tf_op jit(solution)/shard_map/ppermute | solution.py:292
  30.2 1.7 %shard_map.105 = (bf16[320,768]{1,0:T(8,128)(2,1)S(1)}, f32[320,768]{1,0:T(8,128)S(1)}, bf16[320,768]{1,0:T(8,128)(2,1)S(1)}) custom-call(bf16[640,768]{1,0:T(8,128)(2,1)S(1)} %get-tuple-element.54.q, bf16[640,768]{1,0:T(8,128)(2,1)S(1)} %collective-permute-done.5.r, bf16[640,768]{1,0:T(8,128)(2,1)S(1)} %get-tuple-element.55.x1, ...), custom_call_target="tpu_custom_call" | custom-call | tf_op jit(solution)/shard_map/pallas_call | solution.py:22
  31.8 0.2 collective-permute-start.6
  32.0 0.0 collective-permute-done.7.r
  32.0 1.1 %shard_map.106 = (bf16[192,768]{1,0:T(8,128)(2,1)S(1)}, f32[192,768]{1,0:T(8,128)S(1)}, bf16[192,768]{1,0:T(8,128)(2,1)S(1)}) custom-call(bf16[384,768]{1,0:T(8,128)(2,1)S(1)} %get-tuple-element.58.q, bf16[384,768]{1,0:T(8,128)(2,1)S(1)} %collective-permute-done.7.r, bf16[512,768]{1,0:T(8,128)(2,1)S(1)} %get-tuple-element.51.x1a.x1, ...), custom_call_target="tpu_custom_call" | custom-call | tf_op jit(solution)/shard_map/pallas_call | solution.py:22
  33.1 0.4 %collective-permute-start.8 = (bf16[192,768]{1,0:T(8,128)(2,1)S(1)}, bf16[192,768]{1,0:T(8,128)(2,1)S(1)}, u32[]{:S(2)}, u32[]{:S(2)}) collective-permute-start(bf16[192,768]{1,0:T(8,128)(2,1)S(1)} %get-tuple-element.59.da), channel_id=1, source_target_pairs={{0,1},{1,0},{2,3},{3,2},{4,5},{5,4},{6,7},{7,6},{8,9},{9,8},{10,11... | collective-permute-start | bytes 884744 | tf_op jit(solution)/shard_map/ppermute | solution.py:292
  33.6 1.2 %collective-permute-done.8.ra = bf16[192,768]{1,0:T(8,128)(2,1)S(1)} collective-permute-done((bf16[192,768]{1,0:T(8,128)(2,1)S(1)}, bf16[192,768]{1,0:T(8,128)(2,1)S(1)}, u32[]{:S(2)}, u32[]{:S(2)}) %collective-permute-start.8) | collective-permute-done | bytes 294944 | tf_op jit(solution)/shard_map/ppermute | solution.py:292
  34.8 1.1 %shard_map.107 = (bf16[192,768]{1,0:T(8,128)(2,1)S(1)}, f32[320,768]{1,0:T(8,128)S(1)}) custom-call(bf16[192,768]{1,0:T(8,128)(2,1)S(1)} %get-tuple-element.59.da, bf16[192,768]{1,0:T(8,128)(2,1)S(1)} %collective-permute-done.8.ra, bf16[320,768]{1,0:T(8,128)(2,1)S(1)} %get-tuple-element.57.db, bf16[1536,768]{1,0:T(8,128)(2,1)S(1)} %get-tuple-element.60.pool, ...), custom_call_target="tpu_custom_call" | custom-call | tf_op jit(solution)/shard_map/pallas_call | solution.py:22
  35.8 0.0 collective-permute-done.6.rb
  35.8 1.5 %shard_map.108 = bf16[512,768]{1,0:T(8,128)(2,1)} custom-call(bf16[320,768]{1,0:T(8,128)(2,1)S(1)} %collective-permute-done.6.rb, f32[320,768]{1,0:T(8,128)S(1)} %get-tuple-element.63.lb, bf16[1536,768]{1,0:T(8,128)(2,1)S(1)} %get-tuple-element.60.pool, f32[320,768]{1,0:T(8,128)S(1)} %get-tuple-element.64.dfb, bf16[320,768]{1,0:T(8,128)(2,1)S(1)} %get-tuple-element.65.xob, ...), custom_call_target="tpu_custom_call" | custom-call | tf_op jit(solution)/shard_map/pallas_call | solution.py:386
Async XLA Ops:
  6.6 13.6 %collective-permute-start.4 = (bf16[528,768]{1,0:T(8,128)(2,1)S(1)}, bf16[528,768]{1,0:T(8,128)(2,1)S(1)}, u32[]{:S(2)}, u32[]{:S(2)}) collective-permute-start(bf16[528,768]{1,0:T(8,128)(2,1)S(1)} %get-tuple-element.47.pa), channel_id=1, source_target_pairs={{0,1},{1,0},{2,3},{3,2},{4,5},{5,4},{6,7},{7,6},{8,9},{9,8},{10,11... | collective-permute-start | bytes 2433032 | tf_op jit(solution)/shard_map/ppermute | solution.py:292
  9.4 13.8 %collective-permute-start = (bf16[448,768]{1,0:T(8,128)(2,1)S(1)}, bf16[448,768]{1,0:T(8,128)(2,1)S(1)}, u32[]{:S(2)}, u32[]{:S(2)}) collective-permute-start(bf16[448,768]{1,0:T(8,128)(2,1)S(1)} %get-tuple-element.38.pb), channel_id=1, source_target_pairs={{0,1},{1,0},{2,3},{3,2},{4,5},{5,4},{6,7},{7,6},{8,9},{9,8},{10,11... | collective-permute-start | bytes 2064392 | tf_op jit(solution)/shard_map/ppermute | solution.py:292
  9.5 4.5 %collective-permute-start.1 = (bf16[80,768]{1,0:T(8,128)(2,1)S(1)}, bf16[80,768]{1,0:T(8,128)(2,1)S(1)}, u32[]{:S(2)}, u32[]{:S(2)}) collective-permute-start(bf16[80,768]{1,0:T(8,128)(2,1)S(1)} %get-tuple-element.39), channel_id=1, source_target_pairs={{0,2},{2,0},{4,6},{6,4},{8,10},{10,8},{12,14},{14,12},{1,3},{3,1},... | collective-permute-start | bytes 368648 | tf_op jit(solution)/shard_map/ppermute | solution.py:330
  10.8 6.9 %collective-permute-start.2 = (bf16[80,768]{1,0:T(8,128)(2,1)S(1)}, bf16[80,768]{1,0:T(8,128)(2,1)S(1)}, u32[]{:S(2)}, u32[]{:S(2)}) collective-permute-start(bf16[80,768]{1,0:T(8,128)(2,1)S(1)} %get-tuple-element.40), channel_id=1, source_target_pairs={{2,4},{4,2},{6,8},{8,6},{10,12},{12,10},{3,5},{5,3},{7,9},{9,7},{1... | collective-permute-start | bytes 368648 | tf_op jit(solution)/shard_map/ppermute | solution.py:331
  18.6 4.7 %collective-permute-start.3 = (bf16[160,768]{1,0:T(8,128)(2,1)S(1)}, bf16[160,768]{1,0:T(8,128)(2,1)S(1)}, u32[]{:S(2)}, u32[]{:S(2)}) collective-permute-start(bf16[160,768]{1,0:T(8,128)(2,1)S(1)} %get-tuple-element.43.pe), channel_id=1, source_target_pairs={{0,1},{1,0},{2,3},{3,2},{4,5},{5,4},{6,7},{7,6},{8,9},{9,8},{10,11... | collective-permute-start | bytes 737288 | tf_op jit(solution)/shard_map/ppermute | solution.py:292
  27.5 2.6 %collective-permute-start.5 = (bf16[640,768]{1,0:T(8,128)(2,1)S(1)}, bf16[640,768]{1,0:T(8,128)(2,1)S(1)}, u32[]{:S(2)}, u32[]{:S(2)}) collective-permute-start(bf16[640,768]{1,0:T(8,128)(2,1)S(1)} %get-tuple-element.54.q), channel_id=1, source_target_pairs={{0,1},{1,0},{2,3},{3,2},{4,5},{5,4},{6,7},{7,6},{8,9},{9,8},{10,11... | collective-permute-start | bytes 2949128 | tf_op jit(solution)/shard_map/ppermute | solution.py:292
  27.6 4.4 %collective-permute-start.7 = (bf16[384,768]{1,0:T(8,128)(2,1)S(1)}, bf16[384,768]{1,0:T(8,128)(2,1)S(1)}, u32[]{:S(2)}, u32[]{:S(2)}) collective-permute-start(bf16[384,768]{1,0:T(8,128)(2,1)S(1)} %get-tuple-element.58.q), channel_id=1, source_target_pairs={{0,1},{1,0},{2,3},{3,2},{4,5},{5,4},{6,7},{7,6},{8,9},{9,8},{10,11... | collective-permute-start | bytes 1769480 | tf_op jit(solution)/shard_map/ppermute | solution.py:292
  31.8 4.0 %collective-permute-start.6 = (bf16[320,768]{1,0:T(8,128)(2,1)S(1)}, bf16[320,768]{1,0:T(8,128)(2,1)S(1)}, u32[]{:S(2)}, u32[]{:S(2)}) collective-permute-start(bf16[320,768]{1,0:T(8,128)(2,1)S(1)} %get-tuple-element.57.db), channel_id=1, source_target_pairs={{0,1},{1,0},{2,3},{3,2},{4,5},{5,4},{6,7},{7,6},{8,9},{9,8},{10,11... | collective-permute-start | bytes 1474568 | tf_op jit(solution)/shard_map/ppermute | solution.py:292
  33.1 1.6 %collective-permute-start.8 = (bf16[192,768]{1,0:T(8,128)(2,1)S(1)}, bf16[192,768]{1,0:T(8,128)(2,1)S(1)}, u32[]{:S(2)}, u32[]{:S(2)}) collective-permute-start(bf16[192,768]{1,0:T(8,128)(2,1)S(1)} %get-tuple-element.59.da), channel_id=1, source_target_pairs={{0,1},{1,0},{2,3},{3,2},{4,5},{5,4},{6,7},{7,6},{8,9},{9,8},{10,11... | collective-permute-start | bytes 884744 | tf_op jit(solution)/shard_map/ppermute | solution.py:292

commit v2 on v1

--- a/solution.py
+++ b/solution.py
@@ -4,6 +4,7 @@
 from jax.experimental import pallas as pl
 from jax.experimental.pallas import tpu as pltpu
 from jax.sharding import PartitionSpec as P
+
 
 D0 = 32
 D1 = 48
@@ -194,41 +195,58 @@
     return kernel
 
 
-def second_rest(rows, a_lo, a_hi, c_lo, c_hi):
-    def kernel(
-        pb, rb, pe, re, x0, lo, hi, x1a, h1a, pw0, w1, mid, s_in, b_in, x1b, qb, h1
-    ):
-        seq = lax.axis_index("seq")
+def second_rest(rows, a_lo, a_hi, c_hi, e_hi):
+    def kernel(pb, rb, x0, x1a, h1a, pw0, w1, mid, s_in, b_in, x1b, x1t, h1t, qb, h1):
         b_hi = rows - D0
+        first = c_hi - D1
+        h1[0 : a_hi - first] = h1a[first - a_lo : a_hi - a_lo]
+        x1b[0 : a_hi - c_hi] = x1a[c_hi - a_lo : a_hi - a_lo]
         for i, n in tiles(0, b_hi - a_hi, 224):
             z = mid_rows(pb[i : i + n], rb[i : i + n], mid, 0)
             g = a_hi + i
             x = (x0[g : g + n].astype(F32) + dot(z, pw0[...])).astype(BF)
-            x1b[c_lo + g - c_hi : c_lo + g - c_hi + n] = x
-            h1[D1 + g : D1 + g + n] = act_rows(x, s_in, b_in, 1)
+            h1[g - first : g - first + n] = act_rows(x, s_in, b_in, 1)
+            keep = min(n, e_hi - g)
+            x1b[g - c_hi : g - c_hi + keep] = x[0:keep]
+            if keep < n:
+                x1t[...] = x[keep:]
+        h1t[...] = h1[e_hi - D1 - first : b_hi - first]
+        for i, n in tiles(c_hi, e_hi, 224):
+            qb[i - c_hi : i - c_hi + n] = conv_rows(h1, i - first, D1, n, w1).astype(BF)
+
+    return kernel
+
+
+def second_edges(rows, a_lo, c_lo, e_hi):
+    def kernel(pe, re, x0, lo, hi, x1a, h1a, x1t, h1t, pw0, w1, mid, s_in, b_in, x1c, qc, ext):
+        seq = lax.axis_index("seq")
         z = mid_rows(pe[...], re[...], mid, 0)
         base = jnp.concatenate(
             [lo[HALO - D1 : HALO], x0[0:D0], x0[rows - D0 : rows], hi[0:D1]], axis=0
         )
         x = (base.astype(F32) + dot(z, pw0[...])).astype(BF)
-        x1b[0:D0] = x[D1 : D1 + D0]
-        x1b[D0:c_lo] = x1a[0 : c_lo - a_lo]
-        x1b[c_lo : c_lo + a_hi - c_hi] = x1a[c_hi - a_lo : a_hi - a_lo]
-        x1b[c_lo + b_hi - c_hi : c_lo + rows - c_hi] = x[HALO : HALO + D0]
+        tail = rows - D0 - e_hi
+        x1c[0:D0] = x[D1 : D1 + D0]
+        x1c[D0:c_lo] = x1a[0 : c_lo - a_lo]
+        x1c[c_lo : c_lo + tail] = x1t[...]
+        x1c[c_lo + tail : c_lo + tail + D0] = x[HALO : HALO + D0]
         h = act_rows(x, s_in, b_in, 1)
         zero = jnp.zeros((D1, h.shape[1]), BF)
-        h1[0:D1] = jnp.where(seq == 0, zero, h[0:D1])
-        h1[D1:HALO] = h[D1:HALO]
-        h1[D1 + b_hi : D1 + rows] = h[HALO : HALO + D0]
-        h1[D1 + rows : 2 * D1 + rows] = jnp.where(
+        top = c_lo + 2 * D1
+        bottom = rows - e_hi + 2 * D1
+        ext[0:D1] = jnp.where(seq == 0, zero, h[0:D1])
+        ext[D1:HALO] = h[D1:HALO]
+        ext[HALO:top] = h1a[0 : c_lo + D1 - a_lo]
+        ext[top : top + bottom - HALO] = h1t[...]
+        ext[top + bottom - HALO : top + bottom - D1] = h[HALO : HALO + D0]
+        ext[top + bottom - D1 : top + bottom] = jnp.where(
             seq == lax.axis_size("seq") - 1, zero, h[HALO + D0 :]
         )
-        keep = 2 * D1
-        h1[D1 + a_lo : D1 + c_lo + D1] = h1a[0 : c_lo + D1 - a_lo]
-        h1[D1 + c_hi - D1 : D1 + a_hi] = h1a[c_hi - D1 - a_lo : a_hi - a_lo]
-        qb[0:c_lo] = conv_rows(h1, D1, D1, c_lo, w1).astype(BF)
-        for i, n in tiles(c_hi, rows, 272):
-            qb[c_lo + i - c_hi : c_lo + i - c_hi + n] = conv_rows(h1, D1 + i, D1, n, w1).astype(BF)
+        lhs = [
+            jnp.concatenate([ext[s + k * D1 : s + k * D1 + n] for k in range(3)], axis=1)
+            for s, n in ((0, c_lo), (top, rows - e_hi))
+        ]
+        qc[...] = dot(jnp.concatenate(lhs, axis=0), w1[...]).astype(BF)
 
     return kernel
 
@@ -253,35 +271,36 @@
     return kernel
 
 
-def pool_first(da, ra, db, pool, dfa, xoa, ya, lb):
+def pool_first(da, ra, db, rb, dc, pool, dfa, xoa, dfb, xob, ya, yb, lc):
     width = da.shape[1]
     chan = lax.axis_index("chan")
     mine = pl.ds(pl.multiple_of(chan * width, 128), width)
     theirs = pl.ds(pl.multiple_of((1 - chan) * width, 128), width)
-    lb[...] = dot(db[...], pool[mine, :])
-    logit = dot(da[...], pool[mine, :]) + dot(ra[...], pool[theirs, :])
-    ya[...] = (xoa[...].astype(F32) + jax.nn.sigmoid(logit) * dfa[...]).astype(BF)
-
-
-def pool_last(p_lo, p_hi, pairs):
-    def kernel(rb, lb, pool, dfb, xob, ya, out, y, sem):
-        width = rb.shape[1]
+    lc[...] = dot(dc[...], pool[mine, :])
+    for d, r, df, xo, y in ((da, ra, dfa, xoa, ya), (db, rb, dfb, xob, yb)):
+        logit = dot(d[...], pool[mine, :]) + dot(r[...], pool[theirs, :])
+        y[...] = (xo[...].astype(F32) + jax.nn.sigmoid(logit) * df[...]).astype(BF)
+
+
+def pool_last(p_lo, p_hi, p_end):
+    def kernel(rc, lc, pool, dfc, xoc, ya, yb, out, y, sem):
+        width = rc.shape[1]
         chan = lax.axis_index("chan")
         theirs = pl.ds(pl.multiple_of((1 - chan) * width, 128), width)
-        copies = [pltpu.make_async_copy(ya, out.at[pl.ds(p_lo, p_hi - p_lo)], sem.at[0])]
+        copy = pltpu.make_async_copy
+        last = rc.shape[0] - p_lo
+        copies = [
+            copy(ya, out.at[pl.ds(p_lo, p_hi - p_lo)], sem.at[0]),
+            copy(yb, out.at[pl.ds(p_hi, p_end - p_hi)], sem.at[1]),
+            copy(y.at[pl.ds(0, p_lo)], out.at[pl.ds(0, p_lo)], sem.at[2]),
+            copy(y.at[pl.ds(p_lo, last)], out.at[pl.ds(p_end, last)], sem.at[3]),
+        ]
         copies[0].start()
-        for slot, (i, n) in enumerate([(0, p_lo)] + tiles(p_lo, rb.shape[0], 160)):
-            logit = lb[i : i + n] + dot(rb[i : i + n], pool[theirs, :])
-            y[i : i + n] = (
-                xob[i : i + n].astype(F32) + jax.nn.sigmoid(logit) * dfb[i : i + n]
-            ).astype(BF)
-            at = i if i < p_lo else i - p_lo + p_hi
-            copies.append(
-                pltpu.make_async_copy(
-                    y.at[pl.ds(i, n)], out.at[pl.ds(at, n)], sem.at[1 + slot]
-                )
-            )
-            copies[-1].start()
+        copies[1].start()
+        logit = lc[...] + dot(rc[...], pool[theirs, :])
+        y[...] = (xoc[...].astype(F32) + jax.nn.sigmoid(logit) * dfc[...]).astype(BF)
+        copies[2].start()
+        copies[3].start()
         for c in copies:
             c.wait()
 
@@ -299,11 +318,11 @@
     rows, width = tower_input.shape
     inner = conv_w.shape[3]
     a_lo, a_hi = D0, rows // 2 + 32
-    c_lo, c_hi = 96, rows // 2 - 32
+    c_lo, c_hi, e_hi = 96, rows // 2 - 32, rows - 96
     b_hi = rows - D0
     n_a, n_b = a_hi - a_lo, b_hi - a_hi
-    m_a = c_hi - c_lo
-    m_b = rows - m_a
+    m_a, m_b = c_hi - c_lo, e_hi - c_hi
+    m_c = rows - m_a - m_b
     dma = pltpu.SemaphoreType.DMA
     x0, h0, e_a, e_b, pa, w0, pw0, w1, s_in, b_in, own_mid = call(
         embed_first(a_lo, a_hi, rows, width),
@@ -337,6 +356,13 @@
         [dma((2,))],
     )
     rb = swap_chan(pb)
+    x1a, h1a, qa, mid = call(
+        second_first(a_lo, a_hi, c_lo, c_hi),
+        [((n_a, width), BF), ((n_a, width), BF), ((m_a, inner), BF), ((4, inner), F32)],
+        [],
+        [pa, ra, x0, pw0, w1, s_in, b_in, own_mid],
+    )
+    sa = swap_chan(qa)
     pe, lo, hi = call(
         first_edges(rows),
         [((2 * HALO, inner), BF), ((HALO, width), BF), ((HALO, width), BF)],
@@ -345,50 +371,54 @@
         [pltpu.VMEM((2 * (HALO + 2 * D0), width), BF)],
     )
     re = swap_chan(pe)
-    x1a, h1a, qa, mid = call(
-        second_first(a_lo, a_hi, c_lo, c_hi),
-        [((n_a, width), BF), ((n_a, width), BF), ((m_a, inner), BF), ((4, inner), F32)],
-        [],
-        [pa, ra, x0, pw0, w1, s_in, b_in, own_mid],
-    )
-    sa = swap_chan(qa)
-    x1b, qb = call(
-        second_rest(rows, a_lo, a_hi, c_lo, c_hi),
-        [((m_b, width), BF), ((m_b, inner), BF)],
-        [],
-        [pb, rb, pe, re, x0, lo, hi, x1a, h1a, pw0, w1, mid, s_in, b_in],
-        [pltpu.VMEM((rows + 2 * D1, width), BF)],
+    x1b, x1t, h1t, qb = call(
+        second_rest(rows, a_lo, a_hi, c_hi, e_hi),
+        [
+            ((m_b, width), BF), ((b_hi - e_hi, width), BF),
+            ((b_hi - e_hi + D1, width), BF), ((m_b, inner), BF),
+        ],
+        [],
+        [pb, rb, x0, x1a, h1a, pw0, w1, mid, s_in, b_in],
+        [pltpu.VMEM((b_hi - c_hi + D1, width), BF)],
     )
     sb = swap_chan(qb)
-    da, dfa, xoa = call(
-        last_point(c_lo - a_lo, m_a, 192),
-        [((m_a // 2, width), BF), ((m_a // 2, width), F32), ((m_a // 2, width), BF)],
-        [],
-        [qa, sa, x1a, pw1, mid],
-        [pltpu.VMEM((width // 128, m_a, 128), F32)],
-    )
-    ta = swap_chan(da)
-    db, dfb, xob = call(
-        last_point(0, m_b, 160),
-        [((m_b // 2, width), BF), ((m_b // 2, width), F32), ((m_b // 2, width), BF)],
-        [],
-        [qb, sb, x1b, pw1, mid],
-        [pltpu.VMEM((width // 128, m_b, 128), F32)],
-    )
-    tb = swap_chan(db)
-    ya, lb = call(
+    x1c, qc = call(
+        second_edges(rows, a_lo, c_lo, e_hi),
+        [((m_c, width), BF), ((m_c, inner), BF)],
+        [],
+        [pe, re, x0, lo, hi, x1a, h1a, x1t, h1t, pw0, w1, mid, s_in, b_in],
+        [pltpu.VMEM((m_c + 4 * D1, width), BF)],
+    )
+    sc = swap_chan(qc)
+    ends = []
+    for q, s, x1, base, m, step in (
+        (qa, sa, x1a, c_lo - a_lo, m_a, 128), (qb, sb, x1b, 0, m_b, 128), (qc, sc, x1c, 0, m_c, 96)
+    ):
+        dm, df, xo = call(
+            last_point(base, m, step),
+            [((m // 2, width), BF), ((m // 2, width), F32), ((m // 2, width), BF)],
+            [],
+            [q, s, x1, pw1, mid],
+            [pltpu.VMEM((width // 128, m, 128), F32)],
+        )
+        ends.append((dm, swap_chan(dm), df, xo))
+    (da, ta, dfa, xoa), (db, tb, dfb, xob), (dc, tc, dfc, xoc) = ends
+    ya, yb, lc = call(
         pool_first,
-        [((m_a // 2, width), BF), ((m_b // 2, width), F32)],
-        [],
-        [da, ta, db, pool, dfa, xoa],
-    )
-    vm = [pltpu.with_memory_space_constraint(a, pltpu.VMEM) for a in (tb, lb, pool, dfb, xob, ya)]
+        [((m_a // 2, width), BF), ((m_b // 2, width), BF), ((m_c // 2, width), F32)],
+        [],
+        [da, ta, db, tb, dc, pool, dfa, xoa, dfb, xob],
+    )
+    vm = [
+        pltpu.with_memory_space_constraint(a, pltpu.VMEM)
+        for a in (tc, lc, pool, dfc, xoc, ya, yb)
+    ]
     return pl.pallas_call(
-        pool_last(c_lo // 2, c_hi // 2, rows // 2),
+        pool_last(c_lo // 2, c_hi // 2, e_hi // 2),
         out_shape=jax.ShapeDtypeStruct((rows // 2, width), BF),
-        in_specs=[VM] * 6,
+        in_specs=[VM] * 7,
         out_specs=HBM,
-        scratch_shapes=[pltpu.VMEM((m_b // 2, width), BF), dma((8,))],
+        scratch_shapes=[pltpu.VMEM((m_c // 2, width), BF), dma((4,))],
         compiler_params=pltpu.CompilerParams(vmem_limit_bytes=GRANT),
     )(*vm)
 

time: 37.7 us -> 36.5 us (0.968)
  waiting for transfers between devices: 8.03 us -> 6.31 us
  starting transfers between devices: 7.17 us -> 7.81 us
    ppermute x7 -> x9, waiting for transfers between devices: 3.28 us -> 1.55 us  [swap_chan(): return lax.ppermute(a, 'chan', [(0, 1), (1, 0)])]
    ppermute x7 -> x9, starting transfers between devices: 3.67 us -> 4.37 us  [swap_chan(): return lax.ppermute(a, 'chan', [(0, 1), (1, 0)])]
    pallas_call x1, Pallas kernels: 1.54 us -> 1.06 us  [local(): pl.pallas_call(pool_last(c_lo // 2, c_hi // 2, e_hi // 2), out_shape=jax....]
    pallas_call x8 -> x10, Pallas kernels: 20.5 us -> 20.9 us  [call(): pl.pallas_call(kernel, out_shape=[pltpu.VMEM(shape, dtype) for shape, dty...]
  transfers between devices with their start and end apart: 9 -> 11, of which waited for: 4 -> 4; matrix products, arithmetic and copies ran while one was open for 0% -> 0% of each run, Pallas kernels for 26% -> 31%
where the time goes in v2:
time: 36.5 us; the launch traced here: 36.4 us
  Pallas kernels  22 us (60%)
  starting transfers between devices  7.81 us (21%)
  waiting for transfers between devices  6.31 us (17%)
    pallas_call x10, Pallas kernels, call(): pl.pallas_call(kernel, out_shape=[pltpu.VMEM(shape, dtype) for shape, dty...  20.9 us
    ppermute x9, starting transfers between devices, swap_chan(): return lax.ppermute(a, 'chan', [(0, 1), (1, 0)])  4.37 us
    ppermute x1, waiting for transfers between devices, local(): r_b = lax.ppermute(e_b, 'seq', pairs_b)  3.74 us
    ppermute x1, starting transfers between devices, local(): r_b = lax.ppermute(e_b, 'seq', pairs_b)  2.19 us
    ppermute x9, waiting for transfers between devices, swap_chan(): return lax.ppermute(a, 'chan', [(0, 1), (1, 0)])  1.55 us
    ppermute x1, starting transfers between devices, local(): r_a = lax.ppermute(e_a, 'seq', pairs_a)  1.24 us
    pallas_call x1, Pallas kernels, local(): pl.pallas_call(pool_last(c_lo // 2, c_hi // 2, e_hi // 2), out_shape=jax....  1.06 us
    ppermute x1, waiting for transfers between devices, local(): r_a = lax.ppermute(e_a, 'seq', pairs_a)  1.01 us
  transfers between devices with their start and end apart: 11, of which 4 were waited for; matrix products, arithmetic and copies ran while one was open for 0% of the time, Pallas kernels for 31%

profile of v2, /device:TPU:17, one launch (start us, length us, event | category | flops | bytes accessed | tf_op | source)
XLA Modules:
  0.0 36.4 jit_solution(13277443906449690923)
XLA Ops:
  0.0 6.6 %shard_map.100 = (bf16[1024,768]{1,0:T(8,128)(2,1)S(1)}, bf16[1024,768]{1,0:T(8,128)(2,1)S(1)}, bf16[80,768]{1,0:T(8,128)(2,1)S(1)}, bf16[80,768]{1,0:T(8,128)(2...) custom-call(bf16[1024,768]{1,0:T(8,128)(2,1)} %tower.1, ...), custom_call_target="tpu_custom_call" | custom-call | tf_op jit(solution)/shard_map/pallas_call | solution.py:23
  6.6 0.7 %collective-permute-start.3 = (bf16[528,768]{1,0:T(8,128)(2,1)S(1)}, bf16[528,768]{1,0:T(8,128)(2,1)S(1)}, u32[]{:S(2)}, u32[]{:S(2)}) collective-permute-start(bf16[528,768]{1,0:T(8,128)(2,1)S(1)} %get-tuple-element.54.pa), channel_id=1, source_target_pairs={{0,1},{1,0},{2,3},{3,2},{4,5},{5,4},{6,7},{7,6},{8,9},{9,8},{10,11... | collective-permute-start | bytes 2433032 | tf_op jit(solution)/shard_map/ppermute | solution.py:311
  7.3 2.1 %shard_map.103 = (bf16[448,768]{1,0:T(8,128)(2,1)S(1)}, bf16[768,768]{1,0:T(8,128)(2,1)S(1)}, bf16[1536,768]{1,0:T(8,128)(2,1)S(1)}) custom-call(bf16[2,768,768]{2,1,0:T(8,128)(2,1)} %point_w.3, bf16[1536,768]{1,0:T(8,128)(2,1)} %pool_w.1, bf16[1024,768]{1,0:T(8,128)(2,1)S(1)} %get-tuple-element.46.h0, bf16[2304,768]{1,0:T(8,128)(2,1)S(1)} %get-tuple-element.47.w0), custom_call_target="tpu_custom_call" | custom-call | tf_op jit(solution)/shard_map/pallas_call | solution.py:23
  9.4 0.1 collective-permute-start.4
  9.5 0.0 collective-permute-done.3.ra
  9.5 3.0 %shard_map.102 = (bf16[512,768]{1,0:T(8,128)(2,1)S(1)}, bf16[512,768]{1,0:T(8,128)(2,1)S(1)}, bf16[384,768]{1,0:T(8,128)(2,1)S(1)}, f32[4,768]{1,0:T(4,128)S(1)}) custom-call(bf16[528,768]{1,0:T(8,128)(2,1)S(1)} %get-tuple-element.54.pa, bf16[528,768]{1,0:T(8,128)(2,1)S(1)} %collective-permute-done.3.ra, bf16[1024,768]{1,0:T(8,128)(2,1)S(1)} %get-tuple-element.51.x0, ...), custom_call_target="tpu_custom_call" | custom-call | tf_op jit(solution)/shard_map/pallas_call | solution.py:23
  12.5 0.0 collective-permute-done.4.rb
  12.6 2.9 %shard_map.104 = (bf16[448,768]{1,0:T(8,128)(2,1)S(1)}, bf16[64,768]{1,0:T(8,128)(2,1)S(1)}, bf16[112,768]{1,0:T(8,128)(2,1)S(1)}, bf16[448,768]{1,0:T(8,128)(2,1)S(1)}) custom-call(bf16[448,768]{1,0:T(8,128)(2,1)S(1)} %get-tuple-element.60.pb, bf16[448,768]{1,0:T(8,128)(2,1)S(1)} %collective-permute-done.4.rb, bf16[1024,768]{1,0:T(8,128)(2,1)S(1)} %get-tuple-element.51.x0, ...), custom_call_target="tpu_custom_call" | custom-call | tf_op jit(solution)/shard_map/pallas_call | solution.py:23
  15.5 0.6 %collective-permute-start.9 = (bf16[448,768]{1,0:T(8,128)(2,1)S(1)}, bf16[448,768]{1,0:T(8,128)(2,1)S(1)}, u32[]{:S(2)}, u32[]{:S(2)}) collective-permute-start(bf16[448,768]{1,0:T(8,128)(2,1)S(1)} %get-tuple-element.70.q), channel_id=1, source_target_pairs={{0,1},{1,0},{2,3},{3,2},{4,5},{5,4},{6,7},{7,6},{8,9},{9,8},{10,11... | collective-permute-start | bytes 2064392 | tf_op jit(solution)/shard_map/ppermute | solution.py:311
  16.0 0.1 collective-permute-start.7
  16.1 1.2 %collective-permute-start = (bf16[80,768]{1,0:T(8,128)(2,1)S(1)}, bf16[80,768]{1,0:T(8,128)(2,1)S(1)}, u32[]{:S(2)}, u32[]{:S(2)}) collective-permute-start(bf16[80,768]{1,0:T(8,128)(2,1)S(1)} %get-tuple-element.44), channel_id=1, source_target_pairs={{0,2},{2,0},{4,6},{6,4},{8,10},{10,8},{12,14},{14,12},{1,3},{3,1},... | collective-permute-start | bytes 368648 | tf_op jit(solution)/shard_map/ppermute | solution.py:349
  17.3 2.2 %collective-permute-start.1 = (bf16[80,768]{1,0:T(8,128)(2,1)S(1)}, bf16[80,768]{1,0:T(8,128)(2,1)S(1)}, u32[]{:S(2)}, u32[]{:S(2)}) collective-permute-start(bf16[80,768]{1,0:T(8,128)(2,1)S(1)} %get-tuple-element.45), channel_id=1, source_target_pairs={{2,4},{4,2},{6,8},{8,6},{10,12},{12,10},{3,5},{5,3},{7,9},{9,7},{1... | collective-permute-start | bytes 368648 | tf_op jit(solution)/shard_map/ppermute | solution.py:350
  19.5 1.0 %collective-permute-done.r_a = bf16[80,768]{1,0:T(8,128)(2,1)S(1)} collective-permute-done((bf16[80,768]{1,0:T(8,128)(2,1)S(1)}, bf16[80,768]{1,0:T(8,128)(2,1)S(1)}, u32[]{:S(2)}, u32[]{:S(2)}) %collective-permute-start) | collective-permute-done | bytes 122912 | tf_op jit(solution)/shard_map/ppermute | solution.py:349
  20.5 3.7 %collective-permute-done.1.r_b = bf16[80,768]{1,0:T(8,128)(2,1)S(1)} collective-permute-done((bf16[80,768]{1,0:T(8,128)(2,1)S(1)}, bf16[80,768]{1,0:T(8,128)(2,1)S(1)}, u32[]{:S(2)}, u32[]{:S(2)}) %collective-permute-start.1) | collective-permute-done | bytes 122912 | tf_op jit(solution)/shard_map/ppermute | solution.py:350
  24.3 0.8 %shard_map.101 = (bf16[160,768]{1,0:T(8,128)(2,1)S(1)}, bf16[80,768]{1,0:T(8,128)(2,1)S(1)}, bf16[80,768]{1,0:T(8,128)(2,1)S(1)}) custom-call(bf16[80,768]{1,0:T(8,128)(2,1)S(1)} %collective-permute-done.r_a, bf16[80,768]{1,0:T(8,128)(2,1)S(1)} %collective-permute-done.1.r_b, bf16[1024,768]{1,0:T(8,128)(2,1)S(1)} %get-tuple-element.46.h0, ...), custom_call_target="tpu_custom_call" | custom-call | tf_op jit(solution)/shard_map/pallas_call | solution.py:23
  25.1 1.6 %collective-permute-start.2 = (bf16[160,768]{1,0:T(8,128)(2,1)S(1)}, bf16[160,768]{1,0:T(8,128)(2,1)S(1)}, u32[]{:S(2)}, u32[]{:S(2)}) collective-permute-start(bf16[160,768]{1,0:T(8,128)(2,1)S(1)} %get-tuple-element.50.pe), channel_id=1, source_target_pairs={{0,1},{1,0},{2,3},{3,2},{4,5},{5,4},{6,7},{7,6},{8,9},{9,8},{10,11... | collective-permute-start | bytes 737288 | tf_op jit(solution)/shard_map/ppermute | solution.py:311
  26.7 1.1 %collective-permute-done.2.re = bf16[160,768]{1,0:T(8,128)(2,1)S(1)} collective-permute-done((bf16[160,768]{1,0:T(8,128)(2,1)S(1)}, bf16[160,768]{1,0:T(8,128)(2,1)S(1)}, u32[]{:S(2)}, u32[]{:S(2)}) %collective-permute-start.2) | collective-permute-done | bytes 245792 | tf_op jit(solution)/shard_map/ppermute | solution.py:311
  27.9 1.3 %shard_map.105 = (bf16[192,768]{1,0:T(8,128)(2,1)S(1)}, bf16[192,768]{1,0:T(8,128)(2,1)S(1)}) custom-call(bf16[160,768]{1,0:T(8,128)(2,1)S(1)} %get-tuple-element.50.pe, bf16[160,768]{1,0:T(8,128)(2,1)S(1)} %collective-permute-done.2.re, bf16[1024,768]{1,0:T(8,128)(2,1)S(1)} %get-tuple-element.51.x0, bf16[80,768]{1,0:T(8,128)(2,1)S(1)} %get-tuple-element.52.lo, ...), custom_call_target="tpu_custom_call" | custom-call | tf_op jit(solution)/shard_map/pallas_call | solution.py:23
  29.2 0.4 %collective-permute-start.5 = (bf16[192,768]{1,0:T(8,128)(2,1)S(1)}, bf16[192,768]{1,0:T(8,128)(2,1)S(1)}, u32[]{:S(2)}, u32[]{:S(2)}) collective-permute-start(bf16[192,768]{1,0:T(8,128)(2,1)S(1)} %get-tuple-element.64.q), channel_id=1, source_target_pairs={{0,1},{1,0},{2,3},{3,2},{4,5},{5,4},{6,7},{7,6},{8,9},{9,8},{10,11... | collective-permute-start | bytes 884744 | tf_op jit(solution)/shard_map/ppermute | solution.py:311
  29.6 0.0 collective-permute-done.9.r
  29.6 1.2 %shard_map.108 = (bf16[224,768]{1,0:T(8,128)(2,1)S(1)}, f32[224,768]{1,0:T(8,128)S(1)}, bf16[224,768]{1,0:T(8,128)(2,1)S(1)}) custom-call(bf16[448,768]{1,0:T(8,128)(2,1)S(1)} %get-tuple-element.70.q, bf16[448,768]{1,0:T(8,128)(2,1)S(1)} %collective-permute-done.9.r, bf16[448,768]{1,0:T(8,128)(2,1)S(1)} %get-tuple-element.71.x1, ...), custom_call_target="tpu_custom_call" | custom-call | tf_op jit(solution)/shard_map/pallas_call | solution.py:23
  30.8 0.2 collective-permute-start.10
  31.0 0.0 collective-permute-done.7.r
  31.0 1.0 %shard_map.107 = (bf16[192,768]{1,0:T(8,128)(2,1)S(1)}, f32[192,768]{1,0:T(8,128)S(1)}, bf16[192,768]{1,0:T(8,128)(2,1)S(1)}) custom-call(bf16[384,768]{1,0:T(8,128)(2,1)S(1)} %get-tuple-element.68.q, bf16[384,768]{1,0:T(8,128)(2,1)S(1)} %collective-permute-done.7.r, bf16[512,768]{1,0:T(8,128)(2,1)S(1)} %get-tuple-element.58.x1a.x1, ...), custom_call_target="tpu_custom_call" | custom-call | tf_op jit(solution)/shard_map/pallas_call | solution.py:23
  32.1 0.4 %collective-permute-start.8 = (bf16[192,768]{1,0:T(8,128)(2,1)S(1)}, bf16[192,768]{1,0:T(8,128)(2,1)S(1)}, u32[]{:S(2)}, u32[]{:S(2)}) collective-permute-start(bf16[192,768]{1,0:T(8,128)(2,1)S(1)} %get-tuple-element.69.da), channel_id=1, source_target_pairs={{0,1},{1,0},{2,3},{3,2},{4,5},{5,4},{6,7},{7,6},{8,9},{9,8},{10,11... | collective-permute-start | bytes 884744 | tf_op jit(solution)/shard_map/ppermute | solution.py:311
  32.5 0.0 collective-permute-done.5.r
  32.5 0.6 %shard_map.106 = (bf16[96,768]{1,0:T(8,128)(2,1)S(1)}, f32[96,768]{1,0:T(8,128)S(1)}, bf16[96,768]{1,0:T(8,128)(2,1)S(1)}) custom-call(bf16[192,768]{1,0:T(8,128)(2,1)S(1)} %get-tuple-element.64.q, bf16[192,768]{1,0:T(8,128)(2,1)S(1)} %collective-permute-done.5.r, bf16[192,768]{1,0:T(8,128)(2,1)S(1)} %get-tuple-element.65.x1, ...), custom_call_target="tpu_custom_call" | custom-call | tf_op jit(solution)/shard_map/pallas_call | solution.py:23
  33.1 0.2 collective-permute-start.6
  33.3 0.4 %collective-permute-done.8.ra = bf16[192,768]{1,0:T(8,128)(2,1)S(1)} collective-permute-done((bf16[192,768]{1,0:T(8,128)(2,1)S(1)}, bf16[192,768]{1,0:T(8,128)(2,1)S(1)}, u32[]{:S(2)}, u32[]{:S(2)}) %collective-permute-start.8) | collective-permute-done | bytes 294944 | tf_op jit(solution)/shard_map/ppermute | solution.py:311
  33.7 0.0 collective-permute-done.10.rb
  33.7 1.4 %shard_map.109 = (bf16[192,768]{1,0:T(8,128)(2,1)S(1)}, bf16[224,768]{1,0:T(8,128)(2,1)S(1)}, f32[96,768]{1,0:T(8,128)S(1)}) custom-call(bf16[192,768]{1,0:T(8,128)(2,1)S(1)} %get-tuple-element.69.da, bf16[192,768]{1,0:T(8,128)(2,1)S(1)} %collective-permute-done.8.ra, bf16[224,768]{1,0:T(8,128)(2,1)S(1)} %get-tuple-element.72.db, ...), custom_call_target="tpu_custom_call" | custom-call | tf_op jit(solution)/shard_map/pallas_call | solution.py:23
  35.1 0.0 collective-permute-done.6.rc
  35.2 1.1 %shard_map.110 = bf16[512,768]{1,0:T(8,128)(2,1)} custom-call(bf16[96,768]{1,0:T(8,128)(2,1)S(1)} %collective-permute-done.6.rc, f32[96,768]{1,0:T(8,128)S(1)} %get-tuple-element.78.lc, bf16[1536,768]{1,0:T(8,128)(2,1)S(1)} %get-tuple-element.73.pool, f32[96,768]{1,0:T(8,128)S(1)} %get-tuple-element.79.dfc, bf16[96,768]{1,0:T(8,128)(2,1)S(1)} %get-tuple-element.80.xoc, ...), custom_call_target="tpu_custom_call" | custom-call | tf_op jit(solution)/shard_map/pallas_call | solution.py:416
Async XLA Ops:
  6.6 2.9 %collective-permute-start.3 = (bf16[528,768]{1,0:T(8,128)(2,1)S(1)}, bf16[528,768]{1,0:T(8,128)(2,1)S(1)}, u32[]{:S(2)}, u32[]{:S(2)}) collective-permute-start(bf16[528,768]{1,0:T(8,128)(2,1)S(1)} %get-tuple-element.54.pa), channel_id=1, source_target_pairs={{0,1},{1,0},{2,3},{3,2},{4,5},{5,4},{6,7},{7,6},{8,9},{9,8},{10,11... | collective-permute-start | bytes 2433032 | tf_op jit(solution)/shard_map/ppermute | solution.py:311
  9.4 3.1 %collective-permute-start.4 = (bf16[448,768]{1,0:T(8,128)(2,1)S(1)}, bf16[448,768]{1,0:T(8,128)(2,1)S(1)}, u32[]{:S(2)}, u32[]{:S(2)}) collective-permute-start(bf16[448,768]{1,0:T(8,128)(2,1)S(1)} %get-tuple-element.60.pb), channel_id=1, source_target_pairs={{0,1},{1,0},{2,3},{3,2},{4,5},{5,4},{6,7},{7,6},{8,9},{9,8},{10,11... | collective-permute-start | bytes 2064392 | tf_op jit(solution)/shard_map/ppermute | solution.py:311
  15.5 14.2 %collective-permute-start.9 = (bf16[448,768]{1,0:T(8,128)(2,1)S(1)}, bf16[448,768]{1,0:T(8,128)(2,1)S(1)}, u32[]{:S(2)}, u32[]{:S(2)}) collective-permute-start(bf16[448,768]{1,0:T(8,128)(2,1)S(1)} %get-tuple-element.70.q), channel_id=1, source_target_pairs={{0,1},{1,0},{2,3},{3,2},{4,5},{5,4},{6,7},{7,6},{8,9},{9,8},{10,11... | collective-permute-start | bytes 2064392 | tf_op jit(solution)/shard_map/ppermute | solution.py:311
  16.0 15.0 %collective-permute-start.7 = (bf16[384,768]{1,0:T(8,128)(2,1)S(1)}, bf16[384,768]{1,0:T(8,128)(2,1)S(1)}, u32[]{:S(2)}, u32[]{:S(2)}) collective-permute-start(bf16[384,768]{1,0:T(8,128)(2,1)S(1)} %get-tuple-element.68.q), channel_id=1, source_target_pairs={{0,1},{1,0},{2,3},{3,2},{4,5},{5,4},{6,7},{7,6},{8,9},{9,8},{10,11... | collective-permute-start | bytes 1769480 | tf_op jit(solution)/shard_map/ppermute | solution.py:311
  16.1 4.4 %collective-permute-start = (bf16[80,768]{1,0:T(8,128)(2,1)S(1)}, bf16[80,768]{1,0:T(8,128)(2,1)S(1)}, u32[]{:S(2)}, u32[]{:S(2)}) collective-permute-start(bf16[80,768]{1,0:T(8,128)(2,1)S(1)} %get-tuple-element.44), channel_id=1, source_target_pairs={{0,2},{2,0},{4,6},{6,4},{8,10},{10,8},{12,14},{14,12},{1,3},{3,1},... | collective-permute-start | bytes 368648 | tf_op jit(solution)/shard_map/ppermute | solution.py:349
  17.3 6.9 %collective-permute-start.1 = (bf16[80,768]{1,0:T(8,128)(2,1)S(1)}, bf16[80,768]{1,0:T(8,128)(2,1)S(1)}, u32[]{:S(2)}, u32[]{:S(2)}) collective-permute-start(bf16[80,768]{1,0:T(8,128)(2,1)S(1)} %get-tuple-element.45), channel_id=1, source_target_pairs={{2,4},{4,2},{6,8},{8,6},{10,12},{12,10},{3,5},{5,3},{7,9},{9,7},{1... | collective-permute-start | bytes 368648 | tf_op jit(solution)/shard_map/ppermute | solution.py:350
  25.1 2.8 %collective-permute-start.2 = (bf16[160,768]{1,0:T(8,128)(2,1)S(1)}, bf16[160,768]{1,0:T(8,128)(2,1)S(1)}, u32[]{:S(2)}, u32[]{:S(2)}) collective-permute-start(bf16[160,768]{1,0:T(8,128)(2,1)S(1)} %get-tuple-element.50.pe), channel_id=1, source_target_pairs={{0,1},{1,0},{2,3},{3,2},{4,5},{5,4},{6,7},{7,6},{8,9},{9,8},{10,11... | collective-permute-start | bytes 737288 | tf_op jit(solution)/shard_map/ppermute | solution.py:311
  29.2 3.3 %collective-permute-start.5 = (bf16[192,768]{1,0:T(8,128)(2,1)S(1)}, bf16[192,768]{1,0:T(8,128)(2,1)S(1)}, u32[]{:S(2)}, u32[]{:S(2)}) collective-permute-start(bf16[192,768]{1,0:T(8,128)(2,1)S(1)} %get-tuple-element.64.q), channel_id=1, source_target_pairs={{0,1},{1,0},{2,3},{3,2},{4,5},{5,4},{6,7},{7,6},{8,9},{9,8},{10,11... | collective-permute-start | bytes 884744 | tf_op jit(solution)/shard_map/ppermute | solution.py:311
  30.8 2.9 %collective-permute-start.10 = (bf16[224,768]{1,0:T(8,128)(2,1)S(1)}, bf16[224,768]{1,0:T(8,128)(2,1)S(1)}, u32[]{:S(2)}, u32[]{:S(2)}) collective-permute-start(bf16[224,768]{1,0:T(8,128)(2,1)S(1)} %get-tuple-element.72.db), channel_id=1, source_target_pairs={{0,1},{1,0},{2,3},{3,2},{4,5},{5,4},{6,7},{7,6},{8,9},{9,8},{10,11... | collective-permute-start | bytes 1032200 | tf_op jit(solution)/shard_map/ppermute | solution.py:311
  32.1 1.6 %collective-permute-start.8 = (bf16[192,768]{1,0:T(8,128)(2,1)S(1)}, bf16[192,768]{1,0:T(8,128)(2,1)S(1)}, u32[]{:S(2)}, u32[]{:S(2)}) collective-permute-start(bf16[192,768]{1,0:T(8,128)(2,1)S(1)} %get-tuple-element.69.da), channel_id=1, source_target_pairs={{0,1},{1,0},{2,3},{3,2},{4,5},{5,4},{6,7},{7,6},{8,9},{9,8},{10,11... | collective-permute-start | bytes 884744 | tf_op jit(solution)/shard_map/ppermute | solution.py:311
  33.1 2.0 %collective-permute-start.6 = (bf16[96,768]{1,0:T(8,128)(2,1)S(1)}, bf16[96,768]{1,0:T(8,128)(2,1)S(1)}, u32[]{:S(2)}, u32[]{:S(2)}) collective-permute-start(bf16[96,768]{1,0:T(8,128)(2,1)S(1)} %get-tuple-element.67.dc), channel_id=1, source_target_pairs={{0,1},{1,0},{2,3},{3,2},{4,5},{5,4},{6,7},{7,6},{8,9},{9,8},{10,11... | collective-permute-start | bytes 442376 | tf_op jit(solution)/shard_map/ppermute | solution.py:311

commit v3 on v2

v3 whole, which is shorter than its diff:
```python
import jax
import jax.numpy as jnp
from jax import lax
from jax.experimental import pallas as pl
from jax.experimental.pallas import tpu as pltpu
from jax.sharding import PartitionSpec as P


D0 = 32
D1 = 48
HALO = D0 + D1
EXTRA = 16
PIECE = 32
BF = jnp.bfloat16
F32 = jnp.float32
VM = pl.BlockSpec(memory_space=pltpu.VMEM)
HBM = pl.BlockSpec(memory_space=pltpu.HBM)
GRANT = 14 << 20


def call(kernel, outs, hbm, vmem, scratch=(), grant=GRANT):
    hbm = [pltpu.with_memory_space_constraint(a, pltpu.HBM) for a in hbm]
    vmem = [pltpu.with_memory_space_constraint(a, pltpu.VMEM) for a in vmem]
    return pl.pallas_call(
        kernel,
        out_shape=[pltpu.VMEM(shape, dtype) for shape, dtype in outs],
        in_specs=[HBM] * len(hbm) + [VM] * len(vmem),
        out_specs=[VM] * len(outs),
        scratch_shapes=list(scratch),
        compiler_params=pltpu.CompilerParams(vmem_limit_bytes=grant),
    )(*hbm, *vmem)


def gelu(v):
    inner = v * (BF(0.7978845608028654) + BF(0.035677408136300125) * (v * v))
    half = BF(0.5) * v
    return half + half * jnp.tanh(inner)


def dot(a, b):
    return jnp.dot(a, b, preferred_element_type=F32)


def tiles(start, stop, step):
    return [(i, min(step, stop - i)) for i in range(start, stop, step)]


def act_rows(x, s_ref, b_ref, layer):
    return gelu(x * s_ref[layer : layer + 1].astype(BF) + b_ref[layer : layer + 1].astype(BF))


def taps(h_ref, base, spread, n):
    return jnp.concatenate(
        [h_ref[base + k * spread : base + k * spread + n] for k in (-1, 0, 1)], axis=1
    )


def put_mid(z_ref, own, other, mid_ref, layer, start, n):
    for i, m in tiles(start, start + n, PIECE):
        scale = mid_ref[layer : layer + 1].astype(BF)
        z_ref[i : i + m] = gelu(
            (own[i : i + m] + other[i : i + m]) * scale
            + mid_ref[2 + layer : 3 + layer].astype(BF)
        )


def sigmoid(v):
    return 0.5 + 0.5 * jnp.tanh(0.5 * v)


def embed_first(a_lo, a_hi, rows, width):
    def kernel(
        tower, dna, embed, ins, inb, conv_w, mids, midb, point_w,
        x0, h0, e_a, e_b, pa, w0, pw0, s_in, b_in, own_mid,
        tower_v, dna_v, embed_v, mids_v, midb_v, codes, emb, sem,
    ):
        cp = pltpu.make_async_copy
        step = 128
        quarter = rows // 4
        c_dna = cp(dna, dna_v, sem.at[0])
        c_emb = cp(embed, embed_v, sem.at[1])
        c_tow = [
            cp(
                tower.at[pl.ds(i * quarter, quarter)],
                tower_v.at[pl.ds(i * quarter, quarter)],
                sem.at[2 + i],
            )
            for i in range(4)
        ]
        c_small = [
            cp(ins, s_in, sem.at[6]), cp(inb, b_in, sem.at[7]),
            cp(mids, mids_v, sem.at[8]), cp(midb, midb_v, sem.at[9]),
        ]
        c_w0 = [
            cp(conv_w.at[0, k], w0.at[pl.ds(k * width, width)], sem.at[10 + k]) for k in range(3)
        ]
        c_pw = cp(point_w.at[0], pw0, sem.at[13])
        for c in [c_dna, c_emb, c_small[0], c_small[1], *c_tow, *c_small[2:]]:
            c.start()
        slots = dna.shape[0]
        row = lax.broadcasted_iota(jnp.int32, (4 * slots, slots), 0)
        col = lax.broadcasted_iota(jnp.int32, (4 * slots, slots), 1)
        spread_map = jnp.where((row >> 2) == col, 1.0, 0.0).astype(BF)
        code = (lax.broadcasted_iota(jnp.int32, (4 * slots, step), 0) & 3).astype(F32)
        c_dna.wait()
        c_w0[0].start()
        for i, n in tiles(0, rows, step):
            base = dot(spread_map, dna_v[:, i : i + n].astype(F32).astype(BF))
            codes[i : i + n] = jnp.where(base == code, 1.0, 0.0).T.astype(BF)
        c_emb.wait()
        c_small[0].wait()
        c_small[1].wait()
        c_w0[1].start()
        c_w0[2].start()
        c_pw.start()

        def embed_tile(i, n):
            emb[i : i + n] = dot(codes[i : i + n], embed_v[...])

        def act_tile(start, n):
            for i, m in tiles(start, start + n, PIECE):
                x = (tower_v[i : i + m].astype(F32) + emb[i : i + m]).astype(BF)
                x0[i : i + m] = x
                h0[i : i + m] = act_rows(x, s_in, b_in, 0)

        work = tiles(0, rows, step)
        embed_tile(*work[0])
        need = -(-(a_hi + D0) // step)
        for t in range(need):
            i, n = work[t]
            if i % quarter == 0:
                c_tow[i // quarter].wait()
            if t + 1 < len(work):
                embed_tile(*work[t + 1])
            act_tile(i, n)
        for q in range(-(-need * step // quarter), 4):
            c_tow[q].wait()
        for t in range(need, len(work)):
            if t + 1 < len(work):
                embed_tile(*work[t + 1])
            act_tile(*work[t])
        for k in range(3):
            c_w0[k].wait()
        for i, n in tiles(a_lo, a_hi, 512):
            pa[i - a_lo : i - a_lo + n] = dot(taps(h0, i, D0, n), w0[...]).astype(BF)
        even = lax.rem(lax.axis_index("seq"), 2) == 0
        low = x0[0:HALO]
        high = x0[rows - HALO : rows]
        e_a[...] = jnp.where(even, high, low)
        e_b[...] = jnp.where(even, low, high)
        c_small[2].wait()
        c_small[3].wait()
        first = lax.axis_index("chan") == 0
        mid = jnp.concatenate([mids_v[...], midb_v[...]], axis=0)
        mid = jnp.concatenate(
            [jnp.where(first, mid, 0.0), jnp.where(first, 0.0, mid)], axis=1
        )
        own_mid[...] = mid
        big = mid.astype(BF)
        rest = mid - big.astype(F32)
        middle = rest.astype(BF)
        small = (rest - middle.astype(F32)).astype(BF)
        pa[a_hi - a_lo : a_hi - a_lo + EXTRA] = jnp.concatenate(
            [big.astype(F32), middle.astype(F32), small.astype(F32), jnp.zeros_like(mid)], axis=0
        ).astype(BF)
        c_pw.wait()

    return kernel


def first_rest(b_lo, b_hi):
    def kernel(conv_w, h0, w0, pb, w1, sem):
        width = w0.shape[1]
        copies = [
            pltpu.make_async_copy(conv_w.at[1, k], w1.at[pl.ds(k * width, width)], sem.at[k])
            for k in range(3)
        ]
        for c in copies:
            c.start()
        for i, n in tiles(b_lo, b_hi, b_hi - b_lo):
            pb[i - b_lo : i - b_lo + n] = dot(taps(h0, i, D0, n), w0[...]).astype(BF)
        for c in copies:
            c.wait()

    return kernel


def first_edges(rows):
    def kernel(r_a, r_b, h0, w0, s_in, b_in, pe, lo, hi, ext):
        seq = lax.axis_index("seq")
        even = lax.rem(seq, 2) == 0
        inner = 2 * D0
        span = HALO + inner
        ext[HALO:span] = h0[0:inner]
        ext[span : span + inner] = h0[rows - inner : rows]
        ends = (
            (lo, r_b, r_a, 0, seq == 0),
            (hi, r_a, r_b, span + inner, seq == lax.axis_size("seq") - 1),
        )
        for i, m in tiles(0, HALO, PIECE):
            zero = jnp.zeros((m, h0.shape[1]), BF)
            for keep, at_even, at_odd, at, outside in ends:
                x = jnp.where(even, at_even[i : i + m], at_odd[i : i + m])
                keep[i : i + m] = x
                ext[at + i : at + i + m] = jnp.where(outside, zero, act_rows(x, s_in, b_in, 0))
        lhs = [taps(ext, s + D0, D0, HALO) for s in (0, span)]
        pe[...] = dot(jnp.concatenate(lhs, axis=0), w0[...]).astype(BF)

    return kernel


def second_first(a_lo, a_hi, c_lo, c_hi):
    def kernel(
        point_w, pool_w, pa, ra, x0, pw0, w1, s_in, b_in, own_mid,
        x1a, h1a, qa, mid, pw1, pool, z, acc, sem,
    ):
        copies = [
            pltpu.make_async_copy(point_w.at[1], pw1, sem.at[0]),
            pltpu.make_async_copy(pool_w, pool, sem.at[1]),
        ]
        for c in copies:
            c.start()
        step = 128
        n_a = a_hi - a_lo
        tail = ra[n_a : n_a + EXTRA].astype(F32)
        mid[...] = own_mid[...] + (tail[0:4] + tail[4:8] + tail[8:12])
        work = tiles(0, n_a, step)
        convs = tiles(c_lo, c_hi, step)

        def act_tile(start, n):
            for i, m in tiles(start, start + n, PIECE):
                x = (x0[a_lo + i : a_lo + i + m].astype(F32) + acc[i : i + m]).astype(BF)
                x1a[i : i + m] = x
                h1a[i : i + m] = act_rows(x, s_in, b_in, 1)

        put_mid(z, pa, ra, mid, 0, *work[0])
        for t in range(len(work) + 2 + len(convs)):
            if t + 1 < len(work):
                put_mid(z, pa, ra, mid, 0, *work[t + 1])
            if 1 <= t <= len(work):
                act_tile(*work[t - 1])
            if t < len(work):
                i, n = work[t]
                acc[i : i + n] = dot(z[i : i + n], pw0[...])
            if convs and sum(convs[0]) + D1 - a_lo <= (t - 1) * step:
                i, n = convs.pop(0)
                qa[i - c_lo : i - c_lo + n] = dot(taps(h1a, i - a_lo, D1, n), w1[...]).astype(BF)
        assert not convs
        for c in copies:
            c.wait()

    return kernel


def second_rest(rows, a_lo, a_hi, c_hi, e_hi):
    def kernel(
        pb, rb, x0, x1a, h1a, pw0, w1, mid, s_in, b_in, x1b, x1t, h1t, qb, h1, z, acc
    ):
        step = 224
        b_hi = rows - D0
        first = c_hi - D1
        h1[0 : a_hi - first] = h1a[first - a_lo : a_hi - a_lo]
        x1b[0 : a_hi - c_hi] = x1a[c_hi - a_lo : a_hi - a_lo]
        work = tiles(0, b_hi - a_hi, step)
        convs = tiles(c_hi, e_hi, step)

        def act_tile(start, n):
            for i, m in tiles(start, start + n, PIECE):
                g = a_hi + i
                x = (x0[g : g + m].astype(F32) + acc[i : i + m]).astype(BF)
                h1[g - first : g - first + m] = act_rows(x, s_in, b_in, 1)
                keep = max(0, min(m, e_hi - g))
                if keep:
                    x1b[g - c_hi : g - c_hi + keep] = x[0:keep]
                if keep < m:
                    x1t[g + keep - e_hi : g + m - e_hi] = x[keep:]

        put_mid(z, pb, rb, mid, 0, *work[0])
        for t in range(len(work) + 2 + len(convs)):
            if t + 1 < len(work):
                put_mid(z, pb, rb, mid, 0, *work[t + 1])
            if 1 <= t <= len(work):
                act_tile(*work[t - 1])
            if t < len(work):
                i, n = work[t]
                acc[i : i + n] = dot(z[i : i + n], pw0[...])
            if t >= 2 and convs:
                i, n = convs.pop(0)
                qb[i - c_hi : i - c_hi + n] = dot(taps(h1, i - first, D1, n), w1[...]).astype(BF)
        h1t[...] = h1[e_hi - D1 - first : b_hi - first]

    return kernel


def second_edges(rows, a_lo, c_lo, e_hi):
    def kernel(
        pe, re, x0, lo, hi, x1a, h1a, x1t, h1t, pw0, w1, mid, s_in, b_in, x1c, qc, ext, z, acc
    ):
        seq = lax.axis_index("seq")
        tail = rows - D0 - e_hi
        top = c_lo + 2 * D1
        bottom = rows - e_hi + 2 * D1
        put_mid(z, pe, re, mid, 0, 0, 2 * HALO)
        acc[...] = dot(z[...], pw0[...])
        x1c[D0:c_lo] = x1a[0 : c_lo - a_lo]
        x1c[c_lo : c_lo + tail] = x1t[...]
        ext[HALO:top] = h1a[0 : c_lo + D1 - a_lo]
        ext[top : top + bottom - HALO] = h1t[...]
        low = top + bottom - HALO
        parts = (
            (0, 32, lo, HALO - D1, 0, None, seq == 0),
            (32, 16, lo, HALO - 16, 32, None, seq == 0),
            (D1, D0, x0, 0, D1, 0, None),
            (HALO, D0, x0, rows - D0, low, c_lo + tail, None),
            (HALO + D0, 32, hi, 0, low + D0, None, seq == lax.axis_size("seq") - 1),
            (HALO + D0 + 32, 16, hi, 32, low + D0 + 32, None, seq == lax.axis_size("seq") - 1),
        )
        for i, m, base, at, to, keep, outside in parts:
            x = (base[at : at + m].astype(F32) + acc[i : i + m]).astype(BF)
            h = act_rows(x, s_in, b_in, 1)
            if keep is not None:
                x1c[keep : keep + m] = x
            if outside is not None:
                h = jnp.where(outside, jnp.zeros_like(h), h)
            ext[to : to + m] = h
        lhs = [taps(ext, s + D1, D1, n) for s, n in ((0, c_lo), (top, rows - e_hi))]
        qc[...] = dot(jnp.concatenate(lhs, axis=0), w1[...]).astype(BF)

    return kernel


def own_half(width):
    chan = lax.axis_index("chan")
    mine = pl.ds(pl.multiple_of(chan * width, 128), width)
    theirs = pl.ds(pl.multiple_of((1 - chan) * width, 128), width)
    return mine, theirs


def last_point(x_base, n_rows, step, has_pool):
    def kernel(q, r, x1, pw1, mid, *rest):
        if has_pool:
            d_prev, pool, dm, df, xo, l_prev, z, acc, wide = rest
        else:
            dm, df, xo, z, acc, wide = rest

        def tail(start, n):
            for i, m in tiles(start, start + n, PIECE):
                x = x1[x_base + i : x_base + i + m].astype(F32) + acc[i : i + m]
                x = x.astype(BF).astype(F32)
                j, half = i // 2, m // 2
                firsts, seconds = [], []
                for k in range(wide.shape[0]):
                    wide[k, i : i + m] = x[:, 128 * k : 128 * (k + 1)]
                    firsts.append(wide[k, pl.ds(i, half, stride=2), :])
                    seconds.append(wide[k, pl.ds(i + 1, half, stride=2), :])
                second = jnp.concatenate(seconds, axis=1)
                d = jnp.concatenate(firsts, axis=1) - second
                dm[j : j + half] = d.astype(BF)
                df[j : j + half] = d
                xo[j : j + half] = second.astype(BF)

        work = tiles(0, n_rows, step)
        put_mid(z, q, r, mid, 1, *work[0])
        if has_pool:
            l_prev[...] = dot(d_prev[...], pool[own_half(pw1.shape[1])[0], :])
        for t in range(len(work) + 1):
            if t + 1 < len(work):
                put_mid(z, q, r, mid, 1, *work[t + 1])
            if t < len(work):
                i, n = work[t]
                acc[i : i + n] = dot(z[i : i + n], pw1[...])
            if t >= 1:
                tail(*work[t - 1])

    return kernel


def finish(y, xo, df, logit):
    for i, m in tiles(0, y.shape[0], PIECE):
        y[i : i + m] = (
            xo[i : i + m].astype(F32) + sigmoid(logit[i : i + m]) * df[i : i + m]
        ).astype(BF)


def pool_first(ra, la, rb, lb, dc, pool, dfa, xoa, dfb, xob, ya, yb, lc, acc_a, acc_b):
    mine, theirs = own_half(ra.shape[1])
    acc_a[...] = la[...] + dot(ra[...], pool[theirs, :])
    acc_b[...] = lb[...] + dot(rb[...], pool[theirs, :])
    finish(ya, xoa, dfa, acc_a)
    lc[...] = dot(dc[...], pool[mine, :])
    finish(yb, xob, dfb, acc_b)


def pool_last(p_lo, p_hi, p_end):
    def kernel(rc, lc, pool, dfc, xoc, ya, yb, out, y, acc, sem):
        theirs = own_half(rc.shape[1])[1]
        copy = pltpu.make_async_copy
        last = rc.shape[0] - p_lo
        copies = [
            copy(ya, out.at[pl.ds(p_lo, p_hi - p_lo)], sem.at[0]),
            copy(yb, out.at[pl.ds(p_hi, p_end - p_hi)], sem.at[1]),
            copy(y.at[pl.ds(0, p_lo)], out.at[pl.ds(0, p_lo)], sem.at[2]),
            copy(y.at[pl.ds(p_lo, last)], out.at[pl.ds(p_end, last)], sem.at[3]),
        ]
        copies[0].start()
        copies[1].start()
        acc[...] = lc[...] + dot(rc[...], pool[theirs, :])
        finish(y, xoc, dfc, acc)
        copies[2].start()
        copies[3].start()
        for c in copies:
            c.wait()

    return kernel


def swap_chan(a):
    return lax.ppermute(a, "chan", [(0, 1), (1, 0)])


def local(
    tower_input, dna_bases, base_embed, in_scale, entry_norm_shift,
    conv_w, mid_scale, mid_shift, point_w, pooling_weight,
):
    rows, width = tower_input.shape
    inner = conv_w.shape[3]
    a_lo, a_hi = D0, rows // 2 + 32
    c_lo, c_hi, e_hi = 96, rows // 2 - 32, rows - 96
    b_hi = rows - D0
    n_a, n_b = a_hi - a_lo, b_hi - a_hi
    m_a, m_b = c_hi - c_lo, e_hi - c_hi
    m_c = rows - m_a - m_b
    dma = pltpu.SemaphoreType.DMA
    x0, h0, e_a, e_b, pa, w0, pw0, s_in, b_in, own_mid = call(
        embed_first(a_lo, a_hi, rows, width),
        [
            ((rows, width), BF), ((rows, width), BF), ((HALO, width), BF), ((HALO, width), BF),
            ((n_a + EXTRA, inner), BF), ((3 * width, inner), BF), ((inner, width), BF),
            ((2, width), F32), ((2, width), F32), ((4, inner), F32),
        ],
        [
            tower_input, dna_bases.T, base_embed, in_scale, entry_norm_shift, conv_w,
            mid_scale, mid_shift, point_w,
        ],
        [],
        [
            pltpu.VMEM((rows, width), BF), pltpu.VMEM(dna_bases.shape[::-1], jnp.int32),
            pltpu.VMEM(base_embed.shape, BF), pltpu.VMEM(mid_scale.shape, F32),
            pltpu.VMEM(mid_shift.shape, F32), pltpu.VMEM((rows, 4 * dna_bases.shape[1]), BF),
            pltpu.VMEM((rows, width), F32), dma((14,)),
        ],
    )
    ra = swap_chan(pa)
    count = lax.axis_size("seq")
    pairs_a = [(i, i ^ 1) for i in range(count)]
    pairs_b = [(i, ((i - 1) ^ 1) + 1) for i in range(1, count - 1)]
    r_a = lax.ppermute(e_a, "seq", pairs_a)
    r_b = lax.ppermute(e_b, "seq", pairs_b)
    pb, w1 = call(
        first_rest(a_hi, b_hi),
        [((n_b, inner), BF), ((3 * width, inner), BF)],
        [conv_w],
        [h0, w0],
        [dma((3,))],
    )
    rb = swap_chan(pb)
    x1a, h1a, qa, mid, pw1, pool = call(
        second_first(a_lo, a_hi, c_lo, c_hi),
        [
            ((n_a, width), BF), ((n_a, width), BF), ((m_a, inner), BF), ((4, inner), F32),
            ((inner, width), BF), (pooling_weight.shape, BF),
        ],
        [point_w, pooling_weight],
        [pa, ra, x0, pw0, w1, s_in, b_in, own_mid],
        [pltpu.VMEM((n_a, inner), BF), pltpu.VMEM((n_a, width), F32), dma((2,))],
    )
    sa = swap_chan(qa)
    pe, lo, hi = call(
        first_edges(rows),
        [((2 * HALO, inner), BF), ((HALO, width), BF), ((HALO, width), BF)],
        [],
        [r_a, r_b, h0, w0, s_in, b_in],
        [pltpu.VMEM((2 * (HALO + 2 * D0), width), BF)],
    )
    re = swap_chan(pe)
    x1b, x1t, h1t, qb = call(
        second_rest(rows, a_lo, a_hi, c_hi, e_hi),
        [
            ((m_b, width), BF), ((b_hi - e_hi, width), BF),
            ((b_hi - e_hi + D1, width), BF), ((m_b, inner), BF),
        ],
        [],
        [pb, rb, x0, x1a, h1a, pw0, w1, mid, s_in, b_in],
        [
            pltpu.VMEM((b_hi - c_hi + D1, width), BF), pltpu.VMEM((n_b, inner), BF),
            pltpu.VMEM((n_b, width), F32),
        ],
    )
    sb = swap_chan(qb)
    x1c, qc = call(
        second_edges(rows, a_lo, c_lo, e_hi),
        [((m_c, width), BF), ((m_c, inner), BF)],
        [],
        [pe, re, x0, lo, hi, x1a, h1a, x1t, h1t, pw0, w1, mid, s_in, b_in],
        [
            pltpu.VMEM((m_c + 4 * D1, width), BF), pltpu.VMEM((2 * HALO, inner), BF),
            pltpu.VMEM((2 * HALO, width), F32),
        ],
    )
    sc = swap_chan(qc)
    ends, halves = [], []
    for q, s, x1, base, m, step in (
        (qa, sa, x1a, c_lo - a_lo, m_a, 128), (qb, sb, x1b, 0, m_b, 128), (qc, sc, x1c, 0, m_c, 96)
    ):
        before = [ends[-1][0], pool] if ends else []
        dm, df, xo, *half = call(
            last_point(base, m, step, bool(before)),
            [((m // 2, width), BF), ((m // 2, width), F32), ((m // 2, width), BF)]
            + [((d.shape[0], width), F32) for d in before[:1]],
            [],
            [q, s, x1, pw1, mid, *before],
            [
                pltpu.VMEM((m, inner), BF), pltpu.VMEM((m, width), F32),
                pltpu.VMEM((width // 128, m, 128), F32),
            ],
        )
        halves += half
        ends.append((dm, swap_chan(dm), df, xo))
    (da, ta, dfa, xoa), (db, tb, dfb, xob), (dc, tc, dfc, xoc) = ends
    la, lb = halves
    ya, yb, lc = call(
        pool_first,
        [((m_a // 2, width), BF), ((m_b // 2, width), BF), ((m_c // 2, width), F32)],
        [],
        [ta, la, tb, lb, dc, pool, dfa, xoa, dfb, xob],
        [pltpu.VMEM((m_a // 2, width), F32), pltpu.VMEM((m_b // 2, width), F32)],
    )
    vm = [
        pltpu.with_memory_space_constraint(a, pltpu.VMEM)
        for a in (tc, lc, pool, dfc, xoc, ya, yb)
    ]
    return pl.pallas_call(
        pool_last(c_lo // 2, c_hi // 2, e_hi // 2),
        out_shape=jax.ShapeDtypeStruct((rows // 2, width), BF),
        in_specs=[VM] * 7,
        out_specs=HBM,
        scratch_shapes=[
            pltpu.VMEM((m_c // 2, width), BF), pltpu.VMEM((m_c // 2, width), F32), dma((4,)),
        ],
        compiler_params=pltpu.CompilerParams(vmem_limit_bytes=GRANT),
    )(*vm)


def solution(mesh):
    return jax.shard_map(
        local,
        mesh=mesh,
        in_specs=(
            P(("groups", "seq"), "chan"),
            P(("groups", "seq"), None),
            P(None, "chan"),
            P(None, "chan"),
            P(None, "chan"),
            P(None, None, "chan", None),
            P(None, "chan"),
            P(None, "chan"),
            P(None, None, "chan"),
            P(None, "chan"),
        ),
        out_specs=P(("groups", "seq"), "chan"),
        check_vma=False,
    )
```

time: 36.5 us -> 34.2 us (0.937)
  Pallas kernels: 22 us -> 19.6 us
    pallas_call x10, Pallas kernels: 20.9 us -> 18.6 us  [call(): pl.pallas_call(kernel, out_shape=[pltpu.VMEM(shape, dtype) for shape, dty...]
  transfers between devices with their start and end apart: 11 -> 11, of which waited for: 4 -> 4; matrix products, arithmetic and copies ran while one was open for 0% -> 0% of each run, Pallas kernels for 31% -> 32%
where the time goes in v3:
time: 34.2 us; the launch traced here: 34.1 us
  Pallas kernels  19.6 us (57%)
  starting transfers between devices  7.75 us (23%)
  waiting for transfers between devices  6.4 us (19%)
    pallas_call x10, Pallas kernels, call(): pl.pallas_call(kernel, out_shape=[pltpu.VMEM(shape, dtype) for shape, dty...  18.6 us
    ppermute x9, starting transfers between devices, swap_chan(): return lax.ppermute(a, 'chan', [(0, 1), (1, 0)])  4.32 us
    ppermute x1, waiting for transfers between devices, local(): r_b = lax.ppermute(e_b, 'seq', pairs_b)  3.75 us
    ppermute x1, starting transfers between devices, local(): r_b = lax.ppermute(e_b, 'seq', pairs_b)  2.19 us
    ppermute x9, waiting for transfers between devices, swap_chan(): return lax.ppermute(a, 'chan', [(0, 1), (1, 0)])  1.65 us
    ppermute x1, starting transfers between devices, local(): r_a = lax.ppermute(e_a, 'seq', pairs_a)  1.25 us
    pallas_call x1, Pallas kernels, local(): pl.pallas_call(pool_last(c_lo // 2, c_hi // 2, e_hi // 2), out_shape=jax....  1.07 us
    ppermute x1, waiting for transfers between devices, local(): r_a = lax.ppermute(e_a, 'seq', pairs_a)  1 us
  transfers between devices with their start and end apart: 11, of which 4 were waited for; matrix products, arithmetic and copies ran while one was open for 0% of the time, Pallas kernels for 32%

profile of v3, /device:TPU:17, one launch (start us, length us, event | category | flops | bytes accessed | tf_op | source)
XLA Modules:
  0.0 34.1 jit_solution(16391693472710460124)
XLA Ops:
  0.0 5.2 %shard_map.100 = (bf16[1024,768]{1,0:T(8,128)(2,1)S(1)}, bf16[1024,768]{1,0:T(8,128)(2,1)S(1)}, bf16[80,768]{1,0:T(8,128)(2,1)S(1)}, bf16[80,768]{1,0:T(8,128)(2...) custom-call(bf16[1024,768]{1,0:T(8,128)(2,1)} %tower.1, ...), custom_call_target="tpu_custom_call" | custom-call | tf_op jit(solution)/shard_map/pallas_call | solution.py:24
  5.2 0.7 %collective-permute-start.3 = (bf16[528,768]{1,0:T(8,128)(2,1)S(1)}, bf16[528,768]{1,0:T(8,128)(2,1)S(1)}, u32[]{:S(2)}, u32[]{:S(2)}) collective-permute-start(bf16[528,768]{1,0:T(8,128)(2,1)S(1)} %get-tuple-element.56.pa), channel_id=1, source_target_pairs={{0,1},{1,0},{2,3},{3,2},{4,5},{5,4},{6,7},{7,6},{8,9},{9,8},{10,11... | collective-permute-start | bytes 2433032 | tf_op jit(solution)/shard_map/ppermute | solution.py:418
  5.9 2.0 %shard_map.102 = (bf16[448,768]{1,0:T(8,128)(2,1)S(1)}, bf16[2304,768]{1,0:T(8,128)(2,1)S(1)}) custom-call(bf16[2,3,768,768]{3,2,1,0:T(8,128)(2,1)} %conv_w.3, bf16[1024,768]{1,0:T(8,128)(2,1)S(1)} %get-tuple-element.48.h0, bf16[2304,768]{1,0:T(8,128)(2,1)S(1)} %get-tuple-element.49.w0), custom_call_target="tpu_custom_call" | custom-call | tf_op jit(solution)/shard_map/pallas_call | solution.py:24
  8.0 0.1 collective-permute-start.4
  8.0 0.0 collective-permute-done.3.ra
  8.0 2.8 %shard_map.103 = (bf16[512,768]{1,0:T(8,128)(2,1)S(1)}, bf16[512,768]{1,0:T(8,128)(2,1)S(1)}, bf16[384,768]{1,0:T(8,128)(2,1)S(1)}, f32[4,768]{1,0:T(4,128)S(1)}...) custom-call(bf16[2,768,768]{2,1,0:T(8,128)(2,1)} %point_w.3, bf16[1536,768]{1,0:T(8,128)(2,1)} %pool_w.1, ...), custom_call_target="tpu_custom_call" | custom-call | tf_op jit(solution)/shard_map/pallas_call | solution.py:24
  10.9 0.0 collective-permute-done.4.rb
  10.9 2.5 %shard_map.104 = (bf16[448,768]{1,0:T(8,128)(2,1)S(1)}, bf16[64,768]{1,0:T(8,128)(2,1)S(1)}, bf16[112,768]{1,0:T(8,128)(2,1)S(1)}, bf16[448,768]{1,0:T(8,128)(2,1)S(1)}) custom-call(bf16[448,768]{1,0:T(8,128)(2,1)S(1)} %get-tuple-element.62.pb, bf16[448,768]{1,0:T(8,128)(2,1)S(1)} %collective-permute-done.4.rb, bf16[1024,768]{1,0:T(8,128)(2,1)S(1)} %get-tuple-element.53.x0, ...), custom_call_target="tpu_custom_call" | custom-call | tf_op jit(solution)/shard_map/pallas_call | solution.py:24
  13.4 0.6 %collective-permute-start.6 = (bf16[448,768]{1,0:T(8,128)(2,1)S(1)}, bf16[448,768]{1,0:T(8,128)(2,1)S(1)}, u32[]{:S(2)}, u32[]{:S(2)}) collective-permute-start(bf16[448,768]{1,0:T(8,128)(2,1)S(1)} %get-tuple-element.69.q), channel_id=1, source_target_pairs={{0,1},{1,0},{2,3},{3,2},{4,5},{5,4},{6,7},{7,6},{8,9},{9,8},{10,11... | collective-permute-start | bytes 2064392 | tf_op jit(solution)/shard_map/ppermute | solution.py:418
  14.0 0.1 collective-permute-start.7
  14.0 1.2 %collective-permute-start = (bf16[80,768]{1,0:T(8,128)(2,1)S(1)}, bf16[80,768]{1,0:T(8,128)(2,1)S(1)}, u32[]{:S(2)}, u32[]{:S(2)}) collective-permute-start(bf16[80,768]{1,0:T(8,128)(2,1)S(1)} %get-tuple-element.46), channel_id=1, source_target_pairs={{0,2},{2,0},{4,6},{6,4},{8,10},{10,8},{12,14},{14,12},{1,3},{3,1},... | collective-permute-start | bytes 368648 | tf_op jit(solution)/shard_map/ppermute | solution.py:457
  15.3 2.2 %collective-permute-start.1 = (bf16[80,768]{1,0:T(8,128)(2,1)S(1)}, bf16[80,768]{1,0:T(8,128)(2,1)S(1)}, u32[]{:S(2)}, u32[]{:S(2)}) collective-permute-start(bf16[80,768]{1,0:T(8,128)(2,1)S(1)} %get-tuple-element.47), channel_id=1, source_target_pairs={{2,4},{4,2},{6,8},{8,6},{10,12},{12,10},{3,5},{5,3},{7,9},{9,7},{1... | collective-permute-start | bytes 368648 | tf_op jit(solution)/shard_map/ppermute | solution.py:458
  17.5 1.0 %collective-permute-done.r_a = bf16[80,768]{1,0:T(8,128)(2,1)S(1)} collective-permute-done((bf16[80,768]{1,0:T(8,128)(2,1)S(1)}, bf16[80,768]{1,0:T(8,128)(2,1)S(1)}, u32[]{:S(2)}, u32[]{:S(2)}) %collective-permute-start) | collective-permute-done | bytes 122912 | tf_op jit(solution)/shard_map/ppermute | solution.py:457
  18.5 3.7 %collective-permute-done.1.r_b = bf16[80,768]{1,0:T(8,128)(2,1)S(1)} collective-permute-done((bf16[80,768]{1,0:T(8,128)(2,1)S(1)}, bf16[80,768]{1,0:T(8,128)(2,1)S(1)}, u32[]{:S(2)}, u32[]{:S(2)}) %collective-permute-start.1) | collective-permute-done | bytes 122912 | tf_op jit(solution)/shard_map/ppermute | solution.py:458
  22.2 0.8 %shard_map.101 = (bf16[160,768]{1,0:T(8,128)(2,1)S(1)}, bf16[80,768]{1,0:T(8,128)(2,1)S(1)}, bf16[80,768]{1,0:T(8,128)(2,1)S(1)}) custom-call(bf16[80,768]{1,0:T(8,128)(2,1)S(1)} %collective-permute-done.r_a, bf16[80,768]{1,0:T(8,128)(2,1)S(1)} %collective-permute-done.1.r_b, bf16[1024,768]{1,0:T(8,128)(2,1)S(1)} %get-tuple-element.48.h0, ...), custom_call_target="tpu_custom_call" | custom-call | tf_op jit(solution)/shard_map/pallas_call | solution.py:24
  23.0 1.6 %collective-permute-start.2 = (bf16[160,768]{1,0:T(8,128)(2,1)S(1)}, bf16[160,768]{1,0:T(8,128)(2,1)S(1)}, u32[]{:S(2)}, u32[]{:S(2)}) collective-permute-start(bf16[160,768]{1,0:T(8,128)(2,1)S(1)} %get-tuple-element.52.pe), channel_id=1, source_target_pairs={{0,1},{1,0},{2,3},{3,2},{4,5},{5,4},{6,7},{7,6},{8,9},{9,8},{10,11... | collective-permute-start | bytes 737288 | tf_op jit(solution)/shard_map/ppermute | solution.py:418
  24.7 1.1 %collective-permute-done.2.re = bf16[160,768]{1,0:T(8,128)(2,1)S(1)} collective-permute-done((bf16[160,768]{1,0:T(8,128)(2,1)S(1)}, bf16[160,768]{1,0:T(8,128)(2,1)S(1)}, u32[]{:S(2)}, u32[]{:S(2)}) %collective-permute-start.2) | collective-permute-done | bytes 245792 | tf_op jit(solution)/shard_map/ppermute | solution.py:418
  25.8 1.3 %shard_map.105 = (bf16[192,768]{1,0:T(8,128)(2,1)S(1)}, bf16[192,768]{1,0:T(8,128)(2,1)S(1)}) custom-call(bf16[160,768]{1,0:T(8,128)(2,1)S(1)} %get-tuple-element.52.pe, bf16[160,768]{1,0:T(8,128)(2,1)S(1)} %collective-permute-done.2.re, bf16[1024,768]{1,0:T(8,128)(2,1)S(1)} %get-tuple-element.53.x0, bf16[80,768]{1,0:T(8,128)(2,1)S(1)} %get-tuple-element.54.lo, ...), custom_call_target="tpu_custom_call" | custom-call | tf_op jit(solution)/shard_map/pallas_call | solution.py:24
  27.1 0.4 %collective-permute-start.5 = (bf16[192,768]{1,0:T(8,128)(2,1)S(1)}, bf16[192,768]{1,0:T(8,128)(2,1)S(1)}, u32[]{:S(2)}, u32[]{:S(2)}) collective-permute-start(bf16[192,768]{1,0:T(8,128)(2,1)S(1)} %get-tuple-element.66.q), channel_id=1, source_target_pairs={{0,1},{1,0},{2,3},{3,2},{4,5},{5,4},{6,7},{7,6},{8,9},{9,8},{10,11... | collective-permute-start | bytes 884744 | tf_op jit(solution)/shard_map/ppermute | solution.py:418
  27.5 0.0 collective-permute-done.7.r
  27.5 0.9 %shard_map.106 = (bf16[192,768]{1,0:T(8,128)(2,1)S(1)}, f32[192,768]{1,0:T(8,128)S(1)}, bf16[192,768]{1,0:T(8,128)(2,1)S(1)}) custom-call(bf16[384,768]{1,0:T(8,128)(2,1)S(1)} %get-tuple-element.71.q, bf16[384,768]{1,0:T(8,128)(2,1)S(1)} %collective-permute-done.7.r, bf16[512,768]{1,0:T(8,128)(2,1)S(1)} %get-tuple-element.60.x1a.x1, ...), custom_call_target="tpu_custom_call" | custom-call | tf_op jit(solution)/shard_map/pallas_call | solution.py:24
  28.4 0.0 collective-permute-done.6.r
  28.4 1.3 %shard_map.107 = (bf16[224,768]{1,0:T(8,128)(2,1)S(1)}, f32[224,768]{1,0:T(8,128)S(1)}, bf16[224,768]{1,0:T(8,128)(2,1)S(1)}, f32[192,768]{1,0:T(8,128)S(1)}) custom-call(bf16[448,768]{1,0:T(8,128)(2,1)S(1)} %get-tuple-element.69.q, bf16[448,768]{1,0:T(8,128)(2,1)S(1)} %collective-permute-done.6.r, bf16[448,768]{1,0:T(8,128)(2,1)S(1)} %get-tuple-element.70.x1, ...), custom_call_target="tpu_custom_call" | custom-call | tf_op jit(solution)/shard_map/pallas_call | solution.py:24
  29.7 0.2 collective-permute-start.10
  29.9 0.4 %collective-permute-start.9 = (bf16[192,768]{1,0:T(8,128)(2,1)S(1)}, bf16[192,768]{1,0:T(8,128)(2,1)S(1)}, u32[]{:S(2)}, u32[]{:S(2)}) collective-permute-start(bf16[192,768]{1,0:T(8,128)(2,1)S(1)} %get-tuple-element.72.rest_0_), channel_id=1, source_target_pairs={{0,1},{1,0},{2,3},{3,2},{4,5},{5,4},{6,7},{7,6},{8,9},{9,8},{10,11... | collective-permute-start | bytes 884744 | tf_op jit(solution)/shard_map/ppermute | solution.py:418
  30.3 0.0 collective-permute-done.5.r
  30.3 0.8 %shard_map.108 = (bf16[96,768]{1,0:T(8,128)(2,1)S(1)}, f32[96,768]{1,0:T(8,128)S(1)}, bf16[96,768]{1,0:T(8,128)(2,1)S(1)}, f32[224,768]{1,0:T(8,128)S(1)}) custom-call(bf16[192,768]{1,0:T(8,128)(2,1)S(1)} %get-tuple-element.66.q, bf16[192,768]{1,0:T(8,128)(2,1)S(1)} %collective-permute-done.5.r, bf16[192,768]{1,0:T(8,128)(2,1)S(1)} %get-tuple-element.67.x1, ...), custom_call_target="tpu_custom_call" | custom-call | tf_op jit(solution)/shard_map/pallas_call | solution.py:24
  31.1 0.2 collective-permute-start.8
  31.4 0.5 %collective-permute-done.9.ra = bf16[192,768]{1,0:T(8,128)(2,1)S(1)} collective-permute-done((bf16[192,768]{1,0:T(8,128)(2,1)S(1)}, bf16[192,768]{1,0:T(8,128)(2,1)S(1)}, u32[]{:S(2)}, u32[]{:S(2)}) %collective-permute-start.9) | collective-permute-done | bytes 294944 | tf_op jit(solution)/shard_map/ppermute | solution.py:418
  31.9 0.0 collective-permute-done.10.rb
  31.9 1.0 %shard_map.109 = (bf16[192,768]{1,0:T(8,128)(2,1)S(1)}, bf16[224,768]{1,0:T(8,128)(2,1)S(1)}, f32[96,768]{1,0:T(8,128)S(1)}) custom-call(bf16[192,768]{1,0:T(8,128)(2,1)S(1)} %collective-permute-done.9.ra, f32[192,768]{1,0:T(8,128)S(1)} %get-tuple-element.76.la, bf16[224,768]{1,0:T(8,128)(2,1)S(1)} %collective-permute-done.10.rb, ...), custom_call_target="tpu_custom_call" | custom-call | tf_op jit(solution)/shard_map/pallas_call | solution.py:24
  32.8 0.0 collective-permute-done.8.rc
  32.8 1.1 %shard_map.110 = bf16[512,768]{1,0:T(8,128)(2,1)} custom-call(bf16[96,768]{1,0:T(8,128)(2,1)S(1)} %collective-permute-done.8.rc, f32[96,768]{1,0:T(8,128)S(1)} %get-tuple-element.82.lc, bf16[1536,768]{1,0:T(8,128)(2,1)S(1)} %get-tuple-element.73.rest_1_.pool, f32[96,768]{1,0:T(8,128)S(1)} %get-tuple-element.83.dfc, ...), custom_call_target="tpu_custom_call" | custom-call | tf_op jit(solution)/shard_map/pallas_call | solution.py:542
Async XLA Ops:
  5.2 2.9 %collective-permute-start.3 = (bf16[528,768]{1,0:T(8,128)(2,1)S(1)}, bf16[528,768]{1,0:T(8,128)(2,1)S(1)}, u32[]{:S(2)}, u32[]{:S(2)}) collective-permute-start(bf16[528,768]{1,0:T(8,128)(2,1)S(1)} %get-tuple-element.56.pa), channel_id=1, source_target_pairs={{0,1},{1,0},{2,3},{3,2},{4,5},{5,4},{6,7},{7,6},{8,9},{9,8},{10,11... | collective-permute-start | bytes 2433032 | tf_op jit(solution)/shard_map/ppermute | solution.py:418
  8.0 2.9 %collective-permute-start.4 = (bf16[448,768]{1,0:T(8,128)(2,1)S(1)}, bf16[448,768]{1,0:T(8,128)(2,1)S(1)}, u32[]{:S(2)}, u32[]{:S(2)}) collective-permute-start(bf16[448,768]{1,0:T(8,128)(2,1)S(1)} %get-tuple-element.62.pb), channel_id=1, source_target_pairs={{0,1},{1,0},{2,3},{3,2},{4,5},{5,4},{6,7},{7,6},{8,9},{9,8},{10,11... | collective-permute-start | bytes 2064392 | tf_op jit(solution)/shard_map/ppermute | solution.py:418
  13.4 15.0 %collective-permute-start.6 = (bf16[448,768]{1,0:T(8,128)(2,1)S(1)}, bf16[448,768]{1,0:T(8,128)(2,1)S(1)}, u32[]{:S(2)}, u32[]{:S(2)}) collective-permute-start(bf16[448,768]{1,0:T(8,128)(2,1)S(1)} %get-tuple-element.69.q), channel_id=1, source_target_pairs={{0,1},{1,0},{2,3},{3,2},{4,5},{5,4},{6,7},{7,6},{8,9},{9,8},{10,11... | collective-permute-start | bytes 2064392 | tf_op jit(solution)/shard_map/ppermute | solution.py:418
  14.0 13.5 %collective-permute-start.7 = (bf16[384,768]{1,0:T(8,128)(2,1)S(1)}, bf16[384,768]{1,0:T(8,128)(2,1)S(1)}, u32[]{:S(2)}, u32[]{:S(2)}) collective-permute-start(bf16[384,768]{1,0:T(8,128)(2,1)S(1)} %get-tuple-element.71.q), channel_id=1, source_target_pairs={{0,1},{1,0},{2,3},{3,2},{4,5},{5,4},{6,7},{7,6},{8,9},{9,8},{10,11... | collective-permute-start | bytes 1769480 | tf_op jit(solution)/shard_map/ppermute | solution.py:418
  14.0 4.4 %collective-permute-start = (bf16[80,768]{1,0:T(8,128)(2,1)S(1)}, bf16[80,768]{1,0:T(8,128)(2,1)S(1)}, u32[]{:S(2)}, u32[]{:S(2)}) collective-permute-start(bf16[80,768]{1,0:T(8,128)(2,1)S(1)} %get-tuple-element.46), channel_id=1, source_target_pairs={{0,2},{2,0},{4,6},{6,4},{8,10},{10,8},{12,14},{14,12},{1,3},{3,1},... | collective-permute-start | bytes 368648 | tf_op jit(solution)/shard_map/ppermute | solution.py:457
  15.3 6.9 %collective-permute-start.1 = (bf16[80,768]{1,0:T(8,128)(2,1)S(1)}, bf16[80,768]{1,0:T(8,128)(2,1)S(1)}, u32[]{:S(2)}, u32[]{:S(2)}) collective-permute-start(bf16[80,768]{1,0:T(8,128)(2,1)S(1)} %get-tuple-element.47), channel_id=1, source_target_pairs={{2,4},{4,2},{6,8},{8,6},{10,12},{12,10},{3,5},{5,3},{7,9},{9,7},{1... | collective-permute-start | bytes 368648 | tf_op jit(solution)/shard_map/ppermute | solution.py:458
  23.0 2.8 %collective-permute-start.2 = (bf16[160,768]{1,0:T(8,128)(2,1)S(1)}, bf16[160,768]{1,0:T(8,128)(2,1)S(1)}, u32[]{:S(2)}, u32[]{:S(2)}) collective-permute-start(bf16[160,768]{1,0:T(8,128)(2,1)S(1)} %get-tuple-element.52.pe), channel_id=1, source_target_pairs={{0,1},{1,0},{2,3},{3,2},{4,5},{5,4},{6,7},{7,6},{8,9},{9,8},{10,11... | collective-permute-start | bytes 737288 | tf_op jit(solution)/shard_map/ppermute | solution.py:418
  27.1 3.2 %collective-permute-start.5 = (bf16[192,768]{1,0:T(8,128)(2,1)S(1)}, bf16[192,768]{1,0:T(8,128)(2,1)S(1)}, u32[]{:S(2)}, u32[]{:S(2)}) collective-permute-start(bf16[192,768]{1,0:T(8,128)(2,1)S(1)} %get-tuple-element.66.q), channel_id=1, source_target_pairs={{0,1},{1,0},{2,3},{3,2},{4,5},{5,4},{6,7},{7,6},{8,9},{9,8},{10,11... | collective-permute-start | bytes 884744 | tf_op jit(solution)/shard_map/ppermute | solution.py:418
  29.7 2.1 %collective-permute-start.10 = (bf16[224,768]{1,0:T(8,128)(2,1)S(1)}, bf16[224,768]{1,0:T(8,128)(2,1)S(1)}, u32[]{:S(2)}, u32[]{:S(2)}) collective-permute-start(bf16[224,768]{1,0:T(8,128)(2,1)S(1)} %get-tuple-element.74.rest_0_), channel_id=1, source_target_pairs={{0,1},{1,0},{2,3},{3,2},{4,5},{5,4},{6,7},{7,6},{8,9},{9,8},{10,11... | collective-permute-start | bytes 1032200 | tf_op jit(solution)/shard_map/ppermute | solution.py:418
  29.9 1.9 %collective-permute-start.9 = (bf16[192,768]{1,0:T(8,128)(2,1)S(1)}, bf16[192,768]{1,0:T(8,128)(2,1)S(1)}, u32[]{:S(2)}, u32[]{:S(2)}) collective-permute-start(bf16[192,768]{1,0:T(8,128)(2,1)S(1)} %get-tuple-element.72.rest_0_), channel_id=1, source_target_pairs={{0,1},{1,0},{2,3},{3,2},{4,5},{5,4},{6,7},{7,6},{8,9},{9,8},{10,11... | collective-permute-start | bytes 884744 | tf_op jit(solution)/shard_map/ppermute | solution.py:418
  31.1 1.7 %collective-permute-start.8 = (bf16[96,768]{1,0:T(8,128)(2,1)S(1)}, bf16[96,768]{1,0:T(8,128)(2,1)S(1)}, u32[]{:S(2)}, u32[]{:S(2)}) collective-permute-start(bf16[96,768]{1,0:T(8,128)(2,1)S(1)} %get-tuple-element.75.dc), channel_id=1, source_target_pairs={{0,1},{1,0},{2,3},{3,2},{4,5},{5,4},{6,7},{7,6},{8,9},{9,8},{10,11... | collective-permute-start | bytes 442376 | tf_op jit(solution)/shard_map/ppermute | solution.py:418

commit v4 on v3

v4 whole, which is shorter than its diff:
```python
import jax
import jax.numpy as jnp
from jax import lax
from jax.experimental import pallas as pl
from jax.experimental.pallas import tpu as pltpu
from jax.sharding import PartitionSpec as P


D0 = 32
D1 = 48
HALO = D0 + D1
EXTRA = 16
PIECE = 32
COST = {"k0": 100}
BF = jnp.bfloat16
F32 = jnp.float32
VM = pl.BlockSpec(memory_space=pltpu.VMEM)
HBM = pl.BlockSpec(memory_space=pltpu.HBM)
GRANT = 14 << 20


def call(name, kernel, outs, hbm, vmem, scratch=(), grant=GRANT):
    hbm = [pltpu.with_memory_space_constraint(a, pltpu.HBM) for a in hbm]
    vmem = [pltpu.with_memory_space_constraint(a, pltpu.VMEM) for a in vmem]
    return pl.pallas_call(
        kernel,
        out_shape=[pltpu.VMEM(shape, dtype) for shape, dtype in outs],
        in_specs=[HBM] * len(hbm) + [VM] * len(vmem),
        out_specs=[VM] * len(outs),
        scratch_shapes=list(scratch),
        compiler_params=pltpu.CompilerParams(vmem_limit_bytes=grant),
        cost_estimate=pl.CostEstimate(
            flops=COST.get(name, 3) * 10**9, bytes_accessed=0, transcendentals=0
        ),
    )(*hbm, *vmem)


def gelu(v):
    inner = v * (BF(0.7978845608028654) + BF(0.035677408136300125) * (v * v))
    half = BF(0.5) * v
    return half + half * jnp.tanh(inner)


def dot(a, b):
    return jnp.dot(a, b, preferred_element_type=F32)


def tiles(start, stop, step):
    return [(i, min(step, stop - i)) for i in range(start, stop, step)]


def act_rows(x, s_ref, b_ref, layer):
    return gelu(x * s_ref[layer : layer + 1].astype(BF) + b_ref[layer : layer + 1].astype(BF))


def taps(h_ref, base, spread, n):
    return jnp.concatenate(
        [h_ref[base + k * spread : base + k * spread + n] for k in (-1, 0, 1)], axis=1
    )


def put_mid(z_ref, own, other, mid_ref, layer, start, n):
    for i, m in tiles(start, start + n, PIECE):
        scale = mid_ref[layer : layer + 1].astype(BF)
        z_ref[i : i + m] = gelu(
            (own[i : i + m] + other[i : i + m]) * scale
            + mid_ref[2 + layer : 3 + layer].astype(BF)
        )


def sigmoid(v):
    return 0.5 + 0.5 * jnp.tanh(0.5 * v)


def embed_edges(rows):
    def kernel(
        tower, dna, embed, ins, inb, mids, midb,
        e_a, e_b, codes, embed_v, s_in, b_in, own_mid, dna_v, ends, mids_v, midb_v, sem,
    ):
        cp = pltpu.make_async_copy
        step = 128
        copies = [
            cp(dna, dna_v, sem.at[0]), cp(embed, embed_v, sem.at[1]),
            cp(tower.at[pl.ds(0, HALO)], ends.at[0], sem.at[2]),
            cp(tower.at[pl.ds(rows - HALO, HALO)], ends.at[1], sem.at[3]),
            cp(ins, s_in, sem.at[4]), cp(inb, b_in, sem.at[5]),
            cp(mids, mids_v, sem.at[6]), cp(midb, midb_v, sem.at[7]),
        ]
        for c in copies:
            c.start()
        slots = dna.shape[0]
        row = lax.broadcasted_iota(jnp.int32, (4 * slots, slots), 0)
        col = lax.broadcasted_iota(jnp.int32, (4 * slots, slots), 1)
        spread_map = jnp.where((row >> 2) == col, 1.0, 0.0).astype(BF)
        code = (lax.broadcasted_iota(jnp.int32, (4 * slots, step), 0) & 3).astype(F32)
        for c in copies:
            c.wait()
        for i, n in tiles(0, rows, step):
            base = dot(spread_map, dna_v[:, i : i + n].astype(F32).astype(BF))
            codes[i : i + n] = jnp.where(base == code, 1.0, 0.0).T.astype(BF)
        even = lax.rem(lax.axis_index("seq"), 2) == 0
        low = (ends[0].astype(F32) + dot(codes[0:HALO], embed_v[...])).astype(BF)
        high = (ends[1].astype(F32) + dot(codes[rows - HALO : rows], embed_v[...])).astype(BF)
        e_a[...] = jnp.where(even, high, low)
        e_b[...] = jnp.where(even, low, high)
        first = lax.axis_index("chan") == 0
        mid = jnp.concatenate([mids_v[...], midb_v[...]], axis=0)
        own_mid[...] = jnp.concatenate(
            [jnp.where(first, mid, 0.0), jnp.where(first, 0.0, mid)], axis=1
        )

    return kernel


def embed_first(a_lo, a_hi, rows):
    def kernel(tower, codes, embed, s_in, b_in, conv_w, own_mid, x0, h0, pa, emb):
        step = 128

        def embed_tile(i, n):
            emb[i : i + n] = dot(codes[i : i + n], embed[...])

        def act_tile(start, n):
            for i, m in tiles(start, start + n, PIECE):
                x = (tower[i : i + m].astype(F32) + emb[i : i + m]).astype(BF)
                x0[i : i + m] = x
                h0[i : i + m] = act_rows(x, s_in, b_in, 0)

        work = tiles(0, rows, step)
        embed_tile(*work[0])
        convs = tiles(a_lo, a_hi, step)
        for t in range(len(work)):
            if t + 1 < len(work):
                embed_tile(*work[t + 1])
            act_tile(*work[t])
            if convs and sum(convs[0]) + D0 <= t * step:
                i, n = convs.pop(0)
                pa[i - a_lo : i - a_lo + n] = dot(taps(h0, i, D0, n), conv_w[0]).astype(BF)
        assert not convs
        mid = own_mid[...]
        big = mid.astype(BF)
        rest = mid - big.astype(F32)
        middle = rest.astype(BF)
        small = (rest - middle.astype(F32)).astype(BF)
        pa[a_hi - a_lo : a_hi - a_lo + EXTRA] = jnp.concatenate(
            [big.astype(F32), middle.astype(F32), small.astype(F32), jnp.zeros_like(mid)], axis=0
        ).astype(BF)

    return kernel


def first_rest(b_lo, b_hi):
    def kernel(h0, conv_w, pb):
        pb[...] = dot(taps(h0, b_lo, D0, b_hi - b_lo), conv_w[0]).astype(BF)

    return kernel


def first_edges(rows):
    def kernel(r_a, r_b, h0, conv_w, s_in, b_in, pe, lo, hi, ext):
        seq = lax.axis_index("seq")
        even = lax.rem(seq, 2) == 0
        inner = 2 * D0
        span = HALO + inner
        ext[HALO:span] = h0[0:inner]
        ext[span : span + inner] = h0[rows - inner : rows]
        ends = (
            (lo, r_b, r_a, 0, seq == 0),
            (hi, r_a, r_b, span + inner, seq == lax.axis_size("seq") - 1),
        )
        for i, m in tiles(0, HALO, PIECE):
            zero = jnp.zeros((m, h0.shape[1]), BF)
            for keep, at_even, at_odd, at, outside in ends:
                x = jnp.where(even, at_even[i : i + m], at_odd[i : i + m])
                keep[i : i + m] = x
                ext[at + i : at + i + m] = jnp.where(outside, zero, act_rows(x, s_in, b_in, 0))
        lhs = [taps(ext, s + D0, D0, HALO) for s in (0, span)]
        pe[...] = dot(jnp.concatenate(lhs, axis=0), conv_w[0]).astype(BF)

    return kernel


def second_first(a_lo, a_hi, c_lo, c_hi):
    def kernel(
        pa, ra, x0, point_w, conv_w, s_in, b_in, own_mid, x1a, h1a, qa, mid, z, acc,
    ):
        step = 128
        n_a = a_hi - a_lo
        tail = ra[n_a : n_a + EXTRA].astype(F32)
        mid[...] = own_mid[...] + (tail[0:4] + tail[4:8] + tail[8:12])
        work = tiles(0, n_a, step)
        convs = tiles(c_lo, c_hi, step)

        def act_tile(start, n):
            for i, m in tiles(start, start + n, PIECE):
                x = (x0[a_lo + i : a_lo + i + m].astype(F32) + acc[i : i + m]).astype(BF)
                x1a[i : i + m] = x
                h1a[i : i + m] = act_rows(x, s_in, b_in, 1)

        put_mid(z, pa, ra, mid, 0, *work[0])
        for t in range(len(work) + 2 + len(convs)):
            if t + 1 < len(work):
                put_mid(z, pa, ra, mid, 0, *work[t + 1])
            if 1 <= t <= len(work):
                act_tile(*work[t - 1])
            if t < len(work):
                i, n = work[t]
                acc[i : i + n] = dot(z[i : i + n], point_w[0])
            if convs and sum(convs[0]) + D1 - a_lo <= (t - 1) * step:
                i, n = convs.pop(0)
                qa[i - c_lo : i - c_lo + n] = dot(taps(h1a, i - a_lo, D1, n), conv_w[1]).astype(BF)
        assert not convs

    return kernel


def second_rest(rows, a_lo, a_hi, c_hi, e_hi):
    def kernel(
        pb, rb, x0, x1a, h1a, point_w, conv_w, mid, s_in, b_in, x1b, x1t, h1t, qb, h1, z, acc
    ):
        step = 224
        b_hi = rows - D0
        first = c_hi - D1
        h1[0 : a_hi - first] = h1a[first - a_lo : a_hi - a_lo]
        x1b[0 : a_hi - c_hi] = x1a[c_hi - a_lo : a_hi - a_lo]
        work = tiles(0, b_hi - a_hi, step)
        convs = tiles(c_hi, e_hi, step)

        def act_tile(start, n):
            for i, m in tiles(start, start + n, PIECE):
                g = a_hi + i
                x = (x0[g : g + m].astype(F32) + acc[i : i + m]).astype(BF)
                h1[g - first : g - first + m] = act_rows(x, s_in, b_in, 1)
                keep = max(0, min(m, e_hi - g))
                if keep:
                    x1b[g - c_hi : g - c_hi + keep] = x[0:keep]
                if keep < m:
                    x1t[g + keep - e_hi : g + m - e_hi] = x[keep:]

        put_mid(z, pb, rb, mid, 0, *work[0])
        for t in range(len(work) + 2 + len(convs)):
            if t + 1 < len(work):
                put_mid(z, pb, rb, mid, 0, *work[t + 1])
            if 1 <= t <= len(work):
                act_tile(*work[t - 1])
            if t < len(work):
                i, n = work[t]
                acc[i : i + n] = dot(z[i : i + n], point_w[0])
            if t >= 2 and convs:
                i, n = convs.pop(0)
                qb[i - c_hi : i - c_hi + n] = dot(taps(h1, i - first, D1, n), conv_w[1]).astype(BF)
        h1t[...] = h1[e_hi - D1 - first : b_hi - first]

    return kernel


def second_edges(rows, a_lo, c_lo, e_hi):
    def kernel(
        pe, re, x0, lo, hi, x1a, h1a, x1t, h1t, point_w, conv_w, mid, s_in, b_in, x1c, qc, ext, z, acc
    ):
        seq = lax.axis_index("seq")
        tail = rows - D0 - e_hi
        top = c_lo + 2 * D1
        bottom = rows - e_hi + 2 * D1
        put_mid(z, pe, re, mid, 0, 0, 2 * HALO)
        acc[...] = dot(z[...], point_w[0])
        x1c[D0:c_lo] = x1a[0 : c_lo - a_lo]
        x1c[c_lo : c_lo + tail] = x1t[...]
        ext[HALO:top] = h1a[0 : c_lo + D1 - a_lo]
        ext[top : top + bottom - HALO] = h1t[...]
        low = top + bottom - HALO
        parts = (
            (0, 32, lo, HALO - D1, 0, None, seq == 0),
            (32, 16, lo, HALO - 16, 32, None, seq == 0),
            (D1, D0, x0, 0, D1, 0, None),
            (HALO, D0, x0, rows - D0, low, c_lo + tail, None),
            (HALO + D0, 32, hi, 0, low + D0, None, seq == lax.axis_size("seq") - 1),
            (HALO + D0 + 32, 16, hi, 32, low + D0 + 32, None, seq == lax.axis_size("seq") - 1),
        )
        for i, m, base, at, to, keep, outside in parts:
            x = (base[at : at + m].astype(F32) + acc[i : i + m]).astype(BF)
            h = act_rows(x, s_in, b_in, 1)
            if keep is not None:
                x1c[keep : keep + m] = x
            if outside is not None:
                h = jnp.where(outside, jnp.zeros_like(h), h)
            ext[to : to + m] = h
        lhs = [taps(ext, s + D1, D1, n) for s, n in ((0, c_lo), (top, rows - e_hi))]
        qc[...] = dot(jnp.concatenate(lhs, axis=0), conv_w[1]).astype(BF)

    return kernel


def own_half(width):
    chan = lax.axis_index("chan")
    mine = pl.ds(pl.multiple_of(chan * width, 128), width)
    theirs = pl.ds(pl.multiple_of((1 - chan) * width, 128), width)
    return mine, theirs


def last_point(x_base, n_rows, step, has_pool):
    def kernel(q, r, x1, point_w, mid, *rest):
        if has_pool:
            d_prev, pool, dm, xo, l_prev, z, acc, x2 = rest
        else:
            dm, xo, z, acc, x2 = rest
        half = step // 2
        row = lax.broadcasted_iota(jnp.int32, (step, step), 0)
        col = lax.broadcasted_iota(jnp.int32, (step, step), 1)
        pair = jnp.where(row < half, row, row - half) * 2
        pick = jnp.where(col == pair + 1, jnp.where(row < half, -1.0, 1.0), 0.0)
        pick = jnp.where((col == pair) & (row < half), 1.0, pick).astype(BF)

        def sum_rows(start, n):
            for i, m in tiles(start, start + n, PIECE):
                x = x1[x_base + i : x_base + i + m].astype(F32) + acc[i : i + m]
                x2[i : i + m] = x.astype(BF)

        def pair_rows(start, n):
            j = start // 2
            both = dot(pick, x2[start : start + n])
            dm[j : j + half] = both[:half].astype(BF)
            xo[j : j + half] = both[half:].astype(BF)

        work = tiles(0, n_rows, step)
        put_mid(z, q, r, mid, 1, *work[0])
        if has_pool:
            l_prev[...] = dot(d_prev[...], pool[own_half(x1.shape[1])[0], :])
        for t in range(len(work) + 2):
            if t + 1 < len(work):
                put_mid(z, q, r, mid, 1, *work[t + 1])
            if 1 <= t <= len(work):
                sum_rows(*work[t - 1])
            if t < len(work):
                i, n = work[t]
                acc[i : i + n] = dot(z[i : i + n], point_w[1])
            if t >= 2:
                pair_rows(*work[t - 2])

    return kernel


def finish(y, xo, d, logit):
    for i, m in tiles(0, y.shape[0], PIECE):
        y[i : i + m] = (
            xo[i : i + m].astype(F32) + sigmoid(logit[i : i + m]) * d[i : i + m].astype(F32)
        ).astype(BF)


def pool_first(ra, la, rb, lb, dc, pool, da, xoa, db, xob, ya, yb, lc, acc_a, acc_b):
    mine, theirs = own_half(ra.shape[1])
    acc_a[...] = la[...] + dot(ra[...], pool[theirs, :])
    acc_b[...] = lb[...] + dot(rb[...], pool[theirs, :])
    finish(ya, xoa, da, acc_a)
    lc[...] = dot(dc[...], pool[mine, :])
    finish(yb, xob, db, acc_b)


def pool_last(p_lo, p_hi, p_end):
    def kernel(rc, lc, pool, dc, xoc, ya, yb, out, y, acc, sem):
        theirs = own_half(rc.shape[1])[1]
        copy = pltpu.make_async_copy
        last = rc.shape[0] - p_lo
        copies = [
            copy(ya, out.at[pl.ds(p_lo, p_hi - p_lo)], sem.at[0]),
            copy(yb, out.at[pl.ds(p_hi, p_end - p_hi)], sem.at[1]),
            copy(y.at[pl.ds(0, p_lo)], out.at[pl.ds(0, p_lo)], sem.at[2]),
            copy(y.at[pl.ds(p_lo, last)], out.at[pl.ds(p_end, last)], sem.at[3]),
        ]
        copies[0].start()
        copies[1].start()
        acc[...] = lc[...] + dot(rc[...], pool[theirs, :])
        finish(y, xoc, dc, acc)
        copies[2].start()
        copies[3].start()
        for c in copies:
            c.wait()

    return kernel


def swap_chan(a):
    return lax.ppermute(a, "chan", [(0, 1), (1, 0)])


def local(
    tower_input, dna_bases, base_embed, in_scale, entry_norm_shift,
    conv_w, mid_scale, mid_shift, point_w, pooling_weight,
):
    rows, width = tower_input.shape
    inner = conv_w.shape[3]
    a_lo, a_hi = D0, rows // 2 + 32
    c_lo, c_hi, e_hi = 96, rows // 2 - 32, rows - 96
    b_hi = rows - D0
    n_a, n_b = a_hi - a_lo, b_hi - a_hi
    m_a, m_b = c_hi - c_lo, e_hi - c_hi
    m_c = rows - m_a - m_b
    dma = pltpu.SemaphoreType.DMA
    weights = conv_w.reshape(conv_w.shape[0], 3 * width, inner)
    e_a, e_b, codes, embed, s_in, b_in, own_mid = call(
        "k0",
        embed_edges(rows),
        [
            ((HALO, width), BF), ((HALO, width), BF), ((rows, base_embed.shape[0]), BF),
            (base_embed.shape, BF), ((2, width), F32), ((2, width), F32), ((4, inner), F32),
        ],
        [
            tower_input, dna_bases.T, base_embed, in_scale, entry_norm_shift, mid_scale, mid_shift,
        ],
        [],
        [
            pltpu.VMEM(dna_bases.shape[::-1], jnp.int32), pltpu.VMEM((2, HALO, width), BF),
            pltpu.VMEM(mid_scale.shape, F32), pltpu.VMEM(mid_shift.shape, F32), dma((8,)),
        ],
    )
    x0, h0, pa = call(
        "k1a",
        embed_first(a_lo, a_hi, rows),
        [((rows, width), BF), ((rows, width), BF), ((n_a + EXTRA, inner), BF)],
        [],
        [tower_input, codes, embed, s_in, b_in, weights, own_mid],
        [pltpu.VMEM((rows, width), F32)],
    )
    ra = swap_chan(pa)
    count = lax.axis_size("seq")
    pairs_a = [(i, i ^ 1) for i in range(count)]
    pairs_b = [(i, ((i - 1) ^ 1) + 1) for i in range(1, count - 1)]
    r_a = lax.ppermute(e_a, "seq", pairs_a)
    r_b = lax.ppermute(e_b, "seq", pairs_b)
    (pb,) = call("k1b", first_rest(a_hi, b_hi), [((n_b, inner), BF)], [], [h0, weights])
    rb = swap_chan(pb)
    x1a, h1a, qa, mid = call(
        "k2a",
        second_first(a_lo, a_hi, c_lo, c_hi),
        [
            ((n_a, width), BF), ((n_a, width), BF), ((m_a, inner), BF), ((4, inner), F32),
        ],
        [],
        [pa, ra, x0, point_w, weights, s_in, b_in, own_mid],
        [pltpu.VMEM((n_a, inner), BF), pltpu.VMEM((n_a, width), F32)],
    )
    sa = swap_chan(qa)
    pe, lo, hi = call(
        "k1e",
        first_edges(rows),
        [((2 * HALO, inner), BF), ((HALO, width), BF), ((HALO, width), BF)],
        [],
        [r_a, r_b, h0, weights, s_in, b_in],
        [pltpu.VMEM((2 * (HALO + 2 * D0), width), BF)],
    )
    re = swap_chan(pe)
    x1b, x1t, h1t, qb = call(
        "k2b",
        second_rest(rows, a_lo, a_hi, c_hi, e_hi),
        [
            ((m_b, width), BF), ((b_hi - e_hi, width), BF),
            ((b_hi - e_hi + D1, width), BF), ((m_b, inner), BF),
        ],
        [],
        [pb, rb, x0, x1a, h1a, point_w, weights, mid, s_in, b_in],
        [
            pltpu.VMEM((b_hi - c_hi + D1, width), BF), pltpu.VMEM((n_b, inner), BF),
            pltpu.VMEM((n_b, width), F32),
        ],
    )
    sb = swap_chan(qb)
    x1c, qc = call(
        "k2c",
        second_edges(rows, a_lo, c_lo, e_hi),
        [((m_c, width), BF), ((m_c, inner), BF)],
        [],
        [pe, re, x0, lo, hi, x1a, h1a, x1t, h1t, point_w, weights, mid, s_in, b_in],
        [
            pltpu.VMEM((m_c + 4 * D1, width), BF), pltpu.VMEM((2 * HALO, inner), BF),
            pltpu.VMEM((2 * HALO, width), F32),
        ],
    )
    sc = swap_chan(qc)
    ends, halves = [], []
    for name, q, s, x1, base, m, step in (
        ("a", qa, sa, x1a, c_lo - a_lo, m_a, 128),
        ("b", qb, sb, x1b, 0, m_b, 224),
        ("c", qc, sc, x1c, 0, m_c, 192),
    ):
        before = [ends[-1][0], pooling_weight] if ends else []
        dm, xo, *half = call(
            "k3" + name,
            last_point(base, m, step, bool(before)),
            [((m // 2, width), BF), ((m // 2, width), BF)]
            + [((d.shape[0], width), F32) for d in before[:1]],
            [],
            [q, s, x1, point_w, mid, *before],
            [
                pltpu.VMEM((m, inner), BF), pltpu.VMEM((m, width), F32),
                pltpu.VMEM((m, width), BF),
            ],
        )
        halves += half
        ends.append((dm, swap_chan(dm), xo))
    (da, ta, xoa), (db, tb, xob), (dc, tc, xoc) = ends
    la, lb = halves
    ya, yb, lc = call(
        "k4",
        pool_first,
        [((m_a // 2, width), BF), ((m_b // 2, width), BF), ((m_c // 2, width), F32)],
        [],
        [ta, la, tb, lb, dc, pooling_weight, da, xoa, db, xob],
        [pltpu.VMEM((m_a // 2, width), F32), pltpu.VMEM((m_b // 2, width), F32)],
    )
    vm = [
        pltpu.with_memory_space_constraint(a, pltpu.VMEM)
        for a in (tc, lc, pooling_weight, dc, xoc, ya, yb)
    ]
    return pl.pallas_call(
        pool_last(c_lo // 2, c_hi // 2, e_hi // 2),
        out_shape=jax.ShapeDtypeStruct((rows // 2, width), BF),
        in_specs=[VM] * 7,
        out_specs=HBM,
        scratch_shapes=[
            pltpu.VMEM((m_c // 2, width), BF), pltpu.VMEM((m_c // 2, width), F32), dma((4,)),
        ],
        compiler_params=pltpu.CompilerParams(vmem_limit_bytes=GRANT),
    )(*vm)


def solution(mesh):
    return jax.shard_map(
        local,
        mesh=mesh,
        in_specs=(
            P(("groups", "seq"), "chan"),
            P(("groups", "seq"), None),
            P(None, "chan"),
            P(None, "chan"),
            P(None, "chan"),
            P(None, None, "chan", None),
            P(None, "chan"),
            P(None, "chan"),
            P(None, None, "chan"),
            P(None, "chan"),
        ),
        out_specs=P(("groups", "seq"), "chan"),
        check_vma=False,
    )
```

time: 34.2 us -> 34.4 us (level)
  local copies, waits for them, and re-layouts: 0 us -> 2.5 us
  waiting for transfers between devices: 6.4 us -> 5.31 us
  Pallas kernels: 19.6 us -> 18.6 us
    unnamed x0 -> x8, local copies, waits for them, and re-layouts: none -> 2.5 us
    ppermute x9, waiting for transfers between devices: 1.65 us -> 0.56 us  [swap_chan(): return lax.ppermute(a, 'chan', [(0, 1), (1, 0)])]
    pallas_call x10 -> x11, Pallas kernels: 18.6 us -> 17.6 us  [call(): pl.pallas_call(kernel, out_shape=[pltpu.VMEM(shape, dtype) for shape, dty...]
    ppermute x9, starting transfers between devices: 4.32 us -> 3.92 us  [swap_chan(): return lax.ppermute(a, 'chan', [(0, 1), (1, 0)])]
  transfers between devices with their start and end apart: 11 -> 11, of which waited for: 4 -> 3; matrix products, arithmetic and copies ran while one was open for 0% -> 0% of each run, Pallas kernels for 32% -> 38%
where the time goes in v4:
time: 34.4 us; the launch traced here: 34.2 us
  Pallas kernels  18.6 us (54%)
  starting transfers between devices  7.53 us (22%)
  waiting for transfers between devices  5.31 us (15%)
  local copies, waits for them, and re-layouts  2.5 us (7%)
    pallas_call x11, Pallas kernels, call(): pl.pallas_call(kernel, out_shape=[pltpu.VMEM(shape, dtype) for shape, dty...  17.6 us
    ppermute x9, starting transfers between devices, swap_chan(): return lax.ppermute(a, 'chan', [(0, 1), (1, 0)])  3.92 us
    ppermute x1, waiting for transfers between devices, local(): r_b = lax.ppermute(e_b, 'seq', pairs_b)  3.87 us
    unnamed x8, local copies, waits for them, and re-layouts  2.5 us
    ppermute x1, starting transfers between devices, local(): r_b = lax.ppermute(e_b, 'seq', pairs_b)  2.32 us
    ppermute x1, starting transfers between devices, local(): r_a = lax.ppermute(e_a, 'seq', pairs_a)  1.3 us
    pallas_call x1, Pallas kernels, local(): pl.pallas_call(pool_last(c_lo // 2, c_hi // 2, e_hi // 2), out_shape=jax....  1.06 us
    ppermute x1, waiting for transfers between devices, local(): r_a = lax.ppermute(e_a, 'seq', pairs_a)  0.88 us
  transfers between devices with their start and end apart: 11, of which 3 were waited for; matrix products, arithmetic and copies ran while one was open for 0% of the time, Pallas kernels for 38%

profile of v4, /device:TPU:17, one launch (start us, length us, event | category | flops | bytes accessed | tf_op | source)
XLA Modules:
  0.0 34.2 jit_solution(8722255412462896772)
XLA Ops:
  0.0 0.0 copy-start
  0.0 0.0 copy-start.3
  0.0 1.8 %shard_map.100 = (bf16[80,768]{1,0:T(8,128)(2,1)S(1)}, bf16[80,768]{1,0:T(8,128)(2,1)S(1)}, bf16[1024,128]{1,0:T(8,128)(2,1)S(1)}, bf16[128,768]{1,0:T(8,128)(2,...) custom-call(bf16[1024,768]{1,0:T(8,128)(2,1)} %tower.3, s32[32,1024]{1,0:T(8,128)} %bitcast.8, ...), custom_call_target="tpu_custom_call" | custom-call | flops 99999997952 | tf_op jit(solution)/shard_map/pallas_call | solution.py:25
  1.8 1.5 %copy-done = bf16[2,3,768,768]{3,2,1,0:T(8,128)(2,1)S(1)} copy-done((bf16[2,3,768,768]{3,2,1,0:T(8,128)(2,1)S(1)}, bf16[2,3,768,768]{3,2,1,0:T(8,128)(2,1)}, u32[]{:S(2)}) %copy-start) | copy-done | bytes 7077912
  3.3 0.4 %copy-done.3 = bf16[1024,768]{1,0:T(8,128)(2,1)S(1)} copy-done((bf16[1024,768]{1,0:T(8,128)(2,1)S(1)}, bf16[1024,768]{1,0:T(8,128)(2,1)}, u32[]{:S(2)}) %copy-start.3) | copy-done | bytes 1572888
  3.7 2.9 %shard_map.101 = (bf16[1024,768]{1,0:T(8,128)(2,1)S(1)}, bf16[1024,768]{1,0:T(8,128)(2,1)S(1)}, bf16[528,768]{1,0:T(8,128)(2,1)S(1)}) custom-call(bf16[1024,768]{1,0:T(8,128)(2,1)S(1)} %copy-done.3, bf16[1024,128]{1,0:T(8,128)(2,1)S(1)} %get-tuple-element.41.codes, bf16[128,768]{1,0:T(8,128)(2,1)S(1)} %get-tuple-element.42.embed, ...), custom_call_target="tpu_custom_call" | custom-call | flops 3000000000 | tf_op jit(solution)/shard_map/pallas_call | solution.py:25
  6.6 0.7 %collective-permute-start.3 = (bf16[528,768]{1,0:T(8,128)(2,1)S(1)}, bf16[528,768]{1,0:T(8,128)(2,1)S(1)}, u32[]{:S(2)}, u32[]{:S(2)}) collective-permute-start(bf16[528,768]{1,0:T(8,128)(2,1)S(1)} %get-tuple-element.51.pa), channel_id=1, source_target_pairs={{0,1},{1,0},{2,3},{3,2},{4,5},{5,4},{6,7},{7,6},{8,9},{9,8},{10,11... | collective-permute-start | bytes 2433032 | tf_op jit(solution)/shard_map/ppermute | solution.py:382
  7.3 1.8 %shard_map.104.pb = bf16[448,768]{1,0:T(8,128)(2,1)S(1)} custom-call(bf16[1024,768]{1,0:T(8,128)(2,1)S(1)} %get-tuple-element.46.h0, bf16[2,2304,768]{2,1,0:T(8,128)(2,1)S(1)} %bitcast.3), custom_call_target="tpu_custom_call" | custom-call | flops 3000000000 | tf_op jit(solution)/shard_map/pallas_call | solution.py:25
  9.1 0.1 collective-permute-start.4
  9.2 1.3 %collective-permute-start = (bf16[80,768]{1,0:T(8,128)(2,1)S(1)}, bf16[80,768]{1,0:T(8,128)(2,1)S(1)}, u32[]{:S(2)}, u32[]{:S(2)}) collective-permute-start(bf16[80,768]{1,0:T(8,128)(2,1)S(1)} %get-tuple-element.39), channel_id=1, source_target_pairs={{0,2},{2,0},{4,6},{6,4},{8,10},{10,8},{12,14},{14,12},{1,3},{3,1},... | collective-permute-start | bytes 368648 | tf_op jit(solution)/shard_map/ppermute | solution.py:427
  10.5 0.0 copy-start.1
  10.5 2.3 %collective-permute-start.1 = (bf16[80,768]{1,0:T(8,128)(2,1)S(1)}, bf16[80,768]{1,0:T(8,128)(2,1)S(1)}, u32[]{:S(2)}, u32[]{:S(2)}) collective-permute-start(bf16[80,768]{1,0:T(8,128)(2,1)S(1)} %get-tuple-element.40), channel_id=1, source_target_pairs={{2,4},{4,2},{6,8},{8,6},{10,12},{12,10},{3,5},{5,3},{7,9},{9,7},{1... | collective-permute-start | bytes 368648 | tf_op jit(solution)/shard_map/ppermute | solution.py:428
  12.8 0.9 %collective-permute-done.r_a = bf16[80,768]{1,0:T(8,128)(2,1)S(1)} collective-permute-done((bf16[80,768]{1,0:T(8,128)(2,1)S(1)}, bf16[80,768]{1,0:T(8,128)(2,1)S(1)}, u32[]{:S(2)}, u32[]{:S(2)}) %collective-permute-start) | collective-permute-done | bytes 122912 | tf_op jit(solution)/shard_map/ppermute | solution.py:427
  13.7 3.9 %collective-permute-done.1.r_b = bf16[80,768]{1,0:T(8,128)(2,1)S(1)} collective-permute-done((bf16[80,768]{1,0:T(8,128)(2,1)S(1)}, bf16[80,768]{1,0:T(8,128)(2,1)S(1)}, u32[]{:S(2)}, u32[]{:S(2)}) %collective-permute-start.1) | collective-permute-done | bytes 122912 | tf_op jit(solution)/shard_map/ppermute | solution.py:428
  17.6 0.8 %shard_map.102 = (bf16[160,768]{1,0:T(8,128)(2,1)S(1)}, bf16[80,768]{1,0:T(8,128)(2,1)S(1)}, bf16[80,768]{1,0:T(8,128)(2,1)S(1)}) custom-call(bf16[80,768]{1,0:T(8,128)(2,1)S(1)} %collective-permute-done.r_a, bf16[80,768]{1,0:T(8,128)(2,1)S(1)} %collective-permute-done.1.r_b, bf16[1024,768]{1,0:T(8,128)(2,1)S(1)} %get-tuple-element.46.h0, ...), custom_call_target="tpu_custom_call" | custom-call | flops 3000000000 | tf_op jit(solution)/shard_map/pallas_call | solution.py:25
  18.4 1.6 %collective-permute-start.2 = (bf16[160,768]{1,0:T(8,128)(2,1)S(1)}, bf16[160,768]{1,0:T(8,128)(2,1)S(1)}, u32[]{:S(2)}, u32[]{:S(2)}) collective-permute-start(bf16[160,768]{1,0:T(8,128)(2,1)S(1)} %get-tuple-element.47.pe), channel_id=1, source_target_pairs={{0,1},{1,0},{2,3},{3,2},{4,5},{5,4},{6,7},{7,6},{8,9},{9,8},{10,11... | collective-permute-start | bytes 737288 | tf_op jit(solution)/shard_map/ppermute | solution.py:382
  20.0 0.0 collective-permute-done.3.ra
  20.0 0.0 copy-done.1
  20.0 2.6 %shard_map.103 = (bf16[512,768]{1,0:T(8,128)(2,1)S(1)}, bf16[512,768]{1,0:T(8,128)(2,1)S(1)}, bf16[384,768]{1,0:T(8,128)(2,1)S(1)}, f32[4,768]{1,0:T(4,128)S(1)}) custom-call(bf16[528,768]{1,0:T(8,128)(2,1)S(1)} %get-tuple-element.51.pa, bf16[528,768]{1,0:T(8,128)(2,1)S(1)} %collective-permute-done.3.ra, bf16[1024,768]{1,0:T(8,128)(2,1)S(1)} %get-tuple-element.48.x0, ...), custom_call_target="tpu_custom_call" | custom-call | flops 3000000000 | tf_op jit(solution)/shard_map/pallas_call | solution.py:25
  22.6 0.1 collective-permute-start.7
  22.7 0.0 collective-permute-done.4.rb
  22.7 2.5 %shard_map.105 = (bf16[448,768]{1,0:T(8,128)(2,1)S(1)}, bf16[64,768]{1,0:T(8,128)(2,1)S(1)}, bf16[112,768]{1,0:T(8,128)(2,1)S(1)}, bf16[448,768]{1,0:T(8,128)(2,1)S(1)}) custom-call(bf16[448,768]{1,0:T(8,128)(2,1)S(1)} %shard_map.104.pb, bf16[448,768]{1,0:T(8,128)(2,1)S(1)} %collective-permute-done.4.rb, bf16[1024,768]{1,0:T(8,128)(2,1)S(1)} %get-tuple-element.48.x0, ...), custom_call_target="tpu_custom_call" | custom-call | flops 3000000000 | tf_op jit(solution)/shard_map/pallas_call | solution.py:25
  25.2 0.5 %collective-permute-start.6 = (bf16[448,768]{1,0:T(8,128)(2,1)S(1)}, bf16[448,768]{1,0:T(8,128)(2,1)S(1)}, u32[]{:S(2)}, u32[]{:S(2)}) collective-permute-start(bf16[448,768]{1,0:T(8,128)(2,1)S(1)} %get-tuple-element.59.q), channel_id=1, source_target_pairs={{0,1},{1,0},{2,3},{3,2},{4,5},{5,4},{6,7},{7,6},{8,9},{9,8},{10,11... | collective-permute-start | bytes 2064392 | tf_op jit(solution)/shard_map/ppermute | solution.py:382
  25.8 0.0 collective-permute-done.2.re
  25.8 1.2 %shard_map.106 = (bf16[192,768]{1,0:T(8,128)(2,1)S(1)}, bf16[192,768]{1,0:T(8,128)(2,1)S(1)}) custom-call(bf16[160,768]{1,0:T(8,128)(2,1)S(1)} %get-tuple-element.47.pe, bf16[160,768]{1,0:T(8,128)(2,1)S(1)} %collective-permute-done.2.re, bf16[1024,768]{1,0:T(8,128)(2,1)S(1)} %get-tuple-element.48.x0, bf16[80,768]{1,0:T(8,128)(2,1)S(1)} %get-tuple-element.49.lo, ...), custom_call_target="tpu_custom_call" | custom-call | flops 3000000000 | tf_op jit(solution)/shard_map/pallas_call | solution.py:25
  27.0 0.0 copy-start.2
  27.0 0.1 collective-permute-start.5
  27.1 0.0 collective-permute-done.7.r
  27.1 0.9 %shard_map.107 = (bf16[192,768]{1,0:T(8,128)(2,1)S(1)}, bf16[192,768]{1,0:T(8,128)(2,1)S(1)}) custom-call(bf16[384,768]{1,0:T(8,128)(2,1)S(1)} %get-tuple-element.61.q, bf16[384,768]{1,0:T(8,128)(2,1)S(1)} %collective-permute-done.7.r, bf16[512,768]{1,0:T(8,128)(2,1)S(1)} %get-tuple-element.52.x1a.x1, bf16[2,768,768]{2,1,0:T(8,128)(2,1)S(1)} %copy-done.1, ...), custom_call_target="tpu_custom_call" | custom-call | flops 3000000000 | tf_op jit(solution)/shard_map/pallas_call | solution.py:25
  28.1 0.0 collective-permute-done.6.r
  28.1 0.6 %copy-done.2 = bf16[1536,768]{1,0:T(8,128)(2,1)S(1)} copy-done((bf16[1536,768]{1,0:T(8,128)(2,1)S(1)}, bf16[1536,768]{1,0:T(8,128)(2,1)}, u32[]{:S(2)}) %copy-start.2) | copy-done | bytes 2359320
  28.7 1.3 %shard_map.108 = (bf16[224,768]{1,0:T(8,128)(2,1)S(1)}, bf16[224,768]{1,0:T(8,128)(2,1)S(1)}, f32[192,768]{1,0:T(8,128)S(1)}) custom-call(bf16[448,768]{1,0:T(8,128)(2,1)S(1)} %get-tuple-element.59.q, bf16[448,768]{1,0:T(8,128)(2,1)S(1)} %collective-permute-done.6.r, bf16[448,768]{1,0:T(8,128)(2,1)S(1)} %get-tuple-element.60.x1, ...), custom_call_target="tpu_custom_call" | custom-call | flops 3000000000 | tf_op jit(solution)/shard_map/pallas_call | solution.py:25
  29.9 0.1 collective-permute-start.10
  30.0 0.5 %collective-permute-start.9 = (bf16[192,768]{1,0:T(8,128)(2,1)S(1)}, bf16[192,768]{1,0:T(8,128)(2,1)S(1)}, u32[]{:S(2)}, u32[]{:S(2)}) collective-permute-start(bf16[192,768]{1,0:T(8,128)(2,1)S(1)} %get-tuple-element.62.rest_0_.da), channel_id=1, source_target_pairs={{0,1},{1,0},{2,3},{3,2},{4,5},{5,4},{6,7},{7,6},{8,9},{9,8},{10,11... | collective-permute-start | bytes 884744 | tf_op jit(solution)/shard_map/ppermute | solution.py:382
  30.5 0.0 collective-permute-done.5.r
  30.5 0.9 %shard_map.109 = (bf16[96,768]{1,0:T(8,128)(2,1)S(1)}, bf16[96,768]{1,0:T(8,128)(2,1)S(1)}, f32[224,768]{1,0:T(8,128)S(1)}) custom-call(bf16[192,768]{1,0:T(8,128)(2,1)S(1)} %get-tuple-element.57.q, bf16[192,768]{1,0:T(8,128)(2,1)S(1)} %collective-permute-done.5.r, bf16[192,768]{1,0:T(8,128)(2,1)S(1)} %get-tuple-element.58.x1, ...), custom_call_target="tpu_custom_call" | custom-call | flops 3000000000 | tf_op jit(solution)/shard_map/pallas_call | solution.py:25
  31.4 0.1 collective-permute-start.8
  31.5 0.5 %collective-permute-done.9.ra = bf16[192,768]{1,0:T(8,128)(2,1)S(1)} collective-permute-done((bf16[192,768]{1,0:T(8,128)(2,1)S(1)}, bf16[192,768]{1,0:T(8,128)(2,1)S(1)}, u32[]{:S(2)}, u32[]{:S(2)}) %collective-permute-start.9) | collective-permute-done | bytes 294944 | tf_op jit(solution)/shard_map/ppermute | solution.py:382
  32.1 0.0 collective-permute-done.10.rb
  32.1 0.9 %shard_map.110 = (bf16[192,768]{1,0:T(8,128)(2,1)S(1)}, bf16[224,768]{1,0:T(8,128)(2,1)S(1)}, f32[96,768]{1,0:T(8,128)S(1)}) custom-call(bf16[192,768]{1,0:T(8,128)(2,1)S(1)} %collective-permute-done.9.ra, f32[192,768]{1,0:T(8,128)S(1)} %get-tuple-element.65.la, bf16[224,768]{1,0:T(8,128)(2,1)S(1)} %collective-permute-done.10.rb, ...), custom_call_target="tpu_custom_call" | custom-call | flops 3000000000 | tf_op jit(solution)/shard_map/pallas_call | solution.py:25
  33.0 0.0 collective-permute-done.8.rc
  33.0 1.1 %shard_map.111 = bf16[512,768]{1,0:T(8,128)(2,1)} custom-call(bf16[96,768]{1,0:T(8,128)(2,1)S(1)} %collective-permute-done.8.rc, f32[96,768]{1,0:T(8,128)S(1)} %get-tuple-element.69.lc, bf16[1536,768]{1,0:T(8,128)(2,1)S(1)} %copy-done.2, bf16[96,768]{1,0:T(8,128)(2,1)S(1)} %get-tuple-element.64.dc, bf16[96,768]{1,0:T(8,128)(2,1)S(1)} %get-tuple-element.70.xoc, ...), custom_call_target="tpu_custom_call" | custom-call | tf_op jit(solution)/shard_map/pallas_call | solution.py:513
Async XLA Ops:
  0.0 3.3 %copy-start = (bf16[2,3,768,768]{3,2,1,0:T(8,128)(2,1)S(1)}, bf16[2,3,768,768]{3,2,1,0:T(8,128)(2,1)}, u32[]{:S(2)}) copy-start(bf16[2,3,768,768]{3,2,1,0:T(8,128)(2,1)} %param.15) | copy-start | bytes 21233668
  0.0 3.7 %copy-start.3 = (bf16[1024,768]{1,0:T(8,128)(2,1)S(1)}, bf16[1024,768]{1,0:T(8,128)(2,1)}, u32[]{:S(2)}) copy-start(bf16[1024,768]{1,0:T(8,128)(2,1)} %tower.3) | copy-start | bytes 4718596
  6.6 13.4 %collective-permute-start.3 = (bf16[528,768]{1,0:T(8,128)(2,1)S(1)}, bf16[528,768]{1,0:T(8,128)(2,1)S(1)}, u32[]{:S(2)}, u32[]{:S(2)}) collective-permute-start(bf16[528,768]{1,0:T(8,128)(2,1)S(1)} %get-tuple-element.51.pa), channel_id=1, source_target_pairs={{0,1},{1,0},{2,3},{3,2},{4,5},{5,4},{6,7},{7,6},{8,9},{9,8},{10,11... | collective-permute-start | bytes 2433032 | tf_op jit(solution)/shard_map/ppermute | solution.py:382
  9.1 13.6 %collective-permute-start.4 = (bf16[448,768]{1,0:T(8,128)(2,1)S(1)}, bf16[448,768]{1,0:T(8,128)(2,1)S(1)}, u32[]{:S(2)}, u32[]{:S(2)}) collective-permute-start(bf16[448,768]{1,0:T(8,128)(2,1)S(1)} %shard_map.104.pb), channel_id=1, source_target_pairs={{0,1},{1,0},{2,3},{3,2},{4,5},{5,4},{6,7},{7,6},{8,9},{9,8},{10,11... | collective-permute-start | bytes 2064392 | tf_op jit(solution)/shard_map/ppermute | solution.py:382
  9.2 4.5 %collective-permute-start = (bf16[80,768]{1,0:T(8,128)(2,1)S(1)}, bf16[80,768]{1,0:T(8,128)(2,1)S(1)}, u32[]{:S(2)}, u32[]{:S(2)}) collective-permute-start(bf16[80,768]{1,0:T(8,128)(2,1)S(1)} %get-tuple-element.39), channel_id=1, source_target_pairs={{0,2},{2,0},{4,6},{6,4},{8,10},{10,8},{12,14},{14,12},{1,3},{3,1},... | collective-permute-start | bytes 368648 | tf_op jit(solution)/shard_map/ppermute | solution.py:427
  10.5 9.5 %copy-start.1 = (bf16[2,768,768]{2,1,0:T(8,128)(2,1)S(1)}, bf16[2,768,768]{2,1,0:T(8,128)(2,1)}, u32[]{:S(2)}) copy-start(bf16[2,768,768]{2,1,0:T(8,128)(2,1)} %point_w.11) | copy-start | bytes 7077892
  10.5 7.1 %collective-permute-start.1 = (bf16[80,768]{1,0:T(8,128)(2,1)S(1)}, bf16[80,768]{1,0:T(8,128)(2,1)S(1)}, u32[]{:S(2)}, u32[]{:S(2)}) collective-permute-start(bf16[80,768]{1,0:T(8,128)(2,1)S(1)} %get-tuple-element.40), channel_id=1, source_target_pairs={{2,4},{4,2},{6,8},{8,6},{10,12},{12,10},{3,5},{5,3},{7,9},{9,7},{1... | collective-permute-start | bytes 368648 | tf_op jit(solution)/shard_map/ppermute | solution.py:428
  18.4 7.4 %collective-permute-start.2 = (bf16[160,768]{1,0:T(8,128)(2,1)S(1)}, bf16[160,768]{1,0:T(8,128)(2,1)S(1)}, u32[]{:S(2)}, u32[]{:S(2)}) collective-permute-start(bf16[160,768]{1,0:T(8,128)(2,1)S(1)} %get-tuple-element.47.pe), channel_id=1, source_target_pairs={{0,1},{1,0},{2,3},{3,2},{4,5},{5,4},{6,7},{7,6},{8,9},{9,8},{10,11... | collective-permute-start | bytes 737288 | tf_op jit(solution)/shard_map/ppermute | solution.py:382
  22.6 4.5 %collective-permute-start.7 = (bf16[384,768]{1,0:T(8,128)(2,1)S(1)}, bf16[384,768]{1,0:T(8,128)(2,1)S(1)}, u32[]{:S(2)}, u32[]{:S(2)}) collective-permute-start(bf16[384,768]{1,0:T(8,128)(2,1)S(1)} %get-tuple-element.61.q), channel_id=1, source_target_pairs={{0,1},{1,0},{2,3},{3,2},{4,5},{5,4},{6,7},{7,6},{8,9},{9,8},{10,11... | collective-permute-start | bytes 1769480 | tf_op jit(solution)/shard_map/ppermute | solution.py:382
  25.2 2.8 %collective-permute-start.6 = (bf16[448,768]{1,0:T(8,128)(2,1)S(1)}, bf16[448,768]{1,0:T(8,128)(2,1)S(1)}, u32[]{:S(2)}, u32[]{:S(2)}) collective-permute-start(bf16[448,768]{1,0:T(8,128)(2,1)S(1)} %get-tuple-element.59.q), channel_id=1, source_target_pairs={{0,1},{1,0},{2,3},{3,2},{4,5},{5,4},{6,7},{7,6},{8,9},{9,8},{10,11... | collective-permute-start | bytes 2064392 | tf_op jit(solution)/shard_map/ppermute | solution.py:382
  27.0 1.7 %copy-start.2 = (bf16[1536,768]{1,0:T(8,128)(2,1)S(1)}, bf16[1536,768]{1,0:T(8,128)(2,1)}, u32[]{:S(2)}) copy-start(bf16[1536,768]{1,0:T(8,128)(2,1)} %pool.3) | copy-start | bytes 7077892
  27.0 3.5 %collective-permute-start.5 = (bf16[192,768]{1,0:T(8,128)(2,1)S(1)}, bf16[192,768]{1,0:T(8,128)(2,1)S(1)}, u32[]{:S(2)}, u32[]{:S(2)}) collective-permute-start(bf16[192,768]{1,0:T(8,128)(2,1)S(1)} %get-tuple-element.57.q), channel_id=1, source_target_pairs={{0,1},{1,0},{2,3},{3,2},{4,5},{5,4},{6,7},{7,6},{8,9},{9,8},{10,11... | collective-permute-start | bytes 884744 | tf_op jit(solution)/shard_map/ppermute | solution.py:382
  29.9 2.1 %collective-permute-start.10 = (bf16[224,768]{1,0:T(8,128)(2,1)S(1)}, bf16[224,768]{1,0:T(8,128)(2,1)S(1)}, u32[]{:S(2)}, u32[]{:S(2)}) collective-permute-start(bf16[224,768]{1,0:T(8,128)(2,1)S(1)} %get-tuple-element.63.rest_0_.db), channel_id=1, source_target_pairs={{0,1},{1,0},{2,3},{3,2},{4,5},{5,4},{6,7},{7,6},{8,9},{9,8},{10,11... | collective-permute-start | bytes 1032200 | tf_op jit(solution)/shard_map/ppermute | solution.py:382
  30.0 2.0 %collective-permute-start.9 = (bf16[192,768]{1,0:T(8,128)(2,1)S(1)}, bf16[192,768]{1,0:T(8,128)(2,1)S(1)}, u32[]{:S(2)}, u32[]{:S(2)}) collective-permute-start(bf16[192,768]{1,0:T(8,128)(2,1)S(1)} %get-tuple-element.62.rest_0_.da), channel_id=1, source_target_pairs={{0,1},{1,0},{2,3},{3,2},{4,5},{5,4},{6,7},{7,6},{8,9},{9,8},{10,11... | collective-permute-start | bytes 884744 | tf_op jit(solution)/shard_map/ppermute | solution.py:382
  31.4 1.6 %collective-permute-start.8 = (bf16[96,768]{1,0:T(8,128)(2,1)S(1)}, bf16[96,768]{1,0:T(8,128)(2,1)S(1)}, u32[]{:S(2)}, u32[]{:S(2)}) collective-permute-start(bf16[96,768]{1,0:T(8,128)(2,1)S(1)} %get-tuple-element.64.dc), channel_id=1, source_target_pairs={{0,1},{1,0},{2,3},{3,2},{4,5},{5,4},{6,7},{7,6},{8,9},{9,8},{10,11... | collective-permute-start | bytes 442376 | tf_op jit(solution)/shard_map/ppermute | solution.py:382

commit v5 on v4

--- a/solution.py
+++ b/solution.py
@@ -57,6 +57,46 @@
     return jnp.concatenate(
         [h_ref[base + k * spread : base + k * spread + n] for k in (-1, 0, 1)], axis=1
     )
+
+
+def put_weights(dst, conv_w, layer, start, stop):
+    width = dst.shape[1]
+    half = BF(0.5)
+    for i, m in tiles(start, stop, PIECE):
+        outer = conv_w[layer, i : i + m] + conv_w[layer, 2 * width + i : 2 * width + i + m]
+        outer = half * outer
+        inner = half * conv_w[layer, width + i : width + i + m]
+        dst[0, i : i + m] = outer + inner
+        dst[1, i : i + m] = outer - inner
+
+
+def pair_conv(h_ref, base, spread, n, conv_w, layer, both, dst, v, between=()):
+    width = both.shape[1]
+    between = list(between)
+    for t in range(n // (2 * spread)):
+        s = base + 2 * spread * t
+        x0, x1, x2, x3 = (h_ref[s + k * spread : s + (k + 1) * spread] for k in (-1, 0, 1, 2))
+        rows = slice(t * spread, (t + 1) * spread)
+        v[0, rows] = x0 - x2
+        v[1, rows] = x1 + x2
+        v[2, rows] = x2 - x1
+        v[3, rows] = x1 - x3
+    cols = dst.shape[1]
+    for c in range(0, cols, 256):
+        if between:
+            between.pop(0)()
+        q = slice(c, min(c + 256, cols))
+        m1 = dot(v[0], conv_w[layer, 0:width, q])
+        m2 = dot(v[1], both[0, :, q])
+        m3 = dot(v[2], both[1, :, q])
+        m4 = dot(v[3], conv_w[layer, 2 * width : 3 * width, q])
+        y0 = (m1 + (m2 + m3)).astype(BF)
+        y1 = ((m2 - m3) - m4).astype(BF)
+        for t in range(n // (2 * spread)):
+            rows = slice(t * spread, (t + 1) * spread)
+            at = 2 * spread * t
+            dst[at : at + spread, q] = y0[rows]
+            dst[at + spread : at + 2 * spread, q] = y1[rows]
 
 
 def put_mid(z_ref, own, other, mid_ref, layer, start, n):
@@ -113,7 +153,7 @@
 
 
 def embed_first(a_lo, a_hi, rows):
-    def kernel(tower, codes, embed, s_in, b_in, conv_w, own_mid, x0, h0, pa, emb):
+    def kernel(tower, codes, embed, s_in, b_in, conv_w, own_mid, x0, h0, pa, both, emb, v):
         step = 128
 
         def embed_tile(i, n):
@@ -127,15 +167,20 @@
 
         work = tiles(0, rows, step)
         embed_tile(*work[0])
-        convs = tiles(a_lo, a_hi, step)
-        for t in range(len(work)):
+
+        def stage(t):
             if t + 1 < len(work):
                 embed_tile(*work[t + 1])
             act_tile(*work[t])
-            if convs and sum(convs[0]) + D0 <= t * step:
-                i, n = convs.pop(0)
-                pa[i - a_lo : i - a_lo + n] = dot(taps(h0, i, D0, n), conv_w[0]).astype(BF)
-        assert not convs
+
+        need = -(-(a_hi + D0) // step)
+        for t in range(need):
+            stage(t)
+        put_weights(both, conv_w, 0, 0, both.shape[1])
+        later = [lambda t=t: stage(t) for t in range(need, len(work))]
+        pair_conv(h0, a_lo, D0, a_hi - a_lo, conv_w, 0, both, pa, v, later[:3])
+        for f in later[3:]:
+            f()
         mid = own_mid[...]
         big = mid.astype(BF)
         rest = mid - big.astype(F32)
@@ -149,8 +194,13 @@
 
 
 def first_rest(b_lo, b_hi):
-    def kernel(h0, conv_w, pb):
-        pb[...] = dot(taps(h0, b_lo, D0, b_hi - b_lo), conv_w[0]).astype(BF)
+    def kernel(h0, conv_w, both, pb, both_next, v):
+        third = both.shape[1] // 3
+        later = [
+            lambda k=k: put_weights(both_next, conv_w, 1, k * third, (k + 1) * third)
+            for k in range(3)
+        ]
+        pair_conv(h0, b_lo, D0, b_hi - b_lo, conv_w, 0, both, pb, v, later)
 
     return kernel
 
@@ -181,14 +231,13 @@
 
 def second_first(a_lo, a_hi, c_lo, c_hi):
     def kernel(
-        pa, ra, x0, point_w, conv_w, s_in, b_in, own_mid, x1a, h1a, qa, mid, z, acc,
+        pa, ra, x0, point_w, conv_w, both, s_in, b_in, own_mid, x1a, h1a, qa, mid, z, acc, v,
     ):
         step = 128
         n_a = a_hi - a_lo
         tail = ra[n_a : n_a + EXTRA].astype(F32)
         mid[...] = own_mid[...] + (tail[0:4] + tail[4:8] + tail[8:12])
         work = tiles(0, n_a, step)
-        convs = tiles(c_lo, c_hi, step)
 
         def act_tile(start, n):
             for i, m in tiles(start, start + n, PIECE):
@@ -197,7 +246,7 @@
                 h1a[i : i + m] = act_rows(x, s_in, b_in, 1)
 
         put_mid(z, pa, ra, mid, 0, *work[0])
-        for t in range(len(work) + 2 + len(convs)):
+        for t in range(len(work) + 1):
             if t + 1 < len(work):
                 put_mid(z, pa, ra, mid, 0, *work[t + 1])
             if 1 <= t <= len(work):
@@ -205,17 +254,14 @@
             if t < len(work):
                 i, n = work[t]
                 acc[i : i + n] = dot(z[i : i + n], point_w[0])
-            if convs and sum(convs[0]) + D1 - a_lo <= (t - 1) * step:
-                i, n = convs.pop(0)
-                qa[i - c_lo : i - c_lo + n] = dot(taps(h1a, i - a_lo, D1, n), conv_w[1]).astype(BF)
-        assert not convs
+        pair_conv(h1a, c_lo - a_lo, D1, c_hi - c_lo, conv_w, 1, both, qa, v)
 
     return kernel
 
 
 def second_rest(rows, a_lo, a_hi, c_hi, e_hi):
     def kernel(
-        pb, rb, x0, x1a, h1a, point_w, conv_w, mid, s_in, b_in, x1b, x1t, h1t, qb, h1, z, acc
+        pb, rb, x0, x1a, h1a, point_w, conv_w, both, mid, s_in, b_in, x1b, x1t, h1t, qb, h1, z, acc, v
     ):
         step = 224
         b_hi = rows - D0
@@ -223,7 +269,6 @@
         h1[0 : a_hi - first] = h1a[first - a_lo : a_hi - a_lo]
         x1b[0 : a_hi - c_hi] = x1a[c_hi - a_lo : a_hi - a_lo]
         work = tiles(0, b_hi - a_hi, step)
-        convs = tiles(c_hi, e_hi, step)
 
         def act_tile(start, n):
             for i, m in tiles(start, start + n, PIECE):
@@ -237,7 +282,7 @@
                     x1t[g + keep - e_hi : g + m - e_hi] = x[keep:]
 
         put_mid(z, pb, rb, mid, 0, *work[0])
-        for t in range(len(work) + 2 + len(convs)):
+        for t in range(len(work) + 1):
             if t + 1 < len(work):
                 put_mid(z, pb, rb, mid, 0, *work[t + 1])
             if 1 <= t <= len(work):
@@ -245,9 +290,7 @@
             if t < len(work):
                 i, n = work[t]
                 acc[i : i + n] = dot(z[i : i + n], point_w[0])
-            if t >= 2 and convs:
-                i, n = convs.pop(0)
-                qb[i - c_hi : i - c_hi + n] = dot(taps(h1, i - first, D1, n), conv_w[1]).astype(BF)
+        pair_conv(h1, c_hi - first, D1, e_hi - c_hi, conv_w, 1, both, qb, v)
         h1t[...] = h1[e_hi - D1 - first : b_hi - first]
 
     return kernel
@@ -389,7 +432,7 @@
     rows, width = tower_input.shape
     inner = conv_w.shape[3]
     a_lo, a_hi = D0, rows // 2 + 32
-    c_lo, c_hi, e_hi = 96, rows // 2 - 32, rows - 96
+    c_lo, c_hi, e_hi = 96, rows // 2 - 32, rows - 160
     b_hi = rows - D0
     n_a, n_b = a_hi - a_lo, b_hi - a_hi
     m_a, m_b = c_hi - c_lo, e_hi - c_hi
@@ -412,13 +455,16 @@
             pltpu.VMEM(mid_scale.shape, F32), pltpu.VMEM(mid_shift.shape, F32), dma((8,)),
         ],
     )
-    x0, h0, pa = call(
+    x0, h0, pa, both0 = call(
         "k1a",
         embed_first(a_lo, a_hi, rows),
-        [((rows, width), BF), ((rows, width), BF), ((n_a + EXTRA, inner), BF)],
+        [
+            ((rows, width), BF), ((rows, width), BF), ((n_a + EXTRA, inner), BF),
+            ((2, width, inner), BF),
+        ],
         [],
         [tower_input, codes, embed, s_in, b_in, weights, own_mid],
-        [pltpu.VMEM((rows, width), F32)],
+        [pltpu.VMEM((rows, width), F32), pltpu.VMEM((4, n_a // 2, width), BF)],
     )
     ra = swap_chan(pa)
     count = lax.axis_size("seq")
@@ -426,7 +472,14 @@
     pairs_b = [(i, ((i - 1) ^ 1) + 1) for i in range(1, count - 1)]
     r_a = lax.ppermute(e_a, "seq", pairs_a)
     r_b = lax.ppermute(e_b, "seq", pairs_b)
-    (pb,) = call("k1b", first_rest(a_hi, b_hi), [((n_b, inner), BF)], [], [h0, weights])
+    pb, both1 = call(
+        "k1b",
+        first_rest(a_hi, b_hi),
+        [((n_b, inner), BF), ((2, width, inner), BF)],
+        [],
+        [h0, weights, both0],
+        [pltpu.VMEM((4, n_b // 2, width), BF)],
+    )
     rb = swap_chan(pb)
     x1a, h1a, qa, mid = call(
         "k2a",
@@ -435,8 +488,11 @@
             ((n_a, width), BF), ((n_a, width), BF), ((m_a, inner), BF), ((4, inner), F32),
         ],
         [],
-        [pa, ra, x0, point_w, weights, s_in, b_in, own_mid],
-        [pltpu.VMEM((n_a, inner), BF), pltpu.VMEM((n_a, width), F32)],
+        [pa, ra, x0, point_w, weights, both1, s_in, b_in, own_mid],
+        [
+            pltpu.VMEM((n_a, inner), BF), pltpu.VMEM((n_a, width), F32),
+            pltpu.VMEM((4, m_a // 2, width), BF),
+        ],
     )
     sa = swap_chan(qa)
     pe, lo, hi = call(
@@ -456,10 +512,10 @@
             ((b_hi - e_hi + D1, width), BF), ((m_b, inner), BF),
         ],
         [],
-        [pb, rb, x0, x1a, h1a, point_w, weights, mid, s_in, b_in],
+        [pb, rb, x0, x1a, h1a, point_w, weights, both1, mid, s_in, b_in],
         [
             pltpu.VMEM((b_hi - c_hi + D1, width), BF), pltpu.VMEM((n_b, inner), BF),
-            pltpu.VMEM((n_b, width), F32),
+            pltpu.VMEM((n_b, width), F32), pltpu.VMEM((4, m_b // 2, width), BF),
         ],
     )
     sb = swap_chan(qb)
@@ -478,8 +534,8 @@
     ends, halves = [], []
     for name, q, s, x1, base, m, step in (
         ("a", qa, sa, x1a, c_lo - a_lo, m_a, 128),
-        ("b", qb, sb, x1b, 0, m_b, 224),
-        ("c", qc, sc, x1c, 0, m_c, 192),
+        ("b", qb, sb, x1b, 0, m_b, 128),
+        ("c", qc, sc, x1c, 0, m_c, 128),
     ):
         before = [ends[-1][0], pooling_weight] if ends else []
         dm, xo, *half = call(

time: 34.4 us -> 33.2 us (0.965)
  Pallas kernels: 18.6 us -> 17.5 us
    pallas_call x11, Pallas kernels: 17.6 us -> 16.4 us  [call(): pl.pallas_call(kernel, out_shape=[pltpu.VMEM(shape, dtype) for shape, dty...]
  transfers between devices with their start and end apart: 11 -> 11, of which waited for: 3 -> 3; matrix products, arithmetic and copies ran while one was open for 0% -> 0% of each run, Pallas kernels for 38% -> 36%
where the time goes in v5:
time: 33.2 us; the launch traced here: 33 us
  Pallas kernels  17.5 us (53%)
  starting transfers between devices  7.54 us (23%)
  waiting for transfers between devices  5.22 us (16%)
  local copies, waits for them, and re-layouts  2.55 us (8%)
    pallas_call x11, Pallas kernels, call(): pl.pallas_call(kernel, out_shape=[pltpu.VMEM(shape, dtype) for shape, dty...  16.4 us
    ppermute x9, starting transfers between devices, swap_chan(): return lax.ppermute(a, 'chan', [(0, 1), (1, 0)])  3.93 us
    ppermute x1, waiting for transfers between devices, local(): r_b = lax.ppermute(e_b, 'seq', pairs_b)  3.87 us
    unnamed x8, local copies, waits for them, and re-layouts  2.55 us
    ppermute x1, starting transfers between devices, local(): r_b = lax.ppermute(e_b, 'seq', pairs_b)  2.32 us
    ppermute x1, starting transfers between devices, local(): r_a = lax.ppermute(e_a, 'seq', pairs_a)  1.29 us
    pallas_call x1, Pallas kernels, local(): pl.pallas_call(pool_last(c_lo // 2, c_hi // 2, e_hi // 2), out_shape=jax....  1.09 us
    ppermute x1, waiting for transfers between devices, local(): r_a = lax.ppermute(e_a, 'seq', pairs_a)  0.88 us
  transfers between devices with their start and end apart: 11, of which 3 were waited for; matrix products, arithmetic and copies ran while one was open for 0% of the time, Pallas kernels for 36%

profile of v5, /device:TPU:17, one launch (start us, length us, event | category | flops | bytes accessed | tf_op | source)
XLA Modules:
  0.0 33.0 jit_solution(7496348945922167969)
XLA Ops:
  0.0 0.0 copy-start
  0.0 0.0 copy-start.3
  0.0 1.8 %shard_map.100 = (bf16[80,768]{1,0:T(8,128)(2,1)S(1)}, bf16[80,768]{1,0:T(8,128)(2,1)S(1)}, bf16[1024,128]{1,0:T(8,128)(2,1)S(1)}, bf16[128,768]{1,0:T(8,128)(2,...) custom-call(bf16[1024,768]{1,0:T(8,128)(2,1)} %tower.3, s32[32,1024]{1,0:T(8,128)} %bitcast.8, ...), custom_call_target="tpu_custom_call" | custom-call | flops 99999997952 | tf_op jit(solution)/shard_map/pallas_call | solution.py:25
  1.8 1.5 %copy-done = bf16[2,3,768,768]{3,2,1,0:T(8,128)(2,1)S(1)} copy-done((bf16[2,3,768,768]{3,2,1,0:T(8,128)(2,1)S(1)}, bf16[2,3,768,768]{3,2,1,0:T(8,128)(2,1)}, u32[]{:S(2)}) %copy-start) | copy-done | bytes 7077912
  3.3 0.4 %copy-done.3 = bf16[1024,768]{1,0:T(8,128)(2,1)S(1)} copy-done((bf16[1024,768]{1,0:T(8,128)(2,1)S(1)}, bf16[1024,768]{1,0:T(8,128)(2,1)}, u32[]{:S(2)}) %copy-start.3) | copy-done | bytes 1572888
  3.7 2.7 %shard_map.101 = (bf16[1024,768]{1,0:T(8,128)(2,1)S(1)}, bf16[1024,768]{1,0:T(8,128)(2,1)S(1)}, bf16[528,768]{1,0:T(8,128)(2,1)S(1)}, bf16[2,768,768]{2,1,0:T(8,128)(2,1)S(1)}) custom-call(bf16[1024,768]{1,0:T(8,128)(2,1)S(1)} %copy-done.3, bf16[1024,128]{1,0:T(8,128)(2,1)S(1)} %get-tuple-element.44.codes, bf16[128,768]{1,0:T(8,128)(2,1)S(1)} %get-tuple-element.45.embed, ...), custom_call_target="tpu_custom_call" | custom-call | flops 3000000000 | tf_op jit(solution)/shard_map/pallas_call | solution.py:25
  6.5 0.7 %collective-permute-start.3 = (bf16[528,768]{1,0:T(8,128)(2,1)S(1)}, bf16[528,768]{1,0:T(8,128)(2,1)S(1)}, u32[]{:S(2)}, u32[]{:S(2)}) collective-permute-start(bf16[528,768]{1,0:T(8,128)(2,1)S(1)} %get-tuple-element.54.pa), channel_id=1, source_target_pairs={{0,1},{1,0},{2,3},{3,2},{4,5},{5,4},{6,7},{7,6},{8,9},{9,8},{10,11... | collective-permute-start | bytes 2433032 | tf_op jit(solution)/shard_map/ppermute | solution.py:425
  7.2 1.7 %shard_map.103 = (bf16[448,768]{1,0:T(8,128)(2,1)S(1)}, bf16[2,768,768]{2,1,0:T(8,128)(2,1)S(1)}) custom-call(bf16[1024,768]{1,0:T(8,128)(2,1)S(1)} %get-tuple-element.49.h0, bf16[2,2304,768]{2,1,0:T(8,128)(2,1)S(1)} %bitcast.3, bf16[2,768,768]{2,1,0:T(8,128)(2,1)S(1)} %get-tuple-element.55.both), custom_call_target="tpu_custom_call" | custom-call | flops 3000000000 | tf_op jit(solution)/shard_map/pallas_call | solution.py:25
  8.9 0.1 collective-permute-start.4
  9.0 1.3 %collective-permute-start = (bf16[80,768]{1,0:T(8,128)(2,1)S(1)}, bf16[80,768]{1,0:T(8,128)(2,1)S(1)}, u32[]{:S(2)}, u32[]{:S(2)}) collective-permute-start(bf16[80,768]{1,0:T(8,128)(2,1)S(1)} %get-tuple-element.42), channel_id=1, source_target_pairs={{0,2},{2,0},{4,6},{6,4},{8,10},{10,8},{12,14},{14,12},{1,3},{3,1},... | collective-permute-start | bytes 368648 | tf_op jit(solution)/shard_map/ppermute | solution.py:473
  10.3 0.0 copy-start.1
  10.3 2.3 %collective-permute-start.1 = (bf16[80,768]{1,0:T(8,128)(2,1)S(1)}, bf16[80,768]{1,0:T(8,128)(2,1)S(1)}, u32[]{:S(2)}, u32[]{:S(2)}) collective-permute-start(bf16[80,768]{1,0:T(8,128)(2,1)S(1)} %get-tuple-element.43), channel_id=1, source_target_pairs={{2,4},{4,2},{6,8},{8,6},{10,12},{12,10},{3,5},{5,3},{7,9},{9,7},{1... | collective-permute-start | bytes 368648 | tf_op jit(solution)/shard_map/ppermute | solution.py:474
  12.6 0.9 %collective-permute-done.r_a = bf16[80,768]{1,0:T(8,128)(2,1)S(1)} collective-permute-done((bf16[80,768]{1,0:T(8,128)(2,1)S(1)}, bf16[80,768]{1,0:T(8,128)(2,1)S(1)}, u32[]{:S(2)}, u32[]{:S(2)}) %collective-permute-start) | collective-permute-done | bytes 122912 | tf_op jit(solution)/shard_map/ppermute | solution.py:473
  13.5 3.9 %collective-permute-done.1.r_b = bf16[80,768]{1,0:T(8,128)(2,1)S(1)} collective-permute-done((bf16[80,768]{1,0:T(8,128)(2,1)S(1)}, bf16[80,768]{1,0:T(8,128)(2,1)S(1)}, u32[]{:S(2)}, u32[]{:S(2)}) %collective-permute-start.1) | collective-permute-done | bytes 122912 | tf_op jit(solution)/shard_map/ppermute | solution.py:474
  17.3 0.8 %shard_map.102 = (bf16[160,768]{1,0:T(8,128)(2,1)S(1)}, bf16[80,768]{1,0:T(8,128)(2,1)S(1)}, bf16[80,768]{1,0:T(8,128)(2,1)S(1)}) custom-call(bf16[80,768]{1,0:T(8,128)(2,1)S(1)} %collective-permute-done.r_a, bf16[80,768]{1,0:T(8,128)(2,1)S(1)} %collective-permute-done.1.r_b, bf16[1024,768]{1,0:T(8,128)(2,1)S(1)} %get-tuple-element.49.h0, ...), custom_call_target="tpu_custom_call" | custom-call | flops 3000000000 | tf_op jit(solution)/shard_map/pallas_call | solution.py:25
  18.1 1.6 %collective-permute-start.2 = (bf16[160,768]{1,0:T(8,128)(2,1)S(1)}, bf16[160,768]{1,0:T(8,128)(2,1)S(1)}, u32[]{:S(2)}, u32[]{:S(2)}) collective-permute-start(bf16[160,768]{1,0:T(8,128)(2,1)S(1)} %get-tuple-element.50.pe), channel_id=1, source_target_pairs={{0,1},{1,0},{2,3},{3,2},{4,5},{5,4},{6,7},{7,6},{8,9},{9,8},{10,11... | collective-permute-start | bytes 737288 | tf_op jit(solution)/shard_map/ppermute | solution.py:425
  19.8 0.0 collective-permute-done.3.ra
  19.8 0.0 copy-done.1
  19.8 2.1 %shard_map.104 = (bf16[512,768]{1,0:T(8,128)(2,1)S(1)}, bf16[512,768]{1,0:T(8,128)(2,1)S(1)}, bf16[384,768]{1,0:T(8,128)(2,1)S(1)}, f32[4,768]{1,0:T(4,128)S(1)}) custom-call(bf16[528,768]{1,0:T(8,128)(2,1)S(1)} %get-tuple-element.54.pa, bf16[528,768]{1,0:T(8,128)(2,1)S(1)} %collective-permute-done.3.ra, bf16[1024,768]{1,0:T(8,128)(2,1)S(1)} %get-tuple-element.51.x0, ...), custom_call_target="tpu_custom_call" | custom-call | flops 3000000000 | tf_op jit(solution)/shard_map/pallas_call | solution.py:25
  21.9 0.1 collective-permute-start.7
  22.0 0.0 collective-permute-done.4.rb
  22.0 2.0 %shard_map.105 = (bf16[384,768]{1,0:T(8,128)(2,1)S(1)}, bf16[128,768]{1,0:T(8,128)(2,1)S(1)}, bf16[176,768]{1,0:T(8,128)(2,1)S(1)}, bf16[384,768]{1,0:T(8,128)(2,1)S(1)}) custom-call(bf16[448,768]{1,0:T(8,128)(2,1)S(1)} %get-tuple-element.59.pb, bf16[448,768]{1,0:T(8,128)(2,1)S(1)} %collective-permute-done.4.rb, bf16[1024,768]{1,0:T(8,128)(2,1)S(1)} %get-tuple-element.51.x0, ...), custom_call_target="tpu_custom_call" | custom-call | flops 3000000000 | tf_op jit(solution)/shard_map/pallas_call | solution.py:25
  24.0 0.5 %collective-permute-start.6 = (bf16[384,768]{1,0:T(8,128)(2,1)S(1)}, bf16[384,768]{1,0:T(8,128)(2,1)S(1)}, u32[]{:S(2)}, u32[]{:S(2)}) collective-permute-start(bf16[384,768]{1,0:T(8,128)(2,1)S(1)} %get-tuple-element.65.q), channel_id=1, source_target_pairs={{0,1},{1,0},{2,3},{3,2},{4,5},{5,4},{6,7},{7,6},{8,9},{9,8},{10,11... | collective-permute-start | bytes 1769480 | tf_op jit(solution)/shard_map/ppermute | solution.py:425
  24.5 0.0 collective-permute-done.2.re
  24.5 1.4 %shard_map.106 = (bf16[256,768]{1,0:T(8,128)(2,1)S(1)}, bf16[256,768]{1,0:T(8,128)(2,1)S(1)}) custom-call(bf16[160,768]{1,0:T(8,128)(2,1)S(1)} %get-tuple-element.50.pe, bf16[160,768]{1,0:T(8,128)(2,1)S(1)} %collective-permute-done.2.re, bf16[1024,768]{1,0:T(8,128)(2,1)S(1)} %get-tuple-element.51.x0, bf16[80,768]{1,0:T(8,128)(2,1)S(1)} %get-tuple-element.52.lo, ...), custom_call_target="tpu_custom_call" | custom-call | flops 3000000000 | tf_op jit(solution)/shard_map/pallas_call | solution.py:25
  26.0 0.0 copy-start.2
  26.0 0.1 collective-permute-start.5
  26.1 0.0 collective-permute-done.7.r
  26.1 0.9 %shard_map.107 = (bf16[192,768]{1,0:T(8,128)(2,1)S(1)}, bf16[192,768]{1,0:T(8,128)(2,1)S(1)}) custom-call(bf16[384,768]{1,0:T(8,128)(2,1)S(1)} %get-tuple-element.67.q, bf16[384,768]{1,0:T(8,128)(2,1)S(1)} %collective-permute-done.7.r, bf16[512,768]{1,0:T(8,128)(2,1)S(1)} %get-tuple-element.57.x1a.x1, bf16[2,768,768]{2,1,0:T(8,128)(2,1)S(1)} %copy-done.1, ...), custom_call_target="tpu_custom_call" | custom-call | flops 3000000000 | tf_op jit(solution)/shard_map/pallas_call | solution.py:25
  27.0 0.0 collective-permute-done.6.r
  27.0 0.7 %copy-done.2 = bf16[1536,768]{1,0:T(8,128)(2,1)S(1)} copy-done((bf16[1536,768]{1,0:T(8,128)(2,1)S(1)}, bf16[1536,768]{1,0:T(8,128)(2,1)}, u32[]{:S(2)}) %copy-start.2) | copy-done | bytes 2359320
  27.7 1.1 %shard_map.108 = (bf16[192,768]{1,0:T(8,128)(2,1)S(1)}, bf16[192,768]{1,0:T(8,128)(2,1)S(1)}, f32[192,768]{1,0:T(8,128)S(1)}) custom-call(bf16[384,768]{1,0:T(8,128)(2,1)S(1)} %get-tuple-element.65.q, bf16[384,768]{1,0:T(8,128)(2,1)S(1)} %collective-permute-done.6.r, bf16[384,768]{1,0:T(8,128)(2,1)S(1)} %get-tuple-element.66.x1, ...), custom_call_target="tpu_custom_call" | custom-call | flops 3000000000 | tf_op jit(solution)/shard_map/pallas_call | solution.py:25
  28.8 0.1 collective-permute-start.10
  28.9 0.5 %collective-permute-start.9 = (bf16[192,768]{1,0:T(8,128)(2,1)S(1)}, bf16[192,768]{1,0:T(8,128)(2,1)S(1)}, u32[]{:S(2)}, u32[]{:S(2)}) collective-permute-start(bf16[192,768]{1,0:T(8,128)(2,1)S(1)} %get-tuple-element.68.rest_0_.da), channel_id=1, source_target_pairs={{0,1},{1,0},{2,3},{3,2},{4,5},{5,4},{6,7},{7,6},{8,9},{9,8},{10,11... | collective-permute-start | bytes 884744 | tf_op jit(solution)/shard_map/ppermute | solution.py:425
  29.4 0.0 collective-permute-done.5.r
  29.4 0.9 %shard_map.109 = (bf16[128,768]{1,0:T(8,128)(2,1)S(1)}, bf16[128,768]{1,0:T(8,128)(2,1)S(1)}, f32[192,768]{1,0:T(8,128)S(1)}) custom-call(bf16[256,768]{1,0:T(8,128)(2,1)S(1)} %get-tuple-element.63.q, bf16[256,768]{1,0:T(8,128)(2,1)S(1)} %collective-permute-done.5.r, bf16[256,768]{1,0:T(8,128)(2,1)S(1)} %get-tuple-element.64.x1, ...), custom_call_target="tpu_custom_call" | custom-call | flops 3000000000 | tf_op jit(solution)/shard_map/pallas_call | solution.py:25
  30.3 0.1 collective-permute-start.8
  30.4 0.0 collective-permute-done.10.rb
  30.4 0.4 %collective-permute-done.9.ra = bf16[192,768]{1,0:T(8,128)(2,1)S(1)} collective-permute-done((bf16[192,768]{1,0:T(8,128)(2,1)S(1)}, bf16[192,768]{1,0:T(8,128)(2,1)S(1)}, u32[]{:S(2)}, u32[]{:S(2)}) %collective-permute-start.9) | collective-permute-done | bytes 294944 | tf_op jit(solution)/shard_map/ppermute | solution.py:425
  30.9 0.9 %shard_map.110 = (bf16[192,768]{1,0:T(8,128)(2,1)S(1)}, bf16[192,768]{1,0:T(8,128)(2,1)S(1)}, f32[128,768]{1,0:T(8,128)S(1)}) custom-call(bf16[192,768]{1,0:T(8,128)(2,1)S(1)} %collective-permute-done.9.ra, f32[192,768]{1,0:T(8,128)S(1)} %get-tuple-element.71.la, bf16[192,768]{1,0:T(8,128)(2,1)S(1)} %collective-permute-done.10.rb, ...), custom_call_target="tpu_custom_call" | custom-call | flops 3000000000 | tf_op jit(solution)/shard_map/pallas_call | solution.py:25
  31.8 0.0 collective-permute-done.8.rc
  31.8 1.1 %shard_map.111 = bf16[512,768]{1,0:T(8,128)(2,1)} custom-call(bf16[128,768]{1,0:T(8,128)(2,1)S(1)} %collective-permute-done.8.rc, f32[128,768]{1,0:T(8,128)S(1)} %get-tuple-element.75.lc, bf16[1536,768]{1,0:T(8,128)(2,1)S(1)} %copy-done.2, bf16[128,768]{1,0:T(8,128)(2,1)S(1)} %get-tuple-element.70.dc, bf16[128,768]{1,0:T(8,128)(2,1)S(1)} %get-tuple-element.76.xoc, ...), custom_call_target="tpu_custom_call" | custom-call | tf_op jit(solution)/shard_map/pallas_call | solution.py:569
Async XLA Ops:
  0.0 3.3 %copy-start = (bf16[2,3,768,768]{3,2,1,0:T(8,128)(2,1)S(1)}, bf16[2,3,768,768]{3,2,1,0:T(8,128)(2,1)}, u32[]{:S(2)}) copy-start(bf16[2,3,768,768]{3,2,1,0:T(8,128)(2,1)} %param.15) | copy-start | bytes 21233668
  0.0 3.7 %copy-start.3 = (bf16[1024,768]{1,0:T(8,128)(2,1)S(1)}, bf16[1024,768]{1,0:T(8,128)(2,1)}, u32[]{:S(2)}) copy-start(bf16[1024,768]{1,0:T(8,128)(2,1)} %tower.3) | copy-start | bytes 4718596
  6.5 13.3 %collective-permute-start.3 = (bf16[528,768]{1,0:T(8,128)(2,1)S(1)}, bf16[528,768]{1,0:T(8,128)(2,1)S(1)}, u32[]{:S(2)}, u32[]{:S(2)}) collective-permute-start(bf16[528,768]{1,0:T(8,128)(2,1)S(1)} %get-tuple-element.54.pa), channel_id=1, source_target_pairs={{0,1},{1,0},{2,3},{3,2},{4,5},{5,4},{6,7},{7,6},{8,9},{9,8},{10,11... | collective-permute-start | bytes 2433032 | tf_op jit(solution)/shard_map/ppermute | solution.py:425
  8.9 13.1 %collective-permute-start.4 = (bf16[448,768]{1,0:T(8,128)(2,1)S(1)}, bf16[448,768]{1,0:T(8,128)(2,1)S(1)}, u32[]{:S(2)}, u32[]{:S(2)}) collective-permute-start(bf16[448,768]{1,0:T(8,128)(2,1)S(1)} %get-tuple-element.59.pb), channel_id=1, source_target_pairs={{0,1},{1,0},{2,3},{3,2},{4,5},{5,4},{6,7},{7,6},{8,9},{9,8},{10,11... | collective-permute-start | bytes 2064392 | tf_op jit(solution)/shard_map/ppermute | solution.py:425
  9.0 4.5 %collective-permute-start = (bf16[80,768]{1,0:T(8,128)(2,1)S(1)}, bf16[80,768]{1,0:T(8,128)(2,1)S(1)}, u32[]{:S(2)}, u32[]{:S(2)}) collective-permute-start(bf16[80,768]{1,0:T(8,128)(2,1)S(1)} %get-tuple-element.42), channel_id=1, source_target_pairs={{0,2},{2,0},{4,6},{6,4},{8,10},{10,8},{12,14},{14,12},{1,3},{3,1},... | collective-permute-start | bytes 368648 | tf_op jit(solution)/shard_map/ppermute | solution.py:473
  10.3 9.5 %copy-start.1 = (bf16[2,768,768]{2,1,0:T(8,128)(2,1)S(1)}, bf16[2,768,768]{2,1,0:T(8,128)(2,1)}, u32[]{:S(2)}) copy-start(bf16[2,768,768]{2,1,0:T(8,128)(2,1)} %point_w.11) | copy-start | bytes 7077892
  10.3 7.1 %collective-permute-start.1 = (bf16[80,768]{1,0:T(8,128)(2,1)S(1)}, bf16[80,768]{1,0:T(8,128)(2,1)S(1)}, u32[]{:S(2)}, u32[]{:S(2)}) collective-permute-start(bf16[80,768]{1,0:T(8,128)(2,1)S(1)} %get-tuple-element.43), channel_id=1, source_target_pairs={{2,4},{4,2},{6,8},{8,6},{10,12},{12,10},{3,5},{5,3},{7,9},{9,7},{1... | collective-permute-start | bytes 368648 | tf_op jit(solution)/shard_map/ppermute | solution.py:474
  18.1 6.4 %collective-permute-start.2 = (bf16[160,768]{1,0:T(8,128)(2,1)S(1)}, bf16[160,768]{1,0:T(8,128)(2,1)S(1)}, u32[]{:S(2)}, u32[]{:S(2)}) collective-permute-start(bf16[160,768]{1,0:T(8,128)(2,1)S(1)} %get-tuple-element.50.pe), channel_id=1, source_target_pairs={{0,1},{1,0},{2,3},{3,2},{4,5},{5,4},{6,7},{7,6},{8,9},{9,8},{10,11... | collective-permute-start | bytes 737288 | tf_op jit(solution)/shard_map/ppermute | solution.py:425
  21.9 4.2 %collective-permute-start.7 = (bf16[384,768]{1,0:T(8,128)(2,1)S(1)}, bf16[384,768]{1,0:T(8,128)(2,1)S(1)}, u32[]{:S(2)}, u32[]{:S(2)}) collective-permute-start(bf16[384,768]{1,0:T(8,128)(2,1)S(1)} %get-tuple-element.67.q), channel_id=1, source_target_pairs={{0,1},{1,0},{2,3},{3,2},{4,5},{5,4},{6,7},{7,6},{8,9},{9,8},{10,11... | collective-permute-start | bytes 1769480 | tf_op jit(solution)/shard_map/ppermute | solution.py:425
  24.0 3.0 %collective-permute-start.6 = (bf16[384,768]{1,0:T(8,128)(2,1)S(1)}, bf16[384,768]{1,0:T(8,128)(2,1)S(1)}, u32[]{:S(2)}, u32[]{:S(2)}) collective-permute-start(bf16[384,768]{1,0:T(8,128)(2,1)S(1)} %get-tuple-element.65.q), channel_id=1, source_target_pairs={{0,1},{1,0},{2,3},{3,2},{4,5},{5,4},{6,7},{7,6},{8,9},{9,8},{10,11... | collective-permute-start | bytes 1769480 | tf_op jit(solution)/shard_map/ppermute | solution.py:425
  26.0 1.7 %copy-start.2 = (bf16[1536,768]{1,0:T(8,128)(2,1)S(1)}, bf16[1536,768]{1,0:T(8,128)(2,1)}, u32[]{:S(2)}) copy-start(bf16[1536,768]{1,0:T(8,128)(2,1)} %pool.3) | copy-start | bytes 7077892
  26.0 3.4 %collective-permute-start.5 = (bf16[256,768]{1,0:T(8,128)(2,1)S(1)}, bf16[256,768]{1,0:T(8,128)(2,1)S(1)}, u32[]{:S(2)}, u32[]{:S(2)}) collective-permute-start(bf16[256,768]{1,0:T(8,128)(2,1)S(1)} %get-tuple-element.63.q), channel_id=1, source_target_pairs={{0,1},{1,0},{2,3},{3,2},{4,5},{5,4},{6,7},{7,6},{8,9},{9,8},{10,11... | collective-permute-start | bytes 1179656 | tf_op jit(solution)/shard_map/ppermute | solution.py:425
  28.8 1.6 %collective-permute-start.10 = (bf16[192,768]{1,0:T(8,128)(2,1)S(1)}, bf16[192,768]{1,0:T(8,128)(2,1)S(1)}, u32[]{:S(2)}, u32[]{:S(2)}) collective-permute-start(bf16[192,768]{1,0:T(8,128)(2,1)S(1)} %get-tuple-element.69.rest_0_.db), channel_id=1, source_target_pairs={{0,1},{1,0},{2,3},{3,2},{4,5},{5,4},{6,7},{7,6},{8,9},{9,8},{10,11... | collective-permute-start | bytes 884744 | tf_op jit(solution)/shard_map/ppermute | solution.py:425
  28.9 2.0 %collective-permute-start.9 = (bf16[192,768]{1,0:T(8,128)(2,1)S(1)}, bf16[192,768]{1,0:T(8,128)(2,1)S(1)}, u32[]{:S(2)}, u32[]{:S(2)}) collective-permute-start(bf16[192,768]{1,0:T(8,128)(2,1)S(1)} %get-tuple-element.68.rest_0_.da), channel_id=1, source_target_pairs={{0,1},{1,0},{2,3},{3,2},{4,5},{5,4},{6,7},{7,6},{8,9},{9,8},{10,11... | collective-permute-start | bytes 884744 | tf_op jit(solution)/shard_map/ppermute | solution.py:425
  30.3 1.5 %collective-permute-start.8 = (bf16[128,768]{1,0:T(8,128)(2,1)S(1)}, bf16[128,768]{1,0:T(8,128)(2,1)S(1)}, u32[]{:S(2)}, u32[]{:S(2)}) collective-permute-start(bf16[128,768]{1,0:T(8,128)(2,1)S(1)} %get-tuple-element.70.dc), channel_id=1, source_target_pairs={{0,1},{1,0},{2,3},{3,2},{4,5},{5,4},{6,7},{7,6},{8,9},{9,8},{10,11... | collective-permute-start | bytes 589832 | tf_op jit(solution)/shard_map/ppermute | solution.py:425

commit v6 on v5

--- a/solution.py
+++ b/solution.py
@@ -70,7 +70,7 @@
         dst[1, i : i + m] = outer - inner
 
 
-def pair_conv(h_ref, base, spread, n, conv_w, layer, both, dst, v, between=()):
+def pair_conv(h_ref, base, spread, n, conv_w, layer, both, dst, v, between=(), early=None):
     width = both.shape[1]
     between = list(between)
     for t in range(n // (2 * spread)):
@@ -87,9 +87,11 @@
             between.pop(0)()
         q = slice(c, min(c + 256, cols))
         m1 = dot(v[0], conv_w[layer, 0:width, q])
+        m4 = dot(v[3], conv_w[layer, 2 * width : 3 * width, q])
+        if early is not None and c == 0:
+            early()
         m2 = dot(v[1], both[0, :, q])
         m3 = dot(v[2], both[1, :, q])
-        m4 = dot(v[3], conv_w[layer, 2 * width : 3 * width, q])
         y0 = (m1 + (m2 + m3)).astype(BF)
         y1 = ((m2 - m3) - m4).astype(BF)
         for t in range(n // (2 * spread)):
@@ -153,17 +155,16 @@
 
 
 def embed_first(a_lo, a_hi, rows):
-    def kernel(tower, codes, embed, s_in, b_in, conv_w, own_mid, x0, h0, pa, both, emb, v):
+    def kernel(tower, codes, embed, s_in, b_in, conv_w, own_mid, x0, h0, pa, both, v):
         step = 128
 
         def embed_tile(i, n):
-            emb[i : i + n] = dot(codes[i : i + n], embed[...])
+            x = tower[i : i + n].astype(F32) + dot(codes[i : i + n], embed[...])
+            x0[i : i + n] = x.astype(BF)
 
         def act_tile(start, n):
             for i, m in tiles(start, start + n, PIECE):
-                x = (tower[i : i + m].astype(F32) + emb[i : i + m]).astype(BF)
-                x0[i : i + m] = x
-                h0[i : i + m] = act_rows(x, s_in, b_in, 0)
+                h0[i : i + m] = act_rows(x0[i : i + m], s_in, b_in, 0)
 
         work = tiles(0, rows, step)
         embed_tile(*work[0])
@@ -176,10 +177,12 @@
         need = -(-(a_hi + D0) // step)
         for t in range(need):
             stage(t)
-        put_weights(both, conv_w, 0, 0, both.shape[1])
         later = [lambda t=t: stage(t) for t in range(need, len(work))]
-        pair_conv(h0, a_lo, D0, a_hi - a_lo, conv_w, 0, both, pa, v, later[:3])
-        for f in later[3:]:
+        pair_conv(
+            h0, a_lo, D0, a_hi - a_lo, conv_w, 0, both, pa, v, [lambda: None] + later[:2],
+            lambda: put_weights(both, conv_w, 0, 0, both.shape[1]),
+        )
+        for f in later[2:]:
             f()
         mid = own_mid[...]
         big = mid.astype(BF)
@@ -273,7 +276,7 @@
         def act_tile(start, n):
             for i, m in tiles(start, start + n, PIECE):
                 g = a_hi + i
-                x = (x0[g : g + m].astype(F32) + acc[i : i + m]).astype(BF)
+                x = acc[i : i + m]
                 h1[g - first : g - first + m] = act_rows(x, s_in, b_in, 1)
                 keep = max(0, min(m, e_hi - g))
                 if keep:
@@ -289,7 +292,8 @@
                 act_tile(*work[t - 1])
             if t < len(work):
                 i, n = work[t]
-                acc[i : i + n] = dot(z[i : i + n], point_w[0])
+                x = x0[a_hi + i : a_hi + i + n].astype(F32) + dot(z[i : i + n], point_w[0])
+                acc[i : i + n] = x.astype(BF)
         pair_conv(h1, c_hi - first, D1, e_hi - c_hi, conv_w, 1, both, qb, v)
         h1t[...] = h1[e_hi - D1 - first : b_hi - first]
 
@@ -389,10 +393,10 @@
         ).astype(BF)
 
 
-def pool_first(ra, la, rb, lb, dc, pool, da, xoa, db, xob, ya, yb, lc, acc_a, acc_b):
+def pool_first(ra, la, rb, dc, pool, da, xoa, db, xob, ya, yb, lc, acc_a, acc_b):
     mine, theirs = own_half(ra.shape[1])
     acc_a[...] = la[...] + dot(ra[...], pool[theirs, :])
-    acc_b[...] = lb[...] + dot(rb[...], pool[theirs, :])
+    acc_b[...] = dot(db[...], pool[mine, :]) + dot(rb[...], pool[theirs, :])
     finish(ya, xoa, da, acc_a)
     lc[...] = dot(dc[...], pool[mine, :])
     finish(yb, xob, db, acc_b)
@@ -464,7 +468,7 @@
         ],
         [],
         [tower_input, codes, embed, s_in, b_in, weights, own_mid],
-        [pltpu.VMEM((rows, width), F32), pltpu.VMEM((4, n_a // 2, width), BF)],
+        [pltpu.VMEM((4, n_a // 2, width), BF)],
     )
     ra = swap_chan(pa)
     count = lax.axis_size("seq")
@@ -515,7 +519,7 @@
         [pb, rb, x0, x1a, h1a, point_w, weights, both1, mid, s_in, b_in],
         [
             pltpu.VMEM((b_hi - c_hi + D1, width), BF), pltpu.VMEM((n_b, inner), BF),
-            pltpu.VMEM((n_b, width), F32), pltpu.VMEM((4, m_b // 2, width), BF),
+            pltpu.VMEM((n_b, width), BF), pltpu.VMEM((4, m_b // 2, width), BF),
         ],
     )
     sb = swap_chan(qb)
@@ -537,7 +541,7 @@
         ("b", qb, sb, x1b, 0, m_b, 128),
         ("c", qc, sc, x1c, 0, m_c, 128),
     ):
-        before = [ends[-1][0], pooling_weight] if ends else []
+        before = [ends[0][0], pooling_weight] if name == "b" else []
         dm, xo, *half = call(
             "k3" + name,
             last_point(base, m, step, bool(before)),
@@ -553,13 +557,13 @@
         halves += half
         ends.append((dm, swap_chan(dm), xo))
     (da, ta, xoa), (db, tb, xob), (dc, tc, xoc) = ends
-    la, lb = halves
+    (la,) = halves
     ya, yb, lc = call(
         "k4",
         pool_first,
         [((m_a // 2, width), BF), ((m_b // 2, width), BF), ((m_c // 2, width), F32)],
         [],
-        [ta, la, tb, lb, dc, pooling_weight, da, xoa, db, xob],
+        [ta, la, tb, dc, pooling_weight, da, xoa, db, xob],
         [pltpu.VMEM((m_a // 2, width), F32), pltpu.VMEM((m_b // 2, width), F32)],
     )
     vm = [

time: 33.2 us -> 33.1 us (level)
  Pallas kernels: 17.5 us -> 17.1 us
  transfers between devices with their start and end apart: 11 -> 11, of which waited for: 3 -> 4; matrix products, arithmetic and copies ran while one was open for 0% -> 0% of each run, Pallas kernels for 36% -> 36%
where the time goes in v6:
time: 33.1 us; the launch traced here: 32.9 us
  Pallas kernels  17.1 us (52%)
  starting transfers between devices  7.54 us (23%)
  waiting for transfers between devices  5.41 us (16%)
  local copies, waits for them, and re-layouts  2.55 us (8%)
    pallas_call x11, Pallas kernels, call(): pl.pallas_call(kernel, out_shape=[pltpu.VMEM(shape, dtype) for shape, dty...  16 us
    ppermute x9, starting transfers between devices, swap_chan(): return lax.ppermute(a, 'chan', [(0, 1), (1, 0)])  3.92 us
    ppermute x1, waiting for transfers between devices, local(): r_b = lax.ppermute(e_b, 'seq', pairs_b)  3.87 us
    unnamed x8, local copies, waits for them, and re-layouts  2.55 us
    ppermute x1, starting transfers between devices, local(): r_b = lax.ppermute(e_b, 'seq', pairs_b)  2.32 us
    ppermute x1, starting transfers between devices, local(): r_a = lax.ppermute(e_a, 'seq', pairs_a)  1.3 us
    pallas_call x1, Pallas kernels, local(): pl.pallas_call(pool_last(c_lo // 2, c_hi // 2, e_hi // 2), out_shape=jax....  1.09 us
    ppermute x1, waiting for transfers between devices, local(): r_a = lax.ppermute(e_a, 'seq', pairs_a)  0.88 us
  transfers between devices with their start and end apart: 11, of which 4 were waited for; matrix products, arithmetic and copies ran while one was open for 0% of the time, Pallas kernels for 36%

profile of v6, /device:TPU:17, one launch (start us, length us, event | category | flops | bytes accessed | tf_op | source)
XLA Modules:
  0.0 32.9 jit_solution(10730852551635342623)
XLA Ops:
  0.0 0.0 copy-start
  0.0 0.0 copy-start.3
  0.0 1.8 %shard_map.100 = (bf16[80,768]{1,0:T(8,128)(2,1)S(1)}, bf16[80,768]{1,0:T(8,128)(2,1)S(1)}, bf16[1024,128]{1,0:T(8,128)(2,1)S(1)}, bf16[128,768]{1,0:T(8,128)(2,...) custom-call(bf16[1024,768]{1,0:T(8,128)(2,1)} %tower.3, s32[32,1024]{1,0:T(8,128)} %bitcast.8, ...), custom_call_target="tpu_custom_call" | custom-call | flops 99999997952 | tf_op jit(solution)/shard_map/pallas_call | solution.py:25
  1.8 1.5 %copy-done = bf16[2,3,768,768]{3,2,1,0:T(8,128)(2,1)S(1)} copy-done((bf16[2,3,768,768]{3,2,1,0:T(8,128)(2,1)S(1)}, bf16[2,3,768,768]{3,2,1,0:T(8,128)(2,1)}, u32[]{:S(2)}) %copy-start) | copy-done | bytes 7077912
  3.3 0.4 %copy-done.3 = bf16[1024,768]{1,0:T(8,128)(2,1)S(1)} copy-done((bf16[1024,768]{1,0:T(8,128)(2,1)S(1)}, bf16[1024,768]{1,0:T(8,128)(2,1)}, u32[]{:S(2)}) %copy-start.3) | copy-done | bytes 1572888
  3.7 2.5 %shard_map.101 = (bf16[1024,768]{1,0:T(8,128)(2,1)S(1)}, bf16[1024,768]{1,0:T(8,128)(2,1)S(1)}, bf16[528,768]{1,0:T(8,128)(2,1)S(1)}, bf16[2,768,768]{2,1,0:T(8,128)(2,1)S(1)}) custom-call(bf16[1024,768]{1,0:T(8,128)(2,1)S(1)} %copy-done.3, bf16[1024,128]{1,0:T(8,128)(2,1)S(1)} %get-tuple-element.43.codes, bf16[128,768]{1,0:T(8,128)(2,1)S(1)} %get-tuple-element.44.embed, ...), custom_call_target="tpu_custom_call" | custom-call | flops 3000000000 | tf_op jit(solution)/shard_map/pallas_call | solution.py:25
  6.2 0.7 %collective-permute-start.3 = (bf16[528,768]{1,0:T(8,128)(2,1)S(1)}, bf16[528,768]{1,0:T(8,128)(2,1)S(1)}, u32[]{:S(2)}, u32[]{:S(2)}) collective-permute-start(bf16[528,768]{1,0:T(8,128)(2,1)S(1)} %get-tuple-element.53.pa), channel_id=1, source_target_pairs={{0,1},{1,0},{2,3},{3,2},{4,5},{5,4},{6,7},{7,6},{8,9},{9,8},{10,11... | collective-permute-start | bytes 2433032 | tf_op jit(solution)/shard_map/ppermute | solution.py:429
  7.0 1.6 %shard_map.103 = (bf16[448,768]{1,0:T(8,128)(2,1)S(1)}, bf16[2,768,768]{2,1,0:T(8,128)(2,1)S(1)}) custom-call(bf16[1024,768]{1,0:T(8,128)(2,1)S(1)} %get-tuple-element.48.h0, bf16[2,2304,768]{2,1,0:T(8,128)(2,1)S(1)} %bitcast.3, bf16[2,768,768]{2,1,0:T(8,128)(2,1)S(1)} %get-tuple-element.54.both), custom_call_target="tpu_custom_call" | custom-call | flops 3000000000 | tf_op jit(solution)/shard_map/pallas_call | solution.py:25
  8.5 0.1 collective-permute-start.4
  8.6 1.3 %collective-permute-start = (bf16[80,768]{1,0:T(8,128)(2,1)S(1)}, bf16[80,768]{1,0:T(8,128)(2,1)S(1)}, u32[]{:S(2)}, u32[]{:S(2)}) collective-permute-start(bf16[80,768]{1,0:T(8,128)(2,1)S(1)} %get-tuple-element.41), channel_id=1, source_target_pairs={{0,2},{2,0},{4,6},{6,4},{8,10},{10,8},{12,14},{14,12},{1,3},{3,1},... | collective-permute-start | bytes 368648 | tf_op jit(solution)/shard_map/ppermute | solution.py:477
  9.9 0.0 copy-start.1
  9.9 2.3 %collective-permute-start.1 = (bf16[80,768]{1,0:T(8,128)(2,1)S(1)}, bf16[80,768]{1,0:T(8,128)(2,1)S(1)}, u32[]{:S(2)}, u32[]{:S(2)}) collective-permute-start(bf16[80,768]{1,0:T(8,128)(2,1)S(1)} %get-tuple-element.42), channel_id=1, source_target_pairs={{2,4},{4,2},{6,8},{8,6},{10,12},{12,10},{3,5},{5,3},{7,9},{9,7},{1... | collective-permute-start | bytes 368648 | tf_op jit(solution)/shard_map/ppermute | solution.py:478
  12.3 0.9 %collective-permute-done.r_a = bf16[80,768]{1,0:T(8,128)(2,1)S(1)} collective-permute-done((bf16[80,768]{1,0:T(8,128)(2,1)S(1)}, bf16[80,768]{1,0:T(8,128)(2,1)S(1)}, u32[]{:S(2)}, u32[]{:S(2)}) %collective-permute-start) | collective-permute-done | bytes 122912 | tf_op jit(solution)/shard_map/ppermute | solution.py:477
  13.1 3.9 %collective-permute-done.1.r_b = bf16[80,768]{1,0:T(8,128)(2,1)S(1)} collective-permute-done((bf16[80,768]{1,0:T(8,128)(2,1)S(1)}, bf16[80,768]{1,0:T(8,128)(2,1)S(1)}, u32[]{:S(2)}, u32[]{:S(2)}) %collective-permute-start.1) | collective-permute-done | bytes 122912 | tf_op jit(solution)/shard_map/ppermute | solution.py:478
  17.0 0.8 %shard_map.102 = (bf16[160,768]{1,0:T(8,128)(2,1)S(1)}, bf16[80,768]{1,0:T(8,128)(2,1)S(1)}, bf16[80,768]{1,0:T(8,128)(2,1)S(1)}) custom-call(bf16[80,768]{1,0:T(8,128)(2,1)S(1)} %collective-permute-done.r_a, bf16[80,768]{1,0:T(8,128)(2,1)S(1)} %collective-permute-done.1.r_b, bf16[1024,768]{1,0:T(8,128)(2,1)S(1)} %get-tuple-element.48.h0, ...), custom_call_target="tpu_custom_call" | custom-call | flops 3000000000 | tf_op jit(solution)/shard_map/pallas_call | solution.py:25
  17.8 1.6 %collective-permute-start.2 = (bf16[160,768]{1,0:T(8,128)(2,1)S(1)}, bf16[160,768]{1,0:T(8,128)(2,1)S(1)}, u32[]{:S(2)}, u32[]{:S(2)}) collective-permute-start(bf16[160,768]{1,0:T(8,128)(2,1)S(1)} %get-tuple-element.49.pe), channel_id=1, source_target_pairs={{0,1},{1,0},{2,3},{3,2},{4,5},{5,4},{6,7},{7,6},{8,9},{9,8},{10,11... | collective-permute-start | bytes 737288 | tf_op jit(solution)/shard_map/ppermute | solution.py:429
  19.4 0.0 collective-permute-done.3.ra
  19.4 0.0 copy-done.1
  19.4 2.1 %shard_map.104 = (bf16[512,768]{1,0:T(8,128)(2,1)S(1)}, bf16[512,768]{1,0:T(8,128)(2,1)S(1)}, bf16[384,768]{1,0:T(8,128)(2,1)S(1)}, f32[4,768]{1,0:T(4,128)S(1)}) custom-call(bf16[528,768]{1,0:T(8,128)(2,1)S(1)} %get-tuple-element.53.pa, bf16[528,768]{1,0:T(8,128)(2,1)S(1)} %collective-permute-done.3.ra, bf16[1024,768]{1,0:T(8,128)(2,1)S(1)} %get-tuple-element.50.x0, ...), custom_call_target="tpu_custom_call" | custom-call | flops 3000000000 | tf_op jit(solution)/shard_map/pallas_call | solution.py:25
  21.6 0.1 collective-permute-start.7
  21.7 0.0 collective-permute-done.4.rb
  21.7 1.9 %shard_map.105 = (bf16[384,768]{1,0:T(8,128)(2,1)S(1)}, bf16[128,768]{1,0:T(8,128)(2,1)S(1)}, bf16[176,768]{1,0:T(8,128)(2,1)S(1)}, bf16[384,768]{1,0:T(8,128)(2,1)S(1)}) custom-call(bf16[448,768]{1,0:T(8,128)(2,1)S(1)} %get-tuple-element.58.pb, bf16[448,768]{1,0:T(8,128)(2,1)S(1)} %collective-permute-done.4.rb, bf16[1024,768]{1,0:T(8,128)(2,1)S(1)} %get-tuple-element.50.x0, ...), custom_call_target="tpu_custom_call" | custom-call | flops 3000000000 | tf_op jit(solution)/shard_map/pallas_call | solution.py:25
  23.6 0.5 %collective-permute-start.9 = (bf16[384,768]{1,0:T(8,128)(2,1)S(1)}, bf16[384,768]{1,0:T(8,128)(2,1)S(1)}, u32[]{:S(2)}, u32[]{:S(2)}) collective-permute-start(bf16[384,768]{1,0:T(8,128)(2,1)S(1)} %get-tuple-element.67.q), channel_id=1, source_target_pairs={{0,1},{1,0},{2,3},{3,2},{4,5},{5,4},{6,7},{7,6},{8,9},{9,8},{10,11... | collective-permute-start | bytes 1769480 | tf_op jit(solution)/shard_map/ppermute | solution.py:429
  24.2 0.0 collective-permute-done.2.re
  24.2 1.4 %shard_map.106 = (bf16[256,768]{1,0:T(8,128)(2,1)S(1)}, bf16[256,768]{1,0:T(8,128)(2,1)S(1)}) custom-call(bf16[160,768]{1,0:T(8,128)(2,1)S(1)} %get-tuple-element.49.pe, bf16[160,768]{1,0:T(8,128)(2,1)S(1)} %collective-permute-done.2.re, bf16[1024,768]{1,0:T(8,128)(2,1)S(1)} %get-tuple-element.50.x0, bf16[80,768]{1,0:T(8,128)(2,1)S(1)} %get-tuple-element.51.lo, ...), custom_call_target="tpu_custom_call" | custom-call | flops 3000000000 | tf_op jit(solution)/shard_map/pallas_call | solution.py:25
  25.6 0.0 copy-start.2
  25.6 0.1 collective-permute-start.5
  25.7 0.0 collective-permute-done.7.r
  25.7 0.9 %shard_map.108 = (bf16[192,768]{1,0:T(8,128)(2,1)S(1)}, bf16[192,768]{1,0:T(8,128)(2,1)S(1)}) custom-call(bf16[384,768]{1,0:T(8,128)(2,1)S(1)} %get-tuple-element.65.q, bf16[384,768]{1,0:T(8,128)(2,1)S(1)} %collective-permute-done.7.r, bf16[512,768]{1,0:T(8,128)(2,1)S(1)} %get-tuple-element.56.x1a.x1, bf16[2,768,768]{2,1,0:T(8,128)(2,1)S(1)} %copy-done.1, ...), custom_call_target="tpu_custom_call" | custom-call | flops 3000000000 | tf_op jit(solution)/shard_map/pallas_call | solution.py:25
  26.6 0.0 collective-permute-done.9.r
  26.6 0.6 %copy-done.2 = bf16[1536,768]{1,0:T(8,128)(2,1)S(1)} copy-done((bf16[1536,768]{1,0:T(8,128)(2,1)S(1)}, bf16[1536,768]{1,0:T(8,128)(2,1)}, u32[]{:S(2)}) %copy-start.2) | copy-done | bytes 2359320
  27.3 1.1 %shard_map.109 = (bf16[192,768]{1,0:T(8,128)(2,1)S(1)}, bf16[192,768]{1,0:T(8,128)(2,1)S(1)}, f32[192,768]{1,0:T(8,128)S(1)}) custom-call(bf16[384,768]{1,0:T(8,128)(2,1)S(1)} %get-tuple-element.67.q, bf16[384,768]{1,0:T(8,128)(2,1)S(1)} %collective-permute-done.9.r, bf16[384,768]{1,0:T(8,128)(2,1)S(1)} %get-tuple-element.68.x1, ...), custom_call_target="tpu_custom_call" | custom-call | flops 3000000000 | tf_op jit(solution)/shard_map/pallas_call | solution.py:25
  28.4 0.1 collective-permute-start.10
  28.5 0.5 %collective-permute-start.8 = (bf16[192,768]{1,0:T(8,128)(2,1)S(1)}, bf16[192,768]{1,0:T(8,128)(2,1)S(1)}, u32[]{:S(2)}, u32[]{:S(2)}) collective-permute-start(bf16[192,768]{1,0:T(8,128)(2,1)S(1)} %get-tuple-element.66.rest_0_.da), channel_id=1, source_target_pairs={{0,1},{1,0},{2,3},{3,2},{4,5},{5,4},{6,7},{7,6},{8,9},{9,8},{10,11... | collective-permute-start | bytes 884744 | tf_op jit(solution)/shard_map/ppermute | solution.py:429
  29.0 0.0 collective-permute-done.5.r
  29.0 0.7 %shard_map.107 = (bf16[128,768]{1,0:T(8,128)(2,1)S(1)}, bf16[128,768]{1,0:T(8,128)(2,1)S(1)}) custom-call(bf16[256,768]{1,0:T(8,128)(2,1)S(1)} %get-tuple-element.62.q, bf16[256,768]{1,0:T(8,128)(2,1)S(1)} %collective-permute-done.5.r, bf16[256,768]{1,0:T(8,128)(2,1)S(1)} %get-tuple-element.63.x1, bf16[2,768,768]{2,1,0:T(8,128)(2,1)S(1)} %copy-done.1, ...), custom_call_target="tpu_custom_call" | custom-call | flops 3000000000 | tf_op jit(solution)/shard_map/pallas_call | solution.py:25
  29.7 0.1 collective-permute-start.6
  29.8 0.2 collective-permute-done.10.rb
  30.1 0.4 %collective-permute-done.8.ra = bf16[192,768]{1,0:T(8,128)(2,1)S(1)} collective-permute-done((bf16[192,768]{1,0:T(8,128)(2,1)S(1)}, bf16[192,768]{1,0:T(8,128)(2,1)S(1)}, u32[]{:S(2)}, u32[]{:S(2)}) %collective-permute-start.8) | collective-permute-done | bytes 294944 | tf_op jit(solution)/shard_map/ppermute | solution.py:429
  30.5 1.1 %shard_map.110 = (bf16[192,768]{1,0:T(8,128)(2,1)S(1)}, bf16[192,768]{1,0:T(8,128)(2,1)S(1)}, f32[128,768]{1,0:T(8,128)S(1)}) custom-call(bf16[192,768]{1,0:T(8,128)(2,1)S(1)} %collective-permute-done.8.ra, f32[192,768]{1,0:T(8,128)S(1)} %get-tuple-element.69.la, bf16[192,768]{1,0:T(8,128)(2,1)S(1)} %collective-permute-done.10.rb, ...), custom_call_target="tpu_custom_call" | custom-call | flops 3000000000 | tf_op jit(solution)/shard_map/pallas_call | solution.py:25
  31.6 0.0 collective-permute-done.6.rc
  31.7 1.1 %shard_map.111 = bf16[512,768]{1,0:T(8,128)(2,1)} custom-call(bf16[128,768]{1,0:T(8,128)(2,1)S(1)} %collective-permute-done.6.rc, f32[128,768]{1,0:T(8,128)S(1)} %get-tuple-element.73.lc, bf16[1536,768]{1,0:T(8,128)(2,1)S(1)} %copy-done.2, bf16[128,768]{1,0:T(8,128)(2,1)S(1)} %get-tuple-element.64.dc, bf16[128,768]{1,0:T(8,128)(2,1)S(1)} %get-tuple-element.74.xoc, ...), custom_call_target="tpu_custom_call" | custom-call | tf_op jit(solution)/shard_map/pallas_call | solution.py:573
Async XLA Ops:
  0.0 3.3 %copy-start = (bf16[2,3,768,768]{3,2,1,0:T(8,128)(2,1)S(1)}, bf16[2,3,768,768]{3,2,1,0:T(8,128)(2,1)}, u32[]{:S(2)}) copy-start(bf16[2,3,768,768]{3,2,1,0:T(8,128)(2,1)} %param.15) | copy-start | bytes 21233668
  0.0 3.7 %copy-start.3 = (bf16[1024,768]{1,0:T(8,128)(2,1)S(1)}, bf16[1024,768]{1,0:T(8,128)(2,1)}, u32[]{:S(2)}) copy-start(bf16[1024,768]{1,0:T(8,128)(2,1)} %tower.3) | copy-start | bytes 4718596
  6.2 13.2 %collective-permute-start.3 = (bf16[528,768]{1,0:T(8,128)(2,1)S(1)}, bf16[528,768]{1,0:T(8,128)(2,1)S(1)}, u32[]{:S(2)}, u32[]{:S(2)}) collective-permute-start(bf16[528,768]{1,0:T(8,128)(2,1)S(1)} %get-tuple-element.53.pa), channel_id=1, source_target_pairs={{0,1},{1,0},{2,3},{3,2},{4,5},{5,4},{6,7},{7,6},{8,9},{9,8},{10,11... | collective-permute-start | bytes 2433032 | tf_op jit(solution)/shard_map/ppermute | solution.py:429
  8.5 13.1 %collective-permute-start.4 = (bf16[448,768]{1,0:T(8,128)(2,1)S(1)}, bf16[448,768]{1,0:T(8,128)(2,1)S(1)}, u32[]{:S(2)}, u32[]{:S(2)}) collective-permute-start(bf16[448,768]{1,0:T(8,128)(2,1)S(1)} %get-tuple-element.58.pb), channel_id=1, source_target_pairs={{0,1},{1,0},{2,3},{3,2},{4,5},{5,4},{6,7},{7,6},{8,9},{9,8},{10,11... | collective-permute-start | bytes 2064392 | tf_op jit(solution)/shard_map/ppermute | solution.py:429
  8.6 4.5 %collective-permute-start = (bf16[80,768]{1,0:T(8,128)(2,1)S(1)}, bf16[80,768]{1,0:T(8,128)(2,1)S(1)}, u32[]{:S(2)}, u32[]{:S(2)}) collective-permute-start(bf16[80,768]{1,0:T(8,128)(2,1)S(1)} %get-tuple-element.41), channel_id=1, source_target_pairs={{0,2},{2,0},{4,6},{6,4},{8,10},{10,8},{12,14},{14,12},{1,3},{3,1},... | collective-permute-start | bytes 368648 | tf_op jit(solution)/shard_map/ppermute | solution.py:477
  9.9 9.5 %copy-start.1 = (bf16[2,768,768]{2,1,0:T(8,128)(2,1)S(1)}, bf16[2,768,768]{2,1,0:T(8,128)(2,1)}, u32[]{:S(2)}) copy-start(bf16[2,768,768]{2,1,0:T(8,128)(2,1)} %point_w.11) | copy-start | bytes 7077892
  9.9 7.1 %collective-permute-start.1 = (bf16[80,768]{1,0:T(8,128)(2,1)S(1)}, bf16[80,768]{1,0:T(8,128)(2,1)S(1)}, u32[]{:S(2)}, u32[]{:S(2)}) collective-permute-start(bf16[80,768]{1,0:T(8,128)(2,1)S(1)} %get-tuple-element.42), channel_id=1, source_target_pairs={{2,4},{4,2},{6,8},{8,6},{10,12},{12,10},{3,5},{5,3},{7,9},{9,7},{1... | collective-permute-start | bytes 368648 | tf_op jit(solution)/shard_map/ppermute | solution.py:478
  17.8 6.4 %collective-permute-start.2 = (bf16[160,768]{1,0:T(8,128)(2,1)S(1)}, bf16[160,768]{1,0:T(8,128)(2,1)S(1)}, u32[]{:S(2)}, u32[]{:S(2)}) collective-permute-start(bf16[160,768]{1,0:T(8,128)(2,1)S(1)} %get-tuple-element.49.pe), channel_id=1, source_target_pairs={{0,1},{1,0},{2,3},{3,2},{4,5},{5,4},{6,7},{7,6},{8,9},{9,8},{10,11... | collective-permute-start | bytes 737288 | tf_op jit(solution)/shard_map/ppermute | solution.py:429
  21.6 4.1 %collective-permute-start.7 = (bf16[384,768]{1,0:T(8,128)(2,1)S(1)}, bf16[384,768]{1,0:T(8,128)(2,1)S(1)}, u32[]{:S(2)}, u32[]{:S(2)}) collective-permute-start(bf16[384,768]{1,0:T(8,128)(2,1)S(1)} %get-tuple-element.65.q), channel_id=1, source_target_pairs={{0,1},{1,0},{2,3},{3,2},{4,5},{5,4},{6,7},{7,6},{8,9},{9,8},{10,11... | collective-permute-start | bytes 1769480 | tf_op jit(solution)/shard_map/ppermute | solution.py:429
  23.6 3.0 %collective-permute-start.9 = (bf16[384,768]{1,0:T(8,128)(2,1)S(1)}, bf16[384,768]{1,0:T(8,128)(2,1)S(1)}, u32[]{:S(2)}, u32[]{:S(2)}) collective-permute-start(bf16[384,768]{1,0:T(8,128)(2,1)S(1)} %get-tuple-element.67.q), channel_id=1, source_target_pairs={{0,1},{1,0},{2,3},{3,2},{4,5},{5,4},{6,7},{7,6},{8,9},{9,8},{10,11... | collective-permute-start | bytes 1769480 | tf_op jit(solution)/shard_map/ppermute | solution.py:429
  25.6 1.7 %copy-start.2 = (bf16[1536,768]{1,0:T(8,128)(2,1)S(1)}, bf16[1536,768]{1,0:T(8,128)(2,1)}, u32[]{:S(2)}) copy-start(bf16[1536,768]{1,0:T(8,128)(2,1)} %pool.3) | copy-start | bytes 7077892
  25.6 3.4 %collective-permute-start.5 = (bf16[256,768]{1,0:T(8,128)(2,1)S(1)}, bf16[256,768]{1,0:T(8,128)(2,1)S(1)}, u32[]{:S(2)}, u32[]{:S(2)}) collective-permute-start(bf16[256,768]{1,0:T(8,128)(2,1)S(1)} %get-tuple-element.62.q), channel_id=1, source_target_pairs={{0,1},{1,0},{2,3},{3,2},{4,5},{5,4},{6,7},{7,6},{8,9},{9,8},{10,11... | collective-permute-start | bytes 1179656 | tf_op jit(solution)/shard_map/ppermute | solution.py:429
  28.4 1.6 %collective-permute-start.10 = (bf16[192,768]{1,0:T(8,128)(2,1)S(1)}, bf16[192,768]{1,0:T(8,128)(2,1)S(1)}, u32[]{:S(2)}, u32[]{:S(2)}) collective-permute-start(bf16[192,768]{1,0:T(8,128)(2,1)S(1)} %get-tuple-element.70.db), channel_id=1, source_target_pairs={{0,1},{1,0},{2,3},{3,2},{4,5},{5,4},{6,7},{7,6},{8,9},{9,8},{10,11... | collective-permute-start | bytes 884744 | tf_op jit(solution)/shard_map/ppermute | solution.py:429
  28.5 2.0 %collective-permute-start.8 = (bf16[192,768]{1,0:T(8,128)(2,1)S(1)}, bf16[192,768]{1,0:T(8,128)(2,1)S(1)}, u32[]{:S(2)}, u32[]{:S(2)}) collective-permute-start(bf16[192,768]{1,0:T(8,128)(2,1)S(1)} %get-tuple-element.66.rest_0_.da), channel_id=1, source_target_pairs={{0,1},{1,0},{2,3},{3,2},{4,5},{5,4},{6,7},{7,6},{8,9},{9,8},{10,11... | collective-permute-start | bytes 884744 | tf_op jit(solution)/shard_map/ppermute | solution.py:429
  29.7 1.9 %collective-permute-start.6 = (bf16[128,768]{1,0:T(8,128)(2,1)S(1)}, bf16[128,768]{1,0:T(8,128)(2,1)S(1)}, u32[]{:S(2)}, u32[]{:S(2)}) collective-permute-start(bf16[128,768]{1,0:T(8,128)(2,1)S(1)} %get-tuple-element.64.dc), channel_id=1, source_target_pairs={{0,1},{1,0},{2,3},{3,2},{4,5},{5,4},{6,7},{7,6},{8,9},{9,8},{10,11... | collective-permute-start | bytes 589832 | tf_op jit(solution)/shard_map/ppermute | solution.py:429

commit v7 on v6

--- a/solution.py
+++ b/solution.py
@@ -236,7 +236,7 @@
     def kernel(
         pa, ra, x0, point_w, conv_w, both, s_in, b_in, own_mid, x1a, h1a, qa, mid, z, acc, v,
     ):
-        step = 128
+        step = 224
         n_a = a_hi - a_lo
         tail = ra[n_a : n_a + EXTRA].astype(F32)
         mid[...] = own_mid[...] + (tail[0:4] + tail[4:8] + tail[8:12])
@@ -266,7 +266,7 @@
     def kernel(
         pb, rb, x0, x1a, h1a, point_w, conv_w, both, mid, s_in, b_in, x1b, x1t, h1t, qb, h1, z, acc, v
     ):
-        step = 224
+        step = 256
         b_hi = rows - D0
         first = c_hi - D1
         h1[0 : a_hi - first] = h1a[first - a_lo : a_hi - a_lo]
@@ -435,8 +435,8 @@
 ):
     rows, width = tower_input.shape
     inner = conv_w.shape[3]
-    a_lo, a_hi = D0, rows // 2 + 32
-    c_lo, c_hi, e_hi = 96, rows // 2 - 32, rows - 160
+    a_lo, a_hi = D0, rows // 2 - 32
+    c_lo, c_hi, e_hi = 96, rows // 2 - 128, rows - 160
     b_hi = rows - D0
     n_a, n_b = a_hi - a_lo, b_hi - a_hi
     m_a, m_b = c_hi - c_lo, e_hi - c_hi
@@ -537,8 +537,8 @@
     sc = swap_chan(qc)
     ends, halves = [], []
     for name, q, s, x1, base, m, step in (
-        ("a", qa, sa, x1a, c_lo - a_lo, m_a, 128),
-        ("b", qb, sb, x1b, 0, m_b, 128),
+        ("a", qa, sa, x1a, c_lo - a_lo, m_a, 288),
+        ("b", qb, sb, x1b, 0, m_b, 160),
         ("c", qc, sc, x1c, 0, m_c, 128),
     ):
         before = [ends[0][0], pooling_weight] if name == "b" else []

time: 33.1 us -> 33.4 us (level)
  waiting for transfers between devices: 5.41 us -> 6.09 us
  local copies, waits for them, and re-layouts: 2.55 us -> 1.9 us
    ppermute x9, waiting for transfers between devices: 0.66 us -> 1.34 us  [swap_chan(): return lax.ppermute(a, 'chan', [(0, 1), (1, 0)])]
    unnamed x8, local copies, waits for them, and re-layouts: 2.55 us -> 1.9 us
where the time goes in v7:
time: 33.4 us; the launch traced here: 33.2 us
  Pallas kernels  17.3 us (52%)
  starting transfers between devices  7.57 us (23%)
  waiting for transfers between devices  6.09 us (18%)
  local copies, waits for them, and re-layouts  1.9 us (6%)
    pallas_call x11, Pallas kernels, call(): pl.pallas_call(kernel, out_shape=[pltpu.VMEM(shape, dtype) for shape, dty...  16.2 us
    ppermute x9, starting transfers between devices, swap_chan(): return lax.ppermute(a, 'chan', [(0, 1), (1, 0)])  3.94 us
    ppermute x1, waiting for transfers between devices, local(): r_b = lax.ppermute(e_b, 'seq', pairs_b)  3.87 us
    ppermute x1, starting transfers between devices, local(): r_b = lax.ppermute(e_b, 'seq', pairs_b)  2.32 us
    unnamed x8, local copies, waits for them, and re-layouts  1.9 us
    ppermute x9, waiting for transfers between devices, swap_chan(): return lax.ppermute(a, 'chan', [(0, 1), (1, 0)])  1.34 us
    ppermute x1, starting transfers between devices, local(): r_a = lax.ppermute(e_a, 'seq', pairs_a)  1.3 us
    pallas_call x1, Pallas kernels, local(): pl.pallas_call(pool_last(c_lo // 2, c_hi // 2, e_hi // 2), out_shape=jax....  1.09 us
  transfers between devices with their start and end apart: 11, of which 4 were waited for; matrix products, arithmetic and copies ran while one was open for 0% of the time, Pallas kernels for 36%

profile of v7, /device:TPU:17, one launch (start us, length us, event | category | flops | bytes accessed | tf_op | source)
XLA Modules:
  0.0 33.2 jit_solution(4548907223490980366)
XLA Ops:
  0.0 0.0 copy-start
  0.0 0.0 copy-start.3
  0.0 1.8 %shard_map.100 = (bf16[80,768]{1,0:T(8,128)(2,1)S(1)}, bf16[80,768]{1,0:T(8,128)(2,1)S(1)}, bf16[1024,128]{1,0:T(8,128)(2,1)S(1)}, bf16[128,768]{1,0:T(8,128)(2,...) custom-call(bf16[1024,768]{1,0:T(8,128)(2,1)} %tower.3, s32[32,1024]{1,0:T(8,128)} %bitcast.8, ...), custom_call_target="tpu_custom_call" | custom-call | flops 99999997952 | tf_op jit(solution)/shard_map/pallas_call | solution.py:25
  1.8 1.5 %copy-done = bf16[2,3,768,768]{3,2,1,0:T(8,128)(2,1)S(1)} copy-done((bf16[2,3,768,768]{3,2,1,0:T(8,128)(2,1)S(1)}, bf16[2,3,768,768]{3,2,1,0:T(8,128)(2,1)}, u32[]{:S(2)}) %copy-start) | copy-done | bytes 7077912
  3.3 0.4 %copy-done.3 = bf16[1024,768]{1,0:T(8,128)(2,1)S(1)} copy-done((bf16[1024,768]{1,0:T(8,128)(2,1)S(1)}, bf16[1024,768]{1,0:T(8,128)(2,1)}, u32[]{:S(2)}) %copy-start.3) | copy-done | bytes 1572888
  3.7 2.4 %shard_map.101 = (bf16[1024,768]{1,0:T(8,128)(2,1)S(1)}, bf16[1024,768]{1,0:T(8,128)(2,1)S(1)}, bf16[464,768]{1,0:T(8,128)(2,1)S(1)}, bf16[2,768,768]{2,1,0:T(8,128)(2,1)S(1)}) custom-call(bf16[1024,768]{1,0:T(8,128)(2,1)S(1)} %copy-done.3, bf16[1024,128]{1,0:T(8,128)(2,1)S(1)} %get-tuple-element.43.codes, bf16[128,768]{1,0:T(8,128)(2,1)S(1)} %get-tuple-element.44.embed, ...), custom_call_target="tpu_custom_call" | custom-call | flops 3000000000 | tf_op jit(solution)/shard_map/pallas_call | solution.py:25
  6.1 0.7 %collective-permute-start.3 = (bf16[464,768]{1,0:T(8,128)(2,1)S(1)}, bf16[464,768]{1,0:T(8,128)(2,1)S(1)}, u32[]{:S(2)}, u32[]{:S(2)}) collective-permute-start(bf16[464,768]{1,0:T(8,128)(2,1)S(1)} %get-tuple-element.53.pa), channel_id=1, source_target_pairs={{0,1},{1,0},{2,3},{3,2},{4,5},{5,4},{6,7},{7,6},{8,9},{9,8},{10,11... | collective-permute-start | bytes 2138120 | tf_op jit(solution)/shard_map/ppermute | solution.py:429
  6.9 1.7 %shard_map.103 = (bf16[512,768]{1,0:T(8,128)(2,1)S(1)}, bf16[2,768,768]{2,1,0:T(8,128)(2,1)S(1)}) custom-call(bf16[1024,768]{1,0:T(8,128)(2,1)S(1)} %get-tuple-element.48.h0, bf16[2,2304,768]{2,1,0:T(8,128)(2,1)S(1)} %bitcast.3, bf16[2,768,768]{2,1,0:T(8,128)(2,1)S(1)} %get-tuple-element.54.both), custom_call_target="tpu_custom_call" | custom-call | flops 3000000000 | tf_op jit(solution)/shard_map/pallas_call | solution.py:25
  8.6 0.1 collective-permute-start.4
  8.7 1.3 %collective-permute-start = (bf16[80,768]{1,0:T(8,128)(2,1)S(1)}, bf16[80,768]{1,0:T(8,128)(2,1)S(1)}, u32[]{:S(2)}, u32[]{:S(2)}) collective-permute-start(bf16[80,768]{1,0:T(8,128)(2,1)S(1)} %get-tuple-element.41), channel_id=1, source_target_pairs={{0,2},{2,0},{4,6},{6,4},{8,10},{10,8},{12,14},{14,12},{1,3},{3,1},... | collective-permute-start | bytes 368648 | tf_op jit(solution)/shard_map/ppermute | solution.py:477
  10.0 0.0 copy-start.1
  10.0 2.3 %collective-permute-start.1 = (bf16[80,768]{1,0:T(8,128)(2,1)S(1)}, bf16[80,768]{1,0:T(8,128)(2,1)S(1)}, u32[]{:S(2)}, u32[]{:S(2)}) collective-permute-start(bf16[80,768]{1,0:T(8,128)(2,1)S(1)} %get-tuple-element.42), channel_id=1, source_target_pairs={{2,4},{4,2},{6,8},{8,6},{10,12},{12,10},{3,5},{5,3},{7,9},{9,7},{1... | collective-permute-start | bytes 368648 | tf_op jit(solution)/shard_map/ppermute | solution.py:478
  12.3 0.9 %collective-permute-done.r_a = bf16[80,768]{1,0:T(8,128)(2,1)S(1)} collective-permute-done((bf16[80,768]{1,0:T(8,128)(2,1)S(1)}, bf16[80,768]{1,0:T(8,128)(2,1)S(1)}, u32[]{:S(2)}, u32[]{:S(2)}) %collective-permute-start) | collective-permute-done | bytes 122912 | tf_op jit(solution)/shard_map/ppermute | solution.py:477
  13.2 3.9 %collective-permute-done.1.r_b = bf16[80,768]{1,0:T(8,128)(2,1)S(1)} collective-permute-done((bf16[80,768]{1,0:T(8,128)(2,1)S(1)}, bf16[80,768]{1,0:T(8,128)(2,1)S(1)}, u32[]{:S(2)}, u32[]{:S(2)}) %collective-permute-start.1) | collective-permute-done | bytes 122912 | tf_op jit(solution)/shard_map/ppermute | solution.py:478
  17.0 0.8 %shard_map.102 = (bf16[160,768]{1,0:T(8,128)(2,1)S(1)}, bf16[80,768]{1,0:T(8,128)(2,1)S(1)}, bf16[80,768]{1,0:T(8,128)(2,1)S(1)}) custom-call(bf16[80,768]{1,0:T(8,128)(2,1)S(1)} %collective-permute-done.r_a, bf16[80,768]{1,0:T(8,128)(2,1)S(1)} %collective-permute-done.1.r_b, bf16[1024,768]{1,0:T(8,128)(2,1)S(1)} %get-tuple-element.48.h0, ...), custom_call_target="tpu_custom_call" | custom-call | flops 3000000000 | tf_op jit(solution)/shard_map/pallas_call | solution.py:25
  17.8 1.6 %collective-permute-start.2 = (bf16[160,768]{1,0:T(8,128)(2,1)S(1)}, bf16[160,768]{1,0:T(8,128)(2,1)S(1)}, u32[]{:S(2)}, u32[]{:S(2)}) collective-permute-start(bf16[160,768]{1,0:T(8,128)(2,1)S(1)} %get-tuple-element.49.pe), channel_id=1, source_target_pairs={{0,1},{1,0},{2,3},{3,2},{4,5},{5,4},{6,7},{7,6},{8,9},{9,8},{10,11... | collective-permute-start | bytes 737288 | tf_op jit(solution)/shard_map/ppermute | solution.py:429
  19.5 0.0 collective-permute-done.3.ra
  19.5 0.0 copy-done.1
  19.5 1.8 %shard_map.104 = (bf16[448,768]{1,0:T(8,128)(2,1)S(1)}, bf16[448,768]{1,0:T(8,128)(2,1)S(1)}, bf16[288,768]{1,0:T(8,128)(2,1)S(1)}, f32[4,768]{1,0:T(4,128)S(1)}) custom-call(bf16[464,768]{1,0:T(8,128)(2,1)S(1)} %get-tuple-element.53.pa, bf16[464,768]{1,0:T(8,128)(2,1)S(1)} %collective-permute-done.3.ra, bf16[1024,768]{1,0:T(8,128)(2,1)S(1)} %get-tuple-element.50.x0, ...), custom_call_target="tpu_custom_call" | custom-call | flops 3000000000 | tf_op jit(solution)/shard_map/pallas_call | solution.py:25
  21.3 0.0 collective-permute-done.4.rb
  21.3 2.3 %shard_map.105 = (bf16[480,768]{1,0:T(8,128)(2,1)S(1)}, bf16[128,768]{1,0:T(8,128)(2,1)S(1)}, bf16[176,768]{1,0:T(8,128)(2,1)S(1)}, bf16[480,768]{1,0:T(8,128)(2,1)S(1)}) custom-call(bf16[512,768]{1,0:T(8,128)(2,1)S(1)} %get-tuple-element.58.pb, bf16[512,768]{1,0:T(8,128)(2,1)S(1)} %collective-permute-done.4.rb, bf16[1024,768]{1,0:T(8,128)(2,1)S(1)} %get-tuple-element.50.x0, ...), custom_call_target="tpu_custom_call" | custom-call | flops 3000000000 | tf_op jit(solution)/shard_map/pallas_call | solution.py:25
  23.6 0.1 collective-permute-start.9
  23.7 0.5 %collective-permute-start.7 = (bf16[288,768]{1,0:T(8,128)(2,1)S(1)}, bf16[288,768]{1,0:T(8,128)(2,1)S(1)}, u32[]{:S(2)}, u32[]{:S(2)}) collective-permute-start(bf16[288,768]{1,0:T(8,128)(2,1)S(1)} %get-tuple-element.65.q), channel_id=1, source_target_pairs={{0,1},{1,0},{2,3},{3,2},{4,5},{5,4},{6,7},{7,6},{8,9},{9,8},{10,11... | collective-permute-start | bytes 1327112 | tf_op jit(solution)/shard_map/ppermute | solution.py:429
  24.2 0.0 collective-permute-done.2.re
  24.2 1.5 %shard_map.106 = (bf16[256,768]{1,0:T(8,128)(2,1)S(1)}, bf16[256,768]{1,0:T(8,128)(2,1)S(1)}) custom-call(bf16[160,768]{1,0:T(8,128)(2,1)S(1)} %get-tuple-element.49.pe, bf16[160,768]{1,0:T(8,128)(2,1)S(1)} %collective-permute-done.2.re, bf16[1024,768]{1,0:T(8,128)(2,1)S(1)} %get-tuple-element.50.x0, bf16[80,768]{1,0:T(8,128)(2,1)S(1)} %get-tuple-element.51.lo, ...), custom_call_target="tpu_custom_call" | custom-call | flops 3000000000 | tf_op jit(solution)/shard_map/pallas_call | solution.py:25
  25.7 0.0 copy-start.2
  25.7 0.1 collective-permute-start.5
  25.8 0.7 %collective-permute-done.7.r = bf16[288,768]{1,0:T(8,128)(2,1)S(1)} collective-permute-done((bf16[288,768]{1,0:T(8,128)(2,1)S(1)}, bf16[288,768]{1,0:T(8,128)(2,1)S(1)}, u32[]{:S(2)}, u32[]{:S(2)}) %collective-permute-start.7) | collective-permute-done | bytes 442400 | tf_op jit(solution)/shard_map/ppermute | solution.py:429
  26.5 0.9 %shard_map.108 = (bf16[144,768]{1,0:T(8,128)(2,1)S(1)}, bf16[144,768]{1,0:T(8,128)(2,1)S(1)}) custom-call(bf16[288,768]{1,0:T(8,128)(2,1)S(1)} %get-tuple-element.65.q, bf16[288,768]{1,0:T(8,128)(2,1)S(1)} %collective-permute-done.7.r, bf16[448,768]{1,0:T(8,128)(2,1)S(1)} %get-tuple-element.56.x1a.x1, bf16[2,768,768]{2,1,0:T(8,128)(2,1)S(1)} %copy-done.1, ...), custom_call_target="tpu_custom_call" | custom-call | flops 3000000000 | tf_op jit(solution)/shard_map/pallas_call | solution.py:25
  27.5 0.0 collective-permute-done.9.r
  27.5 0.0 copy-done.2
  27.5 1.2 %shard_map.109 = (bf16[240,768]{1,0:T(8,128)(2,1)S(1)}, bf16[240,768]{1,0:T(8,128)(2,1)S(1)}, f32[144,768]{1,0:T(8,128)S(1)}) custom-call(bf16[480,768]{1,0:T(8,128)(2,1)S(1)} %get-tuple-element.67.q, bf16[480,768]{1,0:T(8,128)(2,1)S(1)} %collective-permute-done.9.r, bf16[480,768]{1,0:T(8,128)(2,1)S(1)} %get-tuple-element.68.x1, ...), custom_call_target="tpu_custom_call" | custom-call | flops 3000000000 | tf_op jit(solution)/shard_map/pallas_call | solution.py:25
  28.7 0.2 collective-permute-start.10
  28.9 0.4 %collective-permute-start.8 = (bf16[144,768]{1,0:T(8,128)(2,1)S(1)}, bf16[144,768]{1,0:T(8,128)(2,1)S(1)}, u32[]{:S(2)}, u32[]{:S(2)}) collective-permute-start(bf16[144,768]{1,0:T(8,128)(2,1)S(1)} %get-tuple-element.66.rest_0_.da), channel_id=1, source_target_pairs={{0,1},{1,0},{2,3},{3,2},{4,5},{5,4},{6,7},{7,6},{8,9},{9,8},{10,11... | collective-permute-start | bytes 663560 | tf_op jit(solution)/shard_map/ppermute | solution.py:429
  29.3 0.0 collective-permute-done.5.r
  29.3 0.7 %shard_map.107 = (bf16[128,768]{1,0:T(8,128)(2,1)S(1)}, bf16[128,768]{1,0:T(8,128)(2,1)S(1)}) custom-call(bf16[256,768]{1,0:T(8,128)(2,1)S(1)} %get-tuple-element.62.q, bf16[256,768]{1,0:T(8,128)(2,1)S(1)} %collective-permute-done.5.r, bf16[256,768]{1,0:T(8,128)(2,1)S(1)} %get-tuple-element.63.x1, bf16[2,768,768]{2,1,0:T(8,128)(2,1)S(1)} %copy-done.1, ...), custom_call_target="tpu_custom_call" | custom-call | flops 3000000000 | tf_op jit(solution)/shard_map/pallas_call | solution.py:25
  30.0 0.2 collective-permute-start.6
  30.2 0.6 %collective-permute-done.8.ra = bf16[144,768]{1,0:T(8,128)(2,1)S(1)} collective-permute-done((bf16[144,768]{1,0:T(8,128)(2,1)S(1)}, bf16[144,768]{1,0:T(8,128)(2,1)S(1)}, u32[]{:S(2)}, u32[]{:S(2)}) %collective-permute-start.8) | collective-permute-done | bytes 221216 | tf_op jit(solution)/shard_map/ppermute | solution.py:429
  30.8 0.0 collective-permute-done.10.rb
  30.8 1.1 %shard_map.110 = (bf16[144,768]{1,0:T(8,128)(2,1)S(1)}, bf16[240,768]{1,0:T(8,128)(2,1)S(1)}, f32[128,768]{1,0:T(8,128)S(1)}) custom-call(bf16[144,768]{1,0:T(8,128)(2,1)S(1)} %collective-permute-done.8.ra, f32[144,768]{1,0:T(8,128)S(1)} %get-tuple-element.69.la, bf16[240,768]{1,0:T(8,128)(2,1)S(1)} %collective-permute-done.10.rb, ...), custom_call_target="tpu_custom_call" | custom-call | flops 3000000000 | tf_op jit(solution)/shard_map/pallas_call | solution.py:25
  31.9 0.0 collective-permute-done.6.rc
  31.9 1.1 %shard_map.111 = bf16[512,768]{1,0:T(8,128)(2,1)} custom-call(bf16[128,768]{1,0:T(8,128)(2,1)S(1)} %collective-permute-done.6.rc, f32[128,768]{1,0:T(8,128)S(1)} %get-tuple-element.73.lc, bf16[1536,768]{1,0:T(8,128)(2,1)S(1)} %copy-done.2, bf16[128,768]{1,0:T(8,128)(2,1)S(1)} %get-tuple-element.64.dc, bf16[128,768]{1,0:T(8,128)(2,1)S(1)} %get-tuple-element.74.xoc, ...), custom_call_target="tpu_custom_call" | custom-call | tf_op jit(solution)/shard_map/pallas_call | solution.py:573
Async XLA Ops:
  0.0 3.3 %copy-start = (bf16[2,3,768,768]{3,2,1,0:T(8,128)(2,1)S(1)}, bf16[2,3,768,768]{3,2,1,0:T(8,128)(2,1)}, u32[]{:S(2)}) copy-start(bf16[2,3,768,768]{3,2,1,0:T(8,128)(2,1)} %param.15) | copy-start | bytes 21233668
  0.0 3.7 %copy-start.3 = (bf16[1024,768]{1,0:T(8,128)(2,1)S(1)}, bf16[1024,768]{1,0:T(8,128)(2,1)}, u32[]{:S(2)}) copy-start(bf16[1024,768]{1,0:T(8,128)(2,1)} %tower.3) | copy-start | bytes 4718596
  6.1 13.4 %collective-permute-start.3 = (bf16[464,768]{1,0:T(8,128)(2,1)S(1)}, bf16[464,768]{1,0:T(8,128)(2,1)S(1)}, u32[]{:S(2)}, u32[]{:S(2)}) collective-permute-start(bf16[464,768]{1,0:T(8,128)(2,1)S(1)} %get-tuple-element.53.pa), channel_id=1, source_target_pairs={{0,1},{1,0},{2,3},{3,2},{4,5},{5,4},{6,7},{7,6},{8,9},{9,8},{10,11... | collective-permute-start | bytes 2138120 | tf_op jit(solution)/shard_map/ppermute | solution.py:429
  8.6 12.7 %collective-permute-start.4 = (bf16[512,768]{1,0:T(8,128)(2,1)S(1)}, bf16[512,768]{1,0:T(8,128)(2,1)S(1)}, u32[]{:S(2)}, u32[]{:S(2)}) collective-permute-start(bf16[512,768]{1,0:T(8,128)(2,1)S(1)} %get-tuple-element.58.pb), channel_id=1, source_target_pairs={{0,1},{1,0},{2,3},{3,2},{4,5},{5,4},{6,7},{7,6},{8,9},{9,8},{10,11... | collective-permute-start | bytes 2359304 | tf_op jit(solution)/shard_map/ppermute | solution.py:429
  8.7 4.5 %collective-permute-start = (bf16[80,768]{1,0:T(8,128)(2,1)S(1)}, bf16[80,768]{1,0:T(8,128)(2,1)S(1)}, u32[]{:S(2)}, u32[]{:S(2)}) collective-permute-start(bf16[80,768]{1,0:T(8,128)(2,1)S(1)} %get-tuple-element.41), channel_id=1, source_target_pairs={{0,2},{2,0},{4,6},{6,4},{8,10},{10,8},{12,14},{14,12},{1,3},{3,1},... | collective-permute-start | bytes 368648 | tf_op jit(solution)/shard_map/ppermute | solution.py:477
  10.0 9.5 %copy-start.1 = (bf16[2,768,768]{2,1,0:T(8,128)(2,1)S(1)}, bf16[2,768,768]{2,1,0:T(8,128)(2,1)}, u32[]{:S(2)}) copy-start(bf16[2,768,768]{2,1,0:T(8,128)(2,1)} %point_w.11) | copy-start | bytes 7077892
  10.0 7.1 %collective-permute-start.1 = (bf16[80,768]{1,0:T(8,128)(2,1)S(1)}, bf16[80,768]{1,0:T(8,128)(2,1)S(1)}, u32[]{:S(2)}, u32[]{:S(2)}) collective-permute-start(bf16[80,768]{1,0:T(8,128)(2,1)S(1)} %get-tuple-element.42), channel_id=1, source_target_pairs={{2,4},{4,2},{6,8},{8,6},{10,12},{12,10},{3,5},{5,3},{7,9},{9,7},{1... | collective-permute-start | bytes 368648 | tf_op jit(solution)/shard_map/ppermute | solution.py:478
  17.8 6.4 %collective-permute-start.2 = (bf16[160,768]{1,0:T(8,128)(2,1)S(1)}, bf16[160,768]{1,0:T(8,128)(2,1)S(1)}, u32[]{:S(2)}, u32[]{:S(2)}) collective-permute-start(bf16[160,768]{1,0:T(8,128)(2,1)S(1)} %get-tuple-element.49.pe), channel_id=1, source_target_pairs={{0,1},{1,0},{2,3},{3,2},{4,5},{5,4},{6,7},{7,6},{8,9},{9,8},{10,11... | collective-permute-start | bytes 737288 | tf_op jit(solution)/shard_map/ppermute | solution.py:429
  23.6 3.8 %collective-permute-start.9 = (bf16[480,768]{1,0:T(8,128)(2,1)S(1)}, bf16[480,768]{1,0:T(8,128)(2,1)S(1)}, u32[]{:S(2)}, u32[]{:S(2)}) collective-permute-start(bf16[480,768]{1,0:T(8,128)(2,1)S(1)} %get-tuple-element.67.q), channel_id=1, source_target_pairs={{0,1},{1,0},{2,3},{3,2},{4,5},{5,4},{6,7},{7,6},{8,9},{9,8},{10,11... | collective-permute-start | bytes 2211848 | tf_op jit(solution)/shard_map/ppermute | solution.py:429
  23.7 2.8 %collective-permute-start.7 = (bf16[288,768]{1,0:T(8,128)(2,1)S(1)}, bf16[288,768]{1,0:T(8,128)(2,1)S(1)}, u32[]{:S(2)}, u32[]{:S(2)}) collective-permute-start(bf16[288,768]{1,0:T(8,128)(2,1)S(1)} %get-tuple-element.65.q), channel_id=1, source_target_pairs={{0,1},{1,0},{2,3},{3,2},{4,5},{5,4},{6,7},{7,6},{8,9},{9,8},{10,11... | collective-permute-start | bytes 1327112 | tf_op jit(solution)/shard_map/ppermute | solution.py:429
  25.7 1.8 %copy-start.2 = (bf16[1536,768]{1,0:T(8,128)(2,1)S(1)}, bf16[1536,768]{1,0:T(8,128)(2,1)}, u32[]{:S(2)}) copy-start(bf16[1536,768]{1,0:T(8,128)(2,1)} %pool.3) | copy-start | bytes 7077892
  25.7 3.6 %collective-permute-start.5 = (bf16[256,768]{1,0:T(8,128)(2,1)S(1)}, bf16[256,768]{1,0:T(8,128)(2,1)S(1)}, u32[]{:S(2)}, u32[]{:S(2)}) collective-permute-start(bf16[256,768]{1,0:T(8,128)(2,1)S(1)} %get-tuple-element.62.q), channel_id=1, source_target_pairs={{0,1},{1,0},{2,3},{3,2},{4,5},{5,4},{6,7},{7,6},{8,9},{9,8},{10,11... | collective-permute-start | bytes 1179656 | tf_op jit(solution)/shard_map/ppermute | solution.py:429
  28.7 2.1 %collective-permute-start.10 = (bf16[240,768]{1,0:T(8,128)(2,1)S(1)}, bf16[240,768]{1,0:T(8,128)(2,1)S(1)}, u32[]{:S(2)}, u32[]{:S(2)}) collective-permute-start(bf16[240,768]{1,0:T(8,128)(2,1)S(1)} %get-tuple-element.70.db), channel_id=1, source_target_pairs={{0,1},{1,0},{2,3},{3,2},{4,5},{5,4},{6,7},{7,6},{8,9},{9,8},{10,11... | collective-permute-start | bytes 1105928 | tf_op jit(solution)/shard_map/ppermute | solution.py:429
  28.9 1.9 %collective-permute-start.8 = (bf16[144,768]{1,0:T(8,128)(2,1)S(1)}, bf16[144,768]{1,0:T(8,128)(2,1)S(1)}, u32[]{:S(2)}, u32[]{:S(2)}) collective-permute-start(bf16[144,768]{1,0:T(8,128)(2,1)S(1)} %get-tuple-element.66.rest_0_.da), channel_id=1, source_target_pairs={{0,1},{1,0},{2,3},{3,2},{4,5},{5,4},{6,7},{7,6},{8,9},{9,8},{10,11... | collective-permute-start | bytes 663560 | tf_op jit(solution)/shard_map/ppermute | solution.py:429
  30.0 2.0 %collective-permute-start.6 = (bf16[128,768]{1,0:T(8,128)(2,1)S(1)}, bf16[128,768]{1,0:T(8,128)(2,1)S(1)}, u32[]{:S(2)}, u32[]{:S(2)}) collective-permute-start(bf16[128,768]{1,0:T(8,128)(2,1)S(1)} %get-tuple-element.64.dc), channel_id=1, source_target_pairs={{0,1},{1,0},{2,3},{3,2},{4,5},{5,4},{6,7},{7,6},{8,9},{9,8},{10,11... | collective-permute-start | bytes 589832 | tf_op jit(solution)/shard_map/ppermute | solution.py:429
